TPU v7x, 128 devices: a whole 4x4x4 slice. The times are simulated.
128 devices in a mesh: dom: 8 (over z, core), blk: 16 (over y, x).
Axes of the slice: x: 4, y: 4, z: 4, core: 2. Of those that a mesh axis runs over, the one named last changes fastest.
Arguments:
- queries: bfloat16 [2048, 768], P(('dom', 'blk')), may hold values from -6 to 6
- adapter_w: bfloat16 [768, 768], replicated, may hold values from -0.21875 to 0.21875
- index_rows: bfloat16 [64, 8192, 768], P('dom', 'blk'), may hold values from -16 to 16
- probes: int32 [2048, 16], P(('dom', 'blk')), may hold values from 0 to 63, all different within a row; in each aligned block of 2048 rows (0 to 2047, 2048 to 4095, ...) at most 1024 rows name the same one
- list_slot: int32 [64], replicated, may hold values from 0 to 63, each once
- block_counts: int32 [64], replicated, may hold values from 48 to 64
- target_raw: int32 [2048], P(('dom', 'blk')), may hold values from 0 to 131071
Outputs:
- query_grad: bfloat16 [2048, 768], P(('dom', 'blk'))
- adapter_grad: float32 [768, 768], replicated
Inputs may be any that keep to these rules, and one draw needn't show every extreme that they name: `probes`: each row names 16 different lists; at most 1024 queries name one list, a bound that some block reaches. `list_slot`: each list id once.
All inputs are finite; a program needn't handle non-finite values.
Results may differ from a plain program's by a relative error of at most 0.015.
Values may be sent and summed in bfloat16 or wider, within the bound.
No kernel may reach another device: no remote copies, remote signals or barrier semaphores. Data moves between devices by JAX's collectives and lax.ppermute only.
A program may use at most 128 MiB of HBM per device.

v0:
```python
import functools
import math

import jax
import jax.numpy as jnp
from jax import lax
from jax.experimental import pallas as pl
from jax.experimental.pallas import tpu as pltpu
from jax.sharding import Mesh
from jax.sharding import PartitionSpec as P

ROWS = 128
NEG_FILL = -1e30
LANES = 128
PROBES = 16
SIZES = (4, 2, 4, 4)
AXES = ("z", "core", "y", "x")
CHIPS = ("z", "y", "x")
ORDER = (0, 1, 3, 2)
LOG2E = 1.4426950408889634
WHOLE = pl.BlockSpec(memory_space=pltpu.VMEM)


def from_ahead(value, axis, step):
    size = lax.axis_size(axis)
    return lax.ppermute(value, axis, [((i + step) % size, i) for i in range(size)])


def chunk_of(i):
    return jnp.where(i < 2, i, 5 - i)


def spread_axes(value, axes):
    size = lax.axis_size(axes)
    spread = jnp.broadcast_to(value[None], (size,) + value.shape).reshape((-1,) + value.shape[1:])
    return lax.all_to_all(spread, axes, split_axis=0, concat_axis=0, tiled=True)


def lanes_of(column, tile):
    return jnp.broadcast_to(column, (tile, LANES))


def columns_of(rows, tile):
    return jnp.concatenate([rows, jnp.zeros((LANES - rows.shape[0], tile), jnp.float32)], axis=0).T


def score_kernel(
    place, list_slot, block_counts, own_ref, other_ref, w_ref, rows_ref,
    p_ref, tops_ref, stats_ref, code_ref, q_out, q_ref, bias_ref, s_ref, here_ref,
):
    width = w_ref.shape[0]
    tile = own_ref.shape[0]
    lists, per = rows_ref.shape[0], rows_ref.shape[1]
    factor = LOG2E / math.sqrt(width)
    core = pl.program_id(0)

    def find(n, _):
        at = list_slot[n] - place[2]
        here_ref[jnp.where((at >= 0) & (at < lists), at, lists)] = n
        return 0

    lax.fori_loop(0, list_slot.shape[0], find, 0)
    here = [here_ref[j] for j in range(lists)]
    total_rows = [ROWS * block_counts[n] for n in here]
    live = [n - place[3] for n in total_rows]

    @pl.when(core == place[1])
    def _():
        q_ref[...] = own_ref[...]

    @pl.when(core != place[1])
    def _():
        q_ref[...] = other_ref[...]

    queries = q_ref[:, :width]
    q_out[...] = queries
    adapted = (
        queries.astype(jnp.float32) + jnp.dot(queries, w_ref[...], preferred_element_type=jnp.float32)
    ).astype(jnp.bfloat16)

    info = q_ref[:, width:].astype(jnp.float32).T
    probes = info[0:PROBES, :]
    number = lax.broadcasted_iota(jnp.int32, (PROBES, tile), 0).astype(jnp.float32)
    target = jnp.sum(jnp.where(number == info[PROBES : PROBES + 1, :], probes, 0.0), axis=0, keepdims=True)
    raw_row = info[PROBES + 1 : PROBES + 2, :] * 64.0 + info[PROBES + 2 : PROBES + 3, :]
    code = jnp.full((1, tile), -1.0, jnp.float32)
    bias = []
    for j in range(lists):
        name = here[j].astype(jnp.float32)
        probed = jnp.max(jnp.where(probes == name, 1.0, 0.0), axis=0, keepdims=True)
        bias.append(jnp.where(probed > 0.0, 0.0, NEG_FILL))
        length = total_rows[j].astype(jnp.float32)
        row = raw_row - jnp.where(raw_row >= length, length, 0.0) - place[3].astype(jnp.float32)
        inside = (target == name) & (row >= 0.0) & (row < float(per))
        code = jnp.where(inside, row + float(j * per), code)
    code_ref[...] = code
    bias = columns_of(jnp.concatenate(bias, axis=0), tile)
    for j in range(lists):
        bias_ref[j] = lanes_of(bias[:, j : j + 1], tile)
    bias_ref[lists] = jnp.full((tile, LANES), NEG_FILL, jnp.float32)

    lane = lax.broadcasted_iota(jnp.int32, (tile, LANES), 1)
    blocks = per // LANES

    def matmul(j):
        raw = lax.dot_general(
            adapted, rows_ref[j], (((1,), (1,)), ((), ())), preferred_element_type=jnp.float32
        )
        top = None
        for b in range(blocks):
            which = jnp.where(live[j] > b * LANES, j, lists)
            piece = raw[:, b * LANES : (b + 1) * LANES] + bias_ref[which]
            s_ref[j % 2, :, b * LANES : (b + 1) * LANES] = piece
            top = piece if top is None else jnp.maximum(top, piece)
        return top

    def weigh(j, top):
        peak = lanes_of(jnp.max(top, axis=1, keepdims=True), tile) * factor
        total = None
        for b in range(blocks):
            weight = jnp.exp2(s_ref[j % 2, :, b * LANES : (b + 1) * LANES] * factor - peak)
            total = weight if total is None else total + weight
            at = j * per + b * LANES
            p_ref[:, at : at + LANES] = weight.astype(jnp.bfloat16)
        return peak, lanes_of(jnp.sum(total, axis=1, keepdims=True), tile)

    tops = jnp.full((tile, LANES), NEG_FILL, jnp.float32)
    sums = jnp.zeros((tile, LANES), jnp.float32)
    waiting = matmul(0)
    for j in range(lists):
        following = matmul(j + 1) if j + 1 < lists else None
        peak, total = weigh(j, waiting)
        tops = jnp.where(lane == j, peak, tops)
        sums = jnp.where(lane == j, total, sums)
        waiting = following
    tops = tops.T[0:lists, :]
    sums = sums.T[0:lists, :]
    tops_ref[...] = tops
    high = jnp.max(tops, axis=0, keepdims=True)
    stats_ref[0:1, :] = high
    stats_ref[1:2, :] = jnp.sum(sums * jnp.exp2(tops - high), axis=0, keepdims=True)


def back_kernel(stats_ref, code_ref, tops_ref, p_ref, rows_ref, *refs):
    out_ref, target_ref, g_ref, row_ref = refs[-4:]
    lists, per, width = rows_ref.shape
    tile = p_ref.shape[0]
    share = columns_of(jnp.exp2(tops_ref[...] - stats_ref[0:1, :]), tile)
    acc = None
    for j in range(lists):
        part = lanes_of(share[:, j : j + 1], tile)
        for b in range(per // LANES):
            at = j * per + b * LANES
            g_ref[:, at : at + LANES] = (p_ref[:, at : at + LANES].astype(jnp.float32) * part).astype(jnp.bfloat16)
        out = jnp.dot(g_ref[:, j * per : (j + 1) * per], rows_ref[j], preferred_element_type=jnp.float32)
        acc = out if acc is None else acc + out
    out_ref[...] = acc

    row_ref[...] = jnp.zeros_like(row_ref)
    code = code_ref[...]
    index = lax.broadcasted_iota(jnp.int32, (1, tile), 1).astype(jnp.float32)
    sub = lax.broadcasted_iota(jnp.int32, (16, width), 0)
    none = float(tile)

    def first_after(last):
        return jnp.min(jnp.where((code >= 0.0) & (index > last), index, none))

    def step(at):
        key = jnp.max(jnp.where(index == at, code, -1.0)).astype(jnp.int32)
        group = rows_ref[key // per, pl.ds(pl.multiple_of((key % per) // 16 * 16, 16), 16), :]
        row = jnp.sum(jnp.where(sub == key % 16, group.astype(jnp.float32), 0.0), axis=0, keepdims=True)
        row_ref[pl.ds(at.astype(jnp.int32), 1), :] = row
        return first_after(at)

    lax.while_loop(lambda at: at < none, step, first_after(-1.0))
    target_ref[...] = row_ref[...].astype(jnp.bfloat16)


def scale_kernel(place, local_ref, whole_ref, out_ref, target_ref, mine_ref, theirs_ref, r_ref):
    tile, width = out_ref.shape
    half = tile // 2
    share = jnp.exp2(local_ref[0:1, :] - whole_ref[0:1, :]) / whole_ref[1:2, :]
    share = jnp.broadcast_to(share, (LANES, tile)).T
    for b in range(width // LANES):
        at = slice(b * LANES, (b + 1) * LANES)
        r_ref[:, at] = (
            (out_ref[:, at] * share - target_ref[:, at].astype(jnp.float32)) * (1.0 / math.sqrt(width))
        ).astype(jnp.bfloat16)
    mine_ref[...] = r_ref[pl.ds(pl.multiple_of(place[1] * half, half), half), :]
    theirs_ref[...] = r_ref[pl.ds(pl.multiple_of((1 - place[1]) * half, half), half), :]


def adapter_kernel(place, q0, q1, q2, q3, b_own, b_other, out_ref, q_ref, b_ref):
    tile = q0.shape[0]
    half = tile // 2
    count = 4 * tile

    @pl.when(pl.program_id(0) == 0)
    def _():
        for i in range(4):
            for source, core in ((b_own, place[1]), (b_other, 1 - place[1])):
                to = pl.multiple_of(i * tile + core * half, half)
                b_ref[pl.ds(to, half), :] = source[i * half : (i + 1) * half, :]

    for ahead, q in zip(ORDER, (q0, q1, q2, q3)):
        to = pl.multiple_of(lax.rem(place[0] + ahead, 4) * tile, tile)
        q_ref[pl.ds(to, tile), :] = q[...]
    out_ref[...] = lax.dot_general(
        q_ref[...], b_ref[...], (((0,), (0,)), ((), ())), preferred_element_type=jnp.float32
    ) * (1.0 / math.sqrt(count))


def merge_axis(stats, axis):
    chunk = stats.shape[1] // 4
    parts = [stats]
    for j in range(1, lax.axis_size(axis)):
        part = from_ahead(stats, axis, j)
        if axis == "z":
            at = [ORDER.index((ahead - j) % 4) for ahead in ORDER]
            part = jnp.concatenate([part[:, k * chunk : (k + 1) * chunk] for k in at], axis=1)
        parts.append(part)
    top = functools.reduce(jnp.maximum, [p[0] for p in parts])
    total = sum(p[1] * jnp.exp2(p[0] - top) for p in parts)
    return jnp.stack([top, total])


def all_steps(queries, adapter_w, index_rows, probes, list_slot, block_counts, target_raw):
    width = queries.shape[1]
    lists_here, rows_here = index_rows.shape[0], index_rows.shape[1]
    place_z, place_c = lax.axis_index("z"), lax.axis_index("core")
    place_y, place_x = lax.axis_index("y"), lax.axis_index("x")
    first_slot = (place_z * 2 + place_c) * lists_here
    first_row = (place_y * 4 + place_x) * rows_here
    list_length = rows_here * 16
    place = jnp.stack([place_z, place_c, first_slot, first_row]).astype(jnp.int32)

    lane = jnp.arange(LANES, dtype=jnp.int32)[None, :]
    raw_row = lax.rem(target_raw, list_length)[:, None]
    info = jnp.pad(probes, ((0, 0), (0, LANES - PROBES)))
    info = jnp.where(lane == PROBES, lax.div(target_raw, list_length)[:, None], info)
    info = jnp.where(lane == PROBES + 1, lax.div(raw_row, 64), info)
    info = jnp.where(lane == PROBES + 2, lax.rem(raw_row, 64), info)
    plane = spread_axes(jnp.concatenate([queries, info.astype(jnp.bfloat16)], axis=1), ("y", "x"))

    half = plane.shape[0]
    tile = 2 * half
    steps = 4
    count = steps * tile
    keys = lists_here * rows_here
    owns = [plane]
    for ahead in ORDER[1:]:
        owns.append(from_ahead(plane, "z", ahead))
    weights, tops, stats, codes, gathered = [], [], [], [], []
    for ahead, own in zip(ORDER, owns):
        other = from_ahead(own, "core", 1)
        call = pl.pallas_call(
            score_kernel,
            grid_spec=pltpu.PrefetchScalarGridSpec(
                num_scalar_prefetch=3,
                grid=(2,),
                in_specs=[
                    pl.BlockSpec((half, width + LANES), lambda i, *_: (0, 0)),
                    pl.BlockSpec((half, width + LANES), lambda i, *_: (0, 0)),
                    WHOLE,
                    WHOLE,
                ],
                out_specs=[
                    pl.BlockSpec((half, keys), lambda i, *_: (i, 0)),
                    pl.BlockSpec((lists_here, half), lambda i, *_: (0, i)),
                    pl.BlockSpec((2, half), lambda i, *_: (0, i)),
                    pl.BlockSpec((1, half), lambda i, *_: (0, i)),
                    pl.BlockSpec((half, width), lambda i, *_: (i, 0)),
                ],
                scratch_shapes=[
                    pltpu.VMEM((half, width + LANES), jnp.bfloat16),
                    pltpu.VMEM((lists_here + 1, half, LANES), jnp.float32),
                    pltpu.VMEM((2, half, rows_here), jnp.float32),
                    pltpu.SMEM((lists_here + 1,), jnp.int32),
                ],
            ),
            out_shape=[
                jax.ShapeDtypeStruct((tile, keys), jnp.bfloat16),
                jax.ShapeDtypeStruct((lists_here, tile), jnp.float32),
                jax.ShapeDtypeStruct((2, tile), jnp.float32),
                jax.ShapeDtypeStruct((1, tile), jnp.float32),
                jax.ShapeDtypeStruct((tile, width), jnp.bfloat16),
            ],
            compiler_params=pltpu.CompilerParams(vmem_limit_bytes=24 << 20),
            cost_estimate=pl.CostEstimate(
                flops=2 * tile * width * (keys + width), bytes_accessed=tile * keys * 2, transcendentals=tile * keys
            ),
            name="scores",
        )
        outs = call(place, list_slot, block_counts, own, other, adapter_w, index_rows)
        for kept, value in zip((weights, tops, stats, codes, gathered), outs):
            kept.append(value)

    out_all = target_all = None
    for i in range(steps):
        rest = [] if i == 0 else [out_all, target_all]
        out_all, target_all = pl.pallas_call(
            back_kernel,
            grid=(2,),
            in_specs=[
                pl.BlockSpec((2, half), lambda k: (0, k)),
                pl.BlockSpec((1, half), lambda k: (0, k)),
                pl.BlockSpec((lists_here, half), lambda k: (0, k)),
                pl.BlockSpec((half, keys), lambda k: (k, 0)),
                WHOLE,
            ]
            + [pl.BlockSpec(memory_space=pl.ANY)] * len(rest),
            out_specs=[pl.BlockSpec((half, width), lambda k, i=i: (2 * i + k, 0))] * 2,
            out_shape=[
                jax.ShapeDtypeStruct((count, width), jnp.float32),
                jax.ShapeDtypeStruct((count, width), jnp.bfloat16),
            ],
            scratch_shapes=[
                pltpu.VMEM((half, keys), jnp.bfloat16),
                pltpu.VMEM((half, width), jnp.float32),
            ],
            input_output_aliases={5: 0, 6: 1} if rest else {},
            compiler_params=pltpu.CompilerParams(vmem_limit_bytes=24 << 20),
            cost_estimate=pl.CostEstimate(
                flops=2 * tile * width * keys, bytes_accessed=tile * keys * 2, transcendentals=0
            ),
            name="backs",
        )(stats[i], codes[i], tops[i], weights[i], index_rows, *rest)

    local_stats = jnp.concatenate(stats, axis=1)
    whole_stats = local_stats
    for axis in ("core", "x", "y", "z"):
        whole_stats = merge_axis(whole_stats, axis)

    placed = pl.BlockSpec((half, width), lambda i, place: (lax.rem(place[0] + chunk_of(i), 4), 0))
    mine, theirs = pl.pallas_call(
        scale_kernel,
        grid_spec=pltpu.PrefetchScalarGridSpec(
            num_scalar_prefetch=1,
            grid=(steps,),
            in_specs=[
                pl.BlockSpec((2, tile), lambda i, place: (0, i)),
                pl.BlockSpec((2, tile), lambda i, place: (0, i)),
                pl.BlockSpec((tile, width), lambda i, place: (i, 0)),
                pl.BlockSpec((tile, width), lambda i, place: (i, 0)),
            ],
            out_specs=[placed, placed],
            scratch_shapes=[pltpu.VMEM((tile, width), jnp.bfloat16)],
        ),
        out_shape=[jax.ShapeDtypeStruct((count // 2, width), jnp.bfloat16)] * 2,
        compiler_params=pltpu.CompilerParams(vmem_limit_bytes=24 << 20),
        name="scaled",
    )(place, local_stats, whole_stats, out_all, target_all)
    received = from_ahead(theirs, "core", 1)
    merged = (mine.astype(jnp.float32) + received.astype(jnp.float32)).astype(jnp.bfloat16)
    pieces = lax.all_to_all(merged, CHIPS, split_axis=0, concat_axis=0, tiled=True)
    back = jnp.sum(pieces.reshape(-1, queries.shape[0], width).astype(jnp.float32), axis=0)
    back_low = back.astype(jnp.bfloat16)
    query_grad = (
        back
        + lax.dot_general(back_low, adapter_w, (((1,), (1,)), ((), ())), preferred_element_type=jnp.float32)
    ).astype(jnp.bfloat16)
    b_own = spread_axes(back_low, CHIPS)
    b_other = from_ahead(b_own, "core", 1)
    third = width // 3
    column = pl.BlockSpec((tile, third), lambda i, place: (0, i))
    adapter_grad = pl.pallas_call(
        adapter_kernel,
        grid_spec=pltpu.PrefetchScalarGridSpec(
            num_scalar_prefetch=1,
            grid=(3,),
            in_specs=[column, column, column, column, WHOLE, WHOLE],
            out_specs=pl.BlockSpec((third, width), lambda i, place: (i, 0)),
            scratch_shapes=[
                pltpu.VMEM((count, third), jnp.bfloat16),
                pltpu.VMEM((count, width), jnp.bfloat16),
            ],
        ),
        out_shape=jax.ShapeDtypeStruct((width, width), jnp.float32),
        compiler_params=pltpu.CompilerParams(vmem_limit_bytes=24 << 20),
        cost_estimate=pl.CostEstimate(
            flops=2 * count * width * width, bytes_accessed=count * width * 4, transcendentals=0
        ),
        name="adapter",
    )(place, *gathered, b_own, b_other)
    return (query_grad, adapter_grad)


def solution(mesh):
    split = Mesh(mesh.devices.reshape(SIZES), AXES)
    placed = (
        P(AXES, None),
        P(),
        P(("z", "core"), ("y", "x"), None),
        P(AXES, None),
        P(),
        P(),
        P(AXES),
    )
    return jax.shard_map(
        all_steps,
        mesh=split,
        in_specs=placed,
        out_specs=(P(AXES, None), P()),
        check_vma=False,
    )
```

profile of v0, /device:TPU:1, one launch (start us, length us, event | category | flops | bytes accessed | tf_op | source)
XLA Modules:
  0.0 201.9 jit_solution(17121564926699853986)
XLA Ops:
  0.7 0.7 compare_select_fusion.1
  1.3 0.8 select_convert_fusion
  2.1 0.7 pad_maximum_fusion
  2.9 17.3 %all_to_all.25 = bf16[16,16,896]{2,1,0:T(8,128)(2,1)S(1)} all-to-all(bf16[16,16,896]{2,1,0:T(8,128)(2,1)S(1)} %broadcast_in_dim.57), channel_id=1, replica_groups=mesh['z'=4,'core'=2,'y'=4,'x'=4] {'y','x'}, dimensions={0} | all-to-all | bytes 917504 | tf_op jit(solution)/shard_map/all_to_all | solution.py:36
  20.2 3.8 %collective-permute-start.1 = (bf16[256,896]{1,0:T(8,128)(2,1)S(1)}, bf16[256,896]{1,0:T(8,128)(2,1)S(1)}, u32[]{:S(2)}, u32[]{:S(2)}) collective-permute-start(bf16[256,896]{1,0:T(8,128)(2,1)S(1)} %bitcast.10), channel_id=1, source_target_pairs={{32,0},{64,32},{96,64},{0,96},{33,1},{65,33},{97,65},{1,97},{34,2}... | collective-permute-start | bytes 1376264 | tf_op jit(solution)/shard_map/ppermute | solution.py:26
  23.9 0.0 collective-permute-start.3
  24.0 1.3 collective-permute-start.5
  25.3 2.6 %collective-permute-start = (bf16[256,896]{1,0:T(8,128)(2,1)S(1)}, bf16[256,896]{1,0:T(8,128)(2,1)S(1)}, u32[]{:S(2)}, u32[]{:S(2)}) collective-permute-start(bf16[256,896]{1,0:T(8,128)(2,1)S(1)} %bitcast.13), channel_id=1, source_target_pairs={{16,0},{0,16},{17,1},{1,17},{18,2},{2,18},{19,3},{3,19},{20,4},{4,... | collective-permute-start | bytes 1376264 | tf_op jit(solution)/shard_map/ppermute | solution.py:26
  27.9 0.1 pad_add_fusion.place
  28.0 5.8 %collective-permute-done.1.own_ref = bf16[256,896]{1,0:T(8,128)(2,1)S(1)} collective-permute-done((bf16[256,896]{1,0:T(8,128)(2,1)S(1)}, bf16[256,896]{1,0:T(8,128)(2,1)S(1)}, u32[]{:S(2)}, u32[]{:S(2)}) %collective-permute-start.1) | collective-permute-done | bytes 458784 | tf_op jit(solution)/shard_map/ppermute | solution.py:26
  33.7 10.8 %collective-permute-start.2 = (bf16[256,896]{1,0:T(8,128)(2,1)S(1)}, bf16[256,896]{1,0:T(8,128)(2,1)S(1)}, u32[]{:S(2)}, u32[]{:S(2)}) collective-permute-start(bf16[256,896]{1,0:T(8,128)(2,1)S(1)} %collective-permute-done.1.own_ref), channel_id=1, source_target_pairs={{16,0},{0,16},{17,1},{1,17},{18,2},{2,18},{19,3},{3,19},{20,4},{4,... | collective-permute-start | bytes 1376264 | tf_op jit(solution)/shard_map/ppermute | solution.py:26
  44.5 0.0 collective-permute-done.3.own_ref
  44.5 3.4 %collective-permute-start.4 = (bf16[256,896]{1,0:T(8,128)(2,1)S(1)}, bf16[256,896]{1,0:T(8,128)(2,1)S(1)}, u32[]{:S(2)}, u32[]{:S(2)}) collective-permute-start(bf16[256,896]{1,0:T(8,128)(2,1)S(1)} %collective-permute-done.3.own_ref), channel_id=1, source_target_pairs={{16,0},{0,16},{17,1},{1,17},{18,2},{2,18},{19,3},{3,19},{20,4},{4,... | collective-permute-start | bytes 1376264 | tf_op jit(solution)/shard_map/ppermute | solution.py:26
  47.9 0.0 collective-permute-done.5.own_ref
  47.9 0.0 collective-permute-start.6
  47.9 0.0 collective-permute-done.other_ref
  47.9 0.0 copy-start
  48.0 2.8 %copy-done = bf16[8,512,768]{2,1,0:T(8,128)(2,1)S(1)} copy-done((bf16[8,512,768]{2,1,0:T(8,128)(2,1)S(1)}, bf16[8,512,768]{2,1,0:T(8,128)(2,1)}, u32[]{:S(2)}) %copy-start) | copy-done | bytes 6291480
  50.7 1.3 copy-done.2
  52.0 0.7 copy-done.6
  52.7 0.7 copy-done.7
  53.3 7.9 %scores.4 = (bf16[512,4096]{1,0:T(8,128)(2,1)S(1)}, f32[8,512]{1,0:T(8,128)S(1)}, f32[2,512]{1,0:T(2,128)S(1)}, f32[1,512]{1,0:T(1,128)S(1)}, bf16[512,768]{1,0:T(8,128)(2,1)S(1)}) custom-call(s32[4]{0:T(128)S(1)} %pad_add_fusion.place, s32[64]{0:T(128)S(1)} %copy-done.6, s32[64]{0:T(128)S(1)} %copy-done.7, bf16[256,896]{1,0:T(8,128)(2,1)S(1)} %bitcast.14, ...), custom_call_target="tpu_custom_call" | custom-call | flops 3825205248 | bytes 4194304 | tf_op jit(solution)/shard_map/scores/pallas_call | solution.py:294
  61.3 0.0 collective-permute-done.2.other_ref
  61.3 0.0 copy-start.5
  61.3 1.3 copy-done.5
  62.7 8.2 %scores.5 = (bf16[512,4096]{1,0:T(8,128)(2,1)S(1)}, f32[8,512]{1,0:T(8,128)S(1)}, f32[2,512]{1,0:T(2,128)S(1)}, f32[1,512]{1,0:T(1,128)S(1)}, bf16[512,768]{1,0:T(8,128)(2,1)S(1)}) custom-call(s32[4]{0:T(128)S(1)} %pad_add_fusion.place, s32[64]{0:T(128)S(1)} %copy-done.6, s32[64]{0:T(128)S(1)} %copy-done.7, bf16[256,896]{1,0:T(8,128)(2,1)S(1)} %copy-done.5, ...), custom_call_target="tpu_custom_call" | custom-call | flops 3825205248 | bytes 4194304 | tf_op jit(solution)/shard_map/scores/pallas_call | solution.py:294
  70.9 0.0 copy-start.3
  70.9 0.0 collective-permute-done.4.other_ref
  70.9 8.2 %scores.6 = (bf16[512,4096]{1,0:T(8,128)(2,1)S(1)}, f32[8,512]{1,0:T(8,128)S(1)}, f32[2,512]{1,0:T(2,128)S(1)}, f32[1,512]{1,0:T(1,128)S(1)}, bf16[512,768]{1,0:T(8,128)(2,1)S(1)}) custom-call(s32[4]{0:T(128)S(1)} %pad_add_fusion.place, s32[64]{0:T(128)S(1)} %copy-done.6, s32[64]{0:T(128)S(1)} %copy-done.7, ...), custom_call_target="tpu_custom_call" | custom-call | flops 3825205248 | bytes 4194304 | tf_op jit(solution)/shard_map/scores/pallas_call | solution.py:294
  79.1 0.0 collective-permute-done.6.other_ref
  79.1 8.2 %scores.7 = (bf16[512,4096]{1,0:T(8,128)(2,1)S(1)}, f32[8,512]{1,0:T(8,128)S(1)}, f32[2,512]{1,0:T(2,128)S(1)}, f32[1,512]{1,0:T(1,128)S(1)}, bf16[512,768]{1,0:T(8,128)(2,1)S(1)}) custom-call(s32[4]{0:T(128)S(1)} %pad_add_fusion.place, s32[64]{0:T(128)S(1)} %copy-done.6, s32[64]{0:T(128)S(1)} %copy-done.7, ...), custom_call_target="tpu_custom_call" | custom-call | flops 3825205248 | bytes 4194304 | tf_op jit(solution)/shard_map/scores/pallas_call | solution.py:294
  87.3 0.8 collective-permute-start.7
  88.1 5.8 %backs.4 = (f32[2048,768]{1,0:T(8,128)S(1)}, bf16[2048,768]{1,0:T(8,128)(2,1)S(1)}) custom-call(f32[2,512]{1,0:T(2,128)S(1)} %get-tuple-element.32.stats_ref, f32[1,512]{1,0:T(1,128)S(1)} %get-tuple-element.45.code_ref, f32[8,512]{1,0:T(8,128)S(1)} %get-tuple-element.46.tops_ref, bf16[512,4096]{1,0:T(8,128)(2,1)S(1)} %copy-done.9, ...), custom_call_target="tpu_custom_call" | custom-call | flops 3221225472 | bytes 4194304 | tf_op jit(solution)/shard_map/backs/pallas_call | solution.py:301
  93.9 0.0 collective-permute-done.7
  94.0 0.2 collective-permute-start.10
  94.1 2.6 %collective-permute-start.8 = (f32[2,2048]{1,0:T(2,128)S(1)}, f32[2,2048]{1,0:T(2,128)S(1)}, u32[]{:S(2)}, u32[]{:S(2)}) collective-permute-start(f32[2,2048]{1,0:T(2,128)S(1)} %pad_maximum_fusion.1), channel_id=1, source_target_pairs={{1,0},{2,1},{3,2},{0,3},{5,4},{6,5},{7,6},{4,7},{9,8},{10,9},{11,1... | collective-permute-start | bytes 49160 | tf_op jit(solution)/shard_map/ppermute | solution.py:26
  96.7 0.0 collective-permute-start.9
  96.7 5.9 %backs.5 = (f32[2048,768]{1,0:T(8,128)S(1)}, bf16[2048,768]{1,0:T(8,128)(2,1)S(1)}) custom-call(f32[2,512]{1,0:T(2,128)S(1)} %get-tuple-element.33.stats_ref, f32[1,512]{1,0:T(1,128)S(1)} %get-tuple-element.42.code_ref, f32[8,512]{1,0:T(8,128)S(1)} %get-tuple-element.43.tops_ref, ...), custom_call_target="tpu_custom_call", output_to_operand_aliasing={{0}: (5, {}), {1}: (6, {})} | custom-call | flops 3221225472 | bytes 4194304 | tf_op jit(solution)/shard_map/backs/pallas_call | solution.py:301
  102.6 0.0 collective-permute-done.8
  102.6 0.0 collective-permute-done.9
  102.6 0.1 fusion.7
  102.8 0.1 collective-permute-start.11
  102.8 0.8 collective-permute-start.12
  103.6 0.8 collective-permute-start.13
  104.4 6.4 %backs.6 = (f32[2048,768]{1,0:T(8,128)S(1)}, bf16[2048,768]{1,0:T(8,128)(2,1)S(1)}) custom-call(f32[2,512]{1,0:T(2,128)S(1)} %get-tuple-element.34.stats_ref, f32[1,512]{1,0:T(1,128)S(1)} %get-tuple-element.39.code_ref, f32[8,512]{1,0:T(8,128)S(1)} %get-tuple-element.40.tops_ref, ...), custom_call_target="tpu_custom_call", output_to_operand_aliasing={{0}: (5, {}), {1}: (6, {})} | custom-call | flops 3221225472 | bytes 4194304 | tf_op jit(solution)/shard_map/backs/pallas_call | solution.py:301
  110.8 0.1 fusion.4
  110.9 2.2 %collective-permute-start.14 = (f32[2,2048]{1,0:T(2,128)S(1)}, f32[2,2048]{1,0:T(2,128)S(1)}, u32[]{:S(2)}, u32[]{:S(2)}) collective-permute-start(f32[2,2048]{1,0:T(2,128)S(1)} %pad_maximum_fusion.3), channel_id=1, source_target_pairs={{32,0},{64,32},{96,64},{0,96},{33,1},{65,33},{97,65},{1,97},{34,2}... | collective-permute-start | bytes 49160 | tf_op jit(solution)/shard_map/ppermute | solution.py:26
  113.1 5.9 %backs.7 = (f32[2048,768]{1,0:T(8,128)S(1)}, bf16[2048,768]{1,0:T(8,128)(2,1)S(1)}) custom-call(f32[2,512]{1,0:T(2,128)S(1)} %get-tuple-element.35.stats_ref, f32[1,512]{1,0:T(1,128)S(1)} %get-tuple-element.36.code_ref, f32[8,512]{1,0:T(8,128)S(1)} %get-tuple-element.37.tops_ref, ...), custom_call_target="tpu_custom_call", output_to_operand_aliasing={{0}: (5, {}), {1}: (6, {})} | custom-call | flops 3221225472 | bytes 4194304 | tf_op jit(solution)/shard_map/backs/pallas_call | solution.py:301
  119.0 0.1 collective-permute-start.15
  119.1 1.4 collective-permute-start.16
  120.5 2.7 %collective-permute-done.15 = f32[2,2048]{1,0:T(2,128)S(1)} collective-permute-done((f32[2,2048]{1,0:T(2,128)S(1)}, f32[2,2048]{1,0:T(2,128)S(1)}, u32[]{:S(2)}, u32[]{:S(2)}) %collective-permute-start.15) | collective-permute-done | bytes 16416 | tf_op jit(solution)/shard_map/ppermute | solution.py:26
  123.3 0.1 fusion.1
  123.4 2.2 %scaled.1 = (bf16[1024,768]{1,0:T(8,128)(2,1)S(1)}, bf16[1024,768]{1,0:T(8,128)(2,1)S(1)}) custom-call(s32[4]{0:T(128)S(1)} %pad_add_fusion.place, f32[2,2048]{1,0:T(2,128)S(1)} %constant_dynamic-update-slice_fusion.local_ref, f32[2,2048]{1,0:T(2,128)S(1)} %pad_maximum_fusion.7.whole_ref, f32[2048,768]{1,0:T(8,128)S(1)} %get-tuple-element.54.out_ref, ...), custom_call_target="tpu_custom_call" | custom-call | tf_op jit(solution)/shard_map/scaled/pallas_call | solution.py:335
  125.6 2.5 %collective-permute-start.17 = (bf16[1024,768]{1,0:T(8,128)(2,1)S(1)}, bf16[1024,768]{1,0:T(8,128)(2,1)S(1)}, u32[]{:S(2)}, u32[]{:S(2)}) collective-permute-start(bf16[1024,768]{1,0:T(8,128)(2,1)S(1)} %get-tuple-element.57), channel_id=1, source_target_pairs={{16,0},{0,16},{17,1},{1,17},{18,2},{2,18},{19,3},{3,19},{20,4},{4,... | collective-permute-start | bytes 4718600 | tf_op jit(solution)/shard_map/ppermute | solution.py:26
  128.1 3.0 %collective-permute-done.17 = bf16[1024,768]{1,0:T(8,128)(2,1)S(1)} collective-permute-done((bf16[1024,768]{1,0:T(8,128)(2,1)S(1)}, bf16[1024,768]{1,0:T(8,128)(2,1)S(1)}, u32[]{:S(2)}, u32[]{:S(2)}) %collective-permute-start.17) | collective-permute-done | bytes 1572896 | tf_op jit(solution)/shard_map/ppermute | solution.py:26
  131.1 0.5 add_convert_fusion
  131.6 30.2 %all_to_all.26 = bf16[64,16,768]{2,1,0:T(8,128)(2,1)S(1)} all-to-all(bf16[64,16,768]{2,1,0:T(8,128)(2,1)S(1)} %bitcast.15), channel_id=1, replica_groups=mesh['z'=4,'core'=2,'y'=4,'x'=4] {'z','y','x'}, dimensions={0} | all-to-all | bytes 3145728 | tf_op jit(solution)/shard_map/all_to_all | solution.py:355
  161.8 0.2 convert_reduce_fusion
  162.1 0.1 broadcast_in_dim.58
  162.2 28.8 %all_to_all.27 = bf16[64,16,768]{2,1,0:T(8,128)(2,1)S(1)} all-to-all(bf16[64,16,768]{2,1,0:T(8,128)(2,1)S(1)} %broadcast_in_dim.58), channel_id=1, replica_groups=mesh['z'=4,'core'=2,'y'=4,'x'=4] {'z','y','x'}, dimensions={0} | all-to-all | bytes 3145728 | tf_op jit(solution)/shard_map/all_to_all | solution.py:36
  190.9 2.5 %collective-permute-start.18 = (bf16[1024,768]{1,0:T(8,128)(2,1)S(1)}, bf16[1024,768]{1,0:T(8,128)(2,1)S(1)}, u32[]{:S(2)}, u32[]{:S(2)}) collective-permute-start(bf16[1024,768]{1,0:T(8,128)(2,1)S(1)} %bitcast.8), channel_id=1, source_target_pairs={{16,0},{0,16},{17,1},{1,17},{18,2},{2,18},{19,3},{3,19},{20,4},{4,... | collective-permute-start | bytes 4718600 | tf_op jit(solution)/shard_map/ppermute | solution.py:26
  193.4 1.1 fusion
  194.5 2.0 collective-permute-done.18.b_other
  196.5 5.4 %adapter.1 = f32[768,768]{1,0:T(8,128)} custom-call(s32[4]{0:T(128)S(1)} %pad_add_fusion.place, bf16[512,768]{1,0:T(8,128)(2,1)S(1)} %get-tuple-element.58.q0, bf16[512,768]{1,0:T(8,128)(2,1)S(1)} %get-tuple-element.59.q1, bf16[512,768]{1,0:T(8,128)(2,1)S(1)} %get-tuple-element.60.q2, bf16[512,768]{1,0:T(8,128)(2,1)S(1)} %get-tuple-element.61.q3, ...), custom_call_target="tpu_custom_call" | custom-call | flops 2415919104 | bytes 6291456 | tf_op jit(solution)/shard_map/adapter/pallas_call | solution.py:366
  (38 shorter events, 0.3 us)
Async XLA Ops:
  20.2 13.5 %collective-permute-start.1 = (bf16[256,896]{1,0:T(8,128)(2,1)S(1)}, bf16[256,896]{1,0:T(8,128)(2,1)S(1)}, u32[]{:S(2)}, u32[]{:S(2)}) collective-permute-start(bf16[256,896]{1,0:T(8,128)(2,1)S(1)} %bitcast.10), channel_id=1, source_target_pairs={{32,0},{64,32},{96,64},{0,96},{33,1},{65,33},{97,65},{1,97},{34,2}... | collective-permute-start | bytes 1376264 | tf_op jit(solution)/shard_map/ppermute | solution.py:26
  23.9 20.6 %collective-permute-start.3 = (bf16[256,896]{1,0:T(8,128)(2,1)S(1)}, bf16[256,896]{1,0:T(8,128)(2,1)S(1)}, u32[]{:S(2)}, u32[]{:S(2)}) collective-permute-start(bf16[256,896]{1,0:T(8,128)(2,1)S(1)} %bitcast.11), channel_id=1, source_target_pairs={{96,0},{0,32},{32,64},{64,96},{97,1},{1,33},{33,65},{65,97},{98,2}... | collective-permute-start | bytes 1376264 | tf_op jit(solution)/shard_map/ppermute | solution.py:26
  24.0 24.0 %collective-permute-start.5 = (bf16[256,896]{1,0:T(8,128)(2,1)S(1)}, bf16[256,896]{1,0:T(8,128)(2,1)S(1)}, u32[]{:S(2)}, u32[]{:S(2)}) collective-permute-start(bf16[256,896]{1,0:T(8,128)(2,1)S(1)} %bitcast.12), channel_id=1, source_target_pairs={{64,0},{96,32},{0,64},{32,96},{65,1},{97,33},{1,65},{33,97},{66,2}... | collective-permute-start | bytes 1376264 | tf_op jit(solution)/shard_map/ppermute | solution.py:26
  25.3 22.7 %collective-permute-start = (bf16[256,896]{1,0:T(8,128)(2,1)S(1)}, bf16[256,896]{1,0:T(8,128)(2,1)S(1)}, u32[]{:S(2)}, u32[]{:S(2)}) collective-permute-start(bf16[256,896]{1,0:T(8,128)(2,1)S(1)} %bitcast.13), channel_id=1, source_target_pairs={{16,0},{0,16},{17,1},{1,17},{18,2},{2,18},{19,3},{3,19},{20,4},{4,... | collective-permute-start | bytes 1376264 | tf_op jit(solution)/shard_map/ppermute | solution.py:26
  33.7 27.5 %copy-start.4 = (bf16[256,896]{1,0:T(8,128)(2,1)}, bf16[256,896]{1,0:T(8,128)(2,1)S(1)}, u32[]{:S(2)}) copy-start(bf16[256,896]{1,0:T(8,128)(2,1)S(1)} %collective-permute-done.1.own_ref) | copy-start | bytes 1376260
  33.7 27.5 %collective-permute-start.2 = (bf16[256,896]{1,0:T(8,128)(2,1)S(1)}, bf16[256,896]{1,0:T(8,128)(2,1)S(1)}, u32[]{:S(2)}, u32[]{:S(2)}) collective-permute-start(bf16[256,896]{1,0:T(8,128)(2,1)S(1)} %collective-permute-done.1.own_ref), channel_id=1, source_target_pairs={{16,0},{0,16},{17,1},{1,17},{18,2},{2,18},{19,3},{3,19},{20,4},{4,... | collective-permute-start | bytes 1376264 | tf_op jit(solution)/shard_map/ppermute | solution.py:26
  44.5 26.4 %collective-permute-start.4 = (bf16[256,896]{1,0:T(8,128)(2,1)S(1)}, bf16[256,896]{1,0:T(8,128)(2,1)S(1)}, u32[]{:S(2)}, u32[]{:S(2)}) collective-permute-start(bf16[256,896]{1,0:T(8,128)(2,1)S(1)} %collective-permute-done.3.own_ref), channel_id=1, source_target_pairs={{16,0},{0,16},{17,1},{1,17},{18,2},{2,18},{19,3},{3,19},{20,4},{4,... | collective-permute-start | bytes 1376264 | tf_op jit(solution)/shard_map/ppermute | solution.py:26
  47.9 31.2 %collective-permute-start.6 = (bf16[256,896]{1,0:T(8,128)(2,1)S(1)}, bf16[256,896]{1,0:T(8,128)(2,1)S(1)}, u32[]{:S(2)}, u32[]{:S(2)}) collective-permute-start(bf16[256,896]{1,0:T(8,128)(2,1)S(1)} %collective-permute-done.5.own_ref), channel_id=1, source_target_pairs={{16,0},{0,16},{17,1},{1,17},{18,2},{2,18},{19,3},{3,19},{20,4},{4,... | collective-permute-start | bytes 1376264 | tf_op jit(solution)/shard_map/ppermute | solution.py:26
  47.9 2.8 %copy-start = (bf16[8,512,768]{2,1,0:T(8,128)(2,1)S(1)}, bf16[8,512,768]{2,1,0:T(8,128)(2,1)}, u32[]{:S(2)}) copy-start(bf16[8,512,768]{2,1,0:T(8,128)(2,1)} %rows_ref.15) | copy-start | bytes 18874372
  50.7 1.3 copy-start.2
  52.0 0.7 copy-start.6
  52.7 0.7 copy-start.7
  53.3 8.0 %copy-start.1 = (bf16[8,512,768]{2,1,0:T(8,128)(2,1)S(1)}, bf16[8,512,768]{2,1,0:T(8,128)(2,1)}, u32[]{:S(2)}) copy-start(bf16[8,512,768]{2,1,0:T(8,128)(2,1)} %rows_ref.15) | copy-start | bytes 18874372
  61.3 9.6 %copy-start.8 = (bf16[512,4096]{1,0:T(8,128)(2,1)}, bf16[512,4096]{1,0:T(8,128)(2,1)S(1)}, u32[]{:S(2)}) copy-start(bf16[512,4096]{1,0:T(8,128)(2,1)S(1)} %get-tuple-element.47.p_ref) | copy-start | bytes 12582916
  61.3 1.4 copy-start.5
  70.9 8.2 %copy-start.3 = (bf16[768,768]{1,0:T(8,128)(2,1)S(1)}, bf16[768,768]{1,0:T(8,128)(2,1)}, u32[]{:S(2)}) copy-start(bf16[768,768]{1,0:T(8,128)(2,1)} %w_ref.7) | copy-start | bytes 3538948
  79.1 9.0 %copy-start.9 = (bf16[512,4096]{1,0:T(8,128)(2,1)S(1)}, bf16[512,4096]{1,0:T(8,128)(2,1)}, u32[]{:S(2)}) copy-start(bf16[512,4096]{1,0:T(8,128)(2,1)} %copy-done.8) | copy-start | bytes 12582916
  87.3 6.6 %collective-permute-start.7 = (f32[2,2048]{1,0:T(2,128)S(1)}, f32[2,2048]{1,0:T(2,128)S(1)}, u32[]{:S(2)}, u32[]{:S(2)}) collective-permute-start(f32[2,2048]{1,0:T(2,128)S(1)} %constant_dynamic-update-slice_fusion.local_ref), channel_id=1, source_target_pairs={{16,0},{0,16},{17,1},{1,17},{18,2},{2,18},{19,3},{3,19},{20,4},{4,... | collective-permute-start | bytes 49160 | tf_op jit(solution)/shard_map/ppermute | solution.py:26
  94.0 8.7 %collective-permute-start.10 = (f32[2,2048]{1,0:T(2,128)S(1)}, f32[2,2048]{1,0:T(2,128)S(1)}, u32[]{:S(2)}, u32[]{:S(2)}) collective-permute-start(f32[2,2048]{1,0:T(2,128)S(1)} %pad_maximum_fusion.1), channel_id=1, source_target_pairs={{3,0},{0,1},{1,2},{2,3},{7,4},{4,5},{5,6},{6,7},{11,8},{8,9},{9,10... | collective-permute-start | bytes 49160 | tf_op jit(solution)/shard_map/ppermute | solution.py:26
  94.1 8.5 %collective-permute-start.8 = (f32[2,2048]{1,0:T(2,128)S(1)}, f32[2,2048]{1,0:T(2,128)S(1)}, u32[]{:S(2)}, u32[]{:S(2)}) collective-permute-start(f32[2,2048]{1,0:T(2,128)S(1)} %pad_maximum_fusion.1), channel_id=1, source_target_pairs={{1,0},{2,1},{3,2},{0,3},{5,4},{6,5},{7,6},{4,7},{9,8},{10,9},{11,1... | collective-permute-start | bytes 49160 | tf_op jit(solution)/shard_map/ppermute | solution.py:26
  96.7 5.9 %collective-permute-start.9 = (f32[2,2048]{1,0:T(2,128)S(1)}, f32[2,2048]{1,0:T(2,128)S(1)}, u32[]{:S(2)}, u32[]{:S(2)}) collective-permute-start(f32[2,2048]{1,0:T(2,128)S(1)} %pad_maximum_fusion.1), channel_id=1, source_target_pairs={{2,0},{3,1},{0,2},{1,3},{6,4},{7,5},{4,6},{5,7},{10,8},{11,9},{8,1... | collective-permute-start | bytes 49160 | tf_op jit(solution)/shard_map/ppermute | solution.py:26
  102.8 8.0 %collective-permute-start.11 = (f32[2,2048]{1,0:T(2,128)S(1)}, f32[2,2048]{1,0:T(2,128)S(1)}, u32[]{:S(2)}, u32[]{:S(2)}) collective-permute-start(f32[2,2048]{1,0:T(2,128)S(1)} %pad_maximum_fusion.2), channel_id=1, source_target_pairs={{4,0},{8,4},{12,8},{0,12},{5,1},{9,5},{13,9},{1,13},{6,2},{10,6},{... | collective-permute-start | bytes 49160 | tf_op jit(solution)/shard_map/ppermute | solution.py:26
  102.8 7.9 %collective-permute-start.12 = (f32[2,2048]{1,0:T(2,128)S(1)}, f32[2,2048]{1,0:T(2,128)S(1)}, u32[]{:S(2)}, u32[]{:S(2)}) collective-permute-start(f32[2,2048]{1,0:T(2,128)S(1)} %pad_maximum_fusion.2), channel_id=1, source_target_pairs={{8,0},{12,4},{0,8},{4,12},{9,1},{13,5},{1,9},{5,13},{10,2},{14,6},... | collective-permute-start | bytes 49160 | tf_op jit(solution)/shard_map/ppermute | solution.py:26
  103.6 7.2 %collective-permute-start.13 = (f32[2,2048]{1,0:T(2,128)S(1)}, f32[2,2048]{1,0:T(2,128)S(1)}, u32[]{:S(2)}, u32[]{:S(2)}) collective-permute-start(f32[2,2048]{1,0:T(2,128)S(1)} %pad_maximum_fusion.2), channel_id=1, source_target_pairs={{12,0},{0,4},{4,8},{8,12},{13,1},{1,5},{5,9},{9,13},{14,2},{2,6},{... | collective-permute-start | bytes 49160 | tf_op jit(solution)/shard_map/ppermute | solution.py:26
  110.9 9.6 %collective-permute-start.14 = (f32[2,2048]{1,0:T(2,128)S(1)}, f32[2,2048]{1,0:T(2,128)S(1)}, u32[]{:S(2)}, u32[]{:S(2)}) collective-permute-start(f32[2,2048]{1,0:T(2,128)S(1)} %pad_maximum_fusion.3), channel_id=1, source_target_pairs={{32,0},{64,32},{96,64},{0,96},{33,1},{65,33},{97,65},{1,97},{34,2}... | collective-permute-start | bytes 49160 | tf_op jit(solution)/shard_map/ppermute | solution.py:26
  119.0 4.2 %collective-permute-start.15 = (f32[2,2048]{1,0:T(2,128)S(1)}, f32[2,2048]{1,0:T(2,128)S(1)}, u32[]{:S(2)}, u32[]{:S(2)}) collective-permute-start(f32[2,2048]{1,0:T(2,128)S(1)} %pad_maximum_fusion.3), channel_id=1, source_target_pairs={{64,0},{96,32},{0,64},{32,96},{65,1},{97,33},{1,65},{33,97},{66,2}... | collective-permute-start | bytes 49160 | tf_op jit(solution)/shard_map/ppermute | solution.py:26
  119.1 4.1 %collective-permute-start.16 = (f32[2,2048]{1,0:T(2,128)S(1)}, f32[2,2048]{1,0:T(2,128)S(1)}, u32[]{:S(2)}, u32[]{:S(2)}) collective-permute-start(f32[2,2048]{1,0:T(2,128)S(1)} %pad_maximum_fusion.3), channel_id=1, source_target_pairs={{96,0},{0,32},{32,64},{64,96},{97,1},{1,33},{33,65},{65,97},{98,2}... | collective-permute-start | bytes 49160 | tf_op jit(solution)/shard_map/ppermute | solution.py:26
  125.6 5.5 %collective-permute-start.17 = (bf16[1024,768]{1,0:T(8,128)(2,1)S(1)}, bf16[1024,768]{1,0:T(8,128)(2,1)S(1)}, u32[]{:S(2)}, u32[]{:S(2)}) collective-permute-start(bf16[1024,768]{1,0:T(8,128)(2,1)S(1)} %get-tuple-element.57), channel_id=1, source_target_pairs={{16,0},{0,16},{17,1},{1,17},{18,2},{2,18},{19,3},{3,19},{20,4},{4,... | collective-permute-start | bytes 4718600 | tf_op jit(solution)/shard_map/ppermute | solution.py:26
  190.9 5.5 %collective-permute-start.18 = (bf16[1024,768]{1,0:T(8,128)(2,1)S(1)}, bf16[1024,768]{1,0:T(8,128)(2,1)S(1)}, u32[]{:S(2)}, u32[]{:S(2)}) collective-permute-start(bf16[1024,768]{1,0:T(8,128)(2,1)S(1)} %bitcast.8), channel_id=1, source_target_pairs={{16,0},{0,16},{17,1},{1,17},{18,2},{2,18},{19,3},{3,19},{20,4},{4,... | collective-permute-start | bytes 4718600 | tf_op jit(solution)/shard_map/ppermute | solution.py:26
where the time goes:
time: 202 us
  blocking collectives  76.3 us (38%)
  Pallas kernels  64.1 us (32%)
  starting transfers between devices  35.7 us (18%)
  waiting for transfers between devices  13.5 us (7%)
  local copies, waits for them, and re-layouts  6.91 us (3%)
  other arithmetic  3.4 us (2%)
    all_to_all x2, blocking collectives, spread_axes(): return lax.all_to_all(spread, axes, split_axis=0, concat_axis=0, tiled=True)  46.1 us
    ppermute x19, starting transfers between devices, from_ahead(): lax.ppermute(value, axis, [((i + step) % size, i) for i in range(size)])  35.7 us
    pallas_call x4, Pallas kernels, all_steps(): call(place, list_slot, block_counts, own, other, adapter_w, index_rows)  32.5 us
    all_to_all x1, blocking collectives, all_steps(): lax.all_to_all(merged, CHIPS, split_axis=0, concat_axis=0, tiled=True)  30.2 us
    pallas_call x4, Pallas kernels, all_steps(): pl.pallas_call(back_kernel, grid=(2,), in_specs=[pl.BlockSpec((2, half),...  23.9 us
    ppermute x19, waiting for transfers between devices, from_ahead(): lax.ppermute(value, axis, [((i + step) % size, i) for i in range(size)])  13.5 us
    unnamed x23, local copies, waits for them, and re-layouts  6.75 us
    pallas_call x1, Pallas kernels, all_steps(): pl.pallas_call(adapter_kernel, grid_spec=pltpu.PrefetchScalarGridSpec(num...  5.44 us
  transfers between devices with their start and end apart: 19, of which 4 were waited for; matrix products, arithmetic and copies ran while one was open for 1% of the time, Pallas kernels for 24%

commit v1 on v0

--- a/solution.py
+++ b/solution.py
@@ -45,7 +45,7 @@
 
 
 def score_kernel(
-    place, list_slot, block_counts, own_ref, other_ref, w_ref, rows_ref,
+    table, place, own_ref, other_ref, w_ref, rows_ref,
     p_ref, tops_ref, stats_ref, code_ref, q_out, q_ref, bias_ref, s_ref, here_ref,
 ):
     width = w_ref.shape[0]
@@ -55,13 +55,13 @@
     core = pl.program_id(0)
 
     def find(n, _):
-        at = list_slot[n] - place[2]
+        at = place[4 + n] - place[2]
         here_ref[jnp.where((at >= 0) & (at < lists), at, lists)] = n
         return 0
 
-    lax.fori_loop(0, list_slot.shape[0], find, 0)
+    lax.fori_loop(0, table, find, 0)
     here = [here_ref[j] for j in range(lists)]
-    total_rows = [ROWS * block_counts[n] for n in here]
+    total_rows = [ROWS * place[4 + table + n] for n in here]
     live = [n - place[3] for n in total_rows]
 
     @pl.when(core == place[1])
@@ -73,11 +73,7 @@
         q_ref[...] = other_ref[...]
 
     queries = q_ref[:, :width]
-    q_out[...] = queries
-    adapted = (
-        queries.astype(jnp.float32) + jnp.dot(queries, w_ref[...], preferred_element_type=jnp.float32)
-    ).astype(jnp.bfloat16)
-
+    q_out[...] = queries.astype(jnp.float32).T.astype(jnp.bfloat16)
     info = q_ref[:, width:].astype(jnp.float32).T
     probes = info[0:PROBES, :]
     number = lax.broadcasted_iota(jnp.int32, (PROBES, tile), 0).astype(jnp.float32)
@@ -99,8 +95,13 @@
         bias_ref[j] = lanes_of(bias[:, j : j + 1], tile)
     bias_ref[lists] = jnp.full((tile, LANES), NEG_FILL, jnp.float32)
 
+    adapted = (
+        queries.astype(jnp.float32) + jnp.dot(queries, w_ref[...], preferred_element_type=jnp.float32)
+    ).astype(jnp.bfloat16)
+
     lane = lax.broadcasted_iota(jnp.int32, (tile, LANES), 1)
     blocks = per // LANES
+    rows_at = pl.ds(pl.multiple_of(core * tile, tile), tile)
 
     def matmul(j):
         raw = lax.dot_general(
@@ -121,7 +122,7 @@
             weight = jnp.exp2(s_ref[j % 2, :, b * LANES : (b + 1) * LANES] * factor - peak)
             total = weight if total is None else total + weight
             at = j * per + b * LANES
-            p_ref[:, at : at + LANES] = weight.astype(jnp.bfloat16)
+            p_ref[rows_at, at : at + LANES] = weight.astype(jnp.bfloat16)
         return peak, lanes_of(jnp.sum(total, axis=1, keepdims=True), tile)
 
     tops = jnp.full((tile, LANES), NEG_FILL, jnp.float32)
@@ -144,14 +145,15 @@
 def back_kernel(stats_ref, code_ref, tops_ref, p_ref, rows_ref, *refs):
     out_ref, target_ref, g_ref, row_ref = refs[-4:]
     lists, per, width = rows_ref.shape
-    tile = p_ref.shape[0]
+    tile = tops_ref.shape[1]
+    rows_at = pl.ds(pl.multiple_of(pl.program_id(0) * tile, tile), tile)
     share = columns_of(jnp.exp2(tops_ref[...] - stats_ref[0:1, :]), tile)
     acc = None
     for j in range(lists):
         part = lanes_of(share[:, j : j + 1], tile)
         for b in range(per // LANES):
             at = j * per + b * LANES
-            g_ref[:, at : at + LANES] = (p_ref[:, at : at + LANES].astype(jnp.float32) * part).astype(jnp.bfloat16)
+            g_ref[:, at : at + LANES] = (p_ref[rows_at, at : at + LANES].astype(jnp.float32) * part).astype(jnp.bfloat16)
         out = jnp.dot(g_ref[:, j * per : (j + 1) * per], rows_ref[j], preferred_element_type=jnp.float32)
         acc = out if acc is None else acc + out
     out_ref[...] = acc
@@ -191,7 +193,7 @@
 
 
 def adapter_kernel(place, q0, q1, q2, q3, b_own, b_other, out_ref, q_ref, b_ref):
-    tile = q0.shape[0]
+    tile = q0.shape[1]
     half = tile // 2
     count = 4 * tile
 
@@ -204,10 +206,8 @@
 
     for ahead, q in zip(ORDER, (q0, q1, q2, q3)):
         to = pl.multiple_of(lax.rem(place[0] + ahead, 4) * tile, tile)
-        q_ref[pl.ds(to, tile), :] = q[...]
-    out_ref[...] = lax.dot_general(
-        q_ref[...], b_ref[...], (((0,), (0,)), ((), ())), preferred_element_type=jnp.float32
-    ) * (1.0 / math.sqrt(count))
+        q_ref[:, pl.ds(to, tile)] = q[...]
+    out_ref[...] = jnp.dot(q_ref[...], b_ref[...], preferred_element_type=jnp.float32) * (1.0 / math.sqrt(count))
 
 
 def merge_axis(stats, axis):
@@ -232,7 +232,10 @@
     first_slot = (place_z * 2 + place_c) * lists_here
     first_row = (place_y * 4 + place_x) * rows_here
     list_length = rows_here * 16
-    place = jnp.stack([place_z, place_c, first_slot, first_row]).astype(jnp.int32)
+    table = list_slot.shape[0]
+    place = jnp.concatenate(
+        [jnp.stack([place_z, place_c, first_slot, first_row]).astype(jnp.int32), list_slot, block_counts]
+    )
 
     lane = jnp.arange(LANES, dtype=jnp.int32)[None, :]
     raw_row = lax.rem(target_raw, list_length)[:, None]
@@ -240,7 +243,9 @@
     info = jnp.where(lane == PROBES, lax.div(target_raw, list_length)[:, None], info)
     info = jnp.where(lane == PROBES + 1, lax.div(raw_row, 64), info)
     info = jnp.where(lane == PROBES + 2, lax.rem(raw_row, 64), info)
-    plane = spread_axes(jnp.concatenate([queries, info.astype(jnp.bfloat16)], axis=1), ("y", "x"))
+    packed = jnp.concatenate([queries, info.astype(jnp.bfloat16)], axis=1)
+    packed, place = lax.optimization_barrier((packed, place))
+    plane = spread_axes(packed, ("y", "x"))
 
     half = plane.shape[0]
     tile = 2 * half
@@ -254,9 +259,9 @@
     for ahead, own in zip(ORDER, owns):
         other = from_ahead(own, "core", 1)
         call = pl.pallas_call(
-            score_kernel,
+            functools.partial(score_kernel, table),
             grid_spec=pltpu.PrefetchScalarGridSpec(
-                num_scalar_prefetch=3,
+                num_scalar_prefetch=1,
                 grid=(2,),
                 in_specs=[
                     pl.BlockSpec((half, width + LANES), lambda i, *_: (0, 0)),
@@ -265,11 +270,11 @@
                     WHOLE,
                 ],
                 out_specs=[
-                    pl.BlockSpec((half, keys), lambda i, *_: (i, 0)),
+                    WHOLE,
                     pl.BlockSpec((lists_here, half), lambda i, *_: (0, i)),
                     pl.BlockSpec((2, half), lambda i, *_: (0, i)),
                     pl.BlockSpec((1, half), lambda i, *_: (0, i)),
-                    pl.BlockSpec((half, width), lambda i, *_: (i, 0)),
+                    pl.BlockSpec((width, half), lambda i, *_: (0, i)),
                 ],
                 scratch_shapes=[
                     pltpu.VMEM((half, width + LANES), jnp.bfloat16),
@@ -283,15 +288,15 @@
                 jax.ShapeDtypeStruct((lists_here, tile), jnp.float32),
                 jax.ShapeDtypeStruct((2, tile), jnp.float32),
                 jax.ShapeDtypeStruct((1, tile), jnp.float32),
-                jax.ShapeDtypeStruct((tile, width), jnp.bfloat16),
+                jax.ShapeDtypeStruct((width, tile), jnp.bfloat16),
             ],
-            compiler_params=pltpu.CompilerParams(vmem_limit_bytes=24 << 20),
+            compiler_params=pltpu.CompilerParams(vmem_limit_bytes=16 << 20),
             cost_estimate=pl.CostEstimate(
                 flops=2 * tile * width * (keys + width), bytes_accessed=tile * keys * 2, transcendentals=tile * keys
             ),
             name="scores",
         )
-        outs = call(place, list_slot, block_counts, own, other, adapter_w, index_rows)
+        outs = call(place, own, other, adapter_w, index_rows)
         for kept, value in zip((weights, tops, stats, codes, gathered), outs):
             kept.append(value)
 
@@ -305,7 +310,7 @@
                 pl.BlockSpec((2, half), lambda k: (0, k)),
                 pl.BlockSpec((1, half), lambda k: (0, k)),
                 pl.BlockSpec((lists_here, half), lambda k: (0, k)),
-                pl.BlockSpec((half, keys), lambda k: (k, 0)),
+                WHOLE,
                 WHOLE,
             ]
             + [pl.BlockSpec(memory_space=pl.ANY)] * len(rest),
@@ -362,7 +367,7 @@
     b_own = spread_axes(back_low, CHIPS)
     b_other = from_ahead(b_own, "core", 1)
     third = width // 3
-    column = pl.BlockSpec((tile, third), lambda i, place: (0, i))
+    column = pl.BlockSpec((third, tile), lambda i, place: (i, 0))
     adapter_grad = pl.pallas_call(
         adapter_kernel,
         grid_spec=pltpu.PrefetchScalarGridSpec(
@@ -371,7 +376,7 @@
             in_specs=[column, column, column, column, WHOLE, WHOLE],
             out_specs=pl.BlockSpec((third, width), lambda i, place: (i, 0)),
             scratch_shapes=[
-                pltpu.VMEM((count, third), jnp.bfloat16),
+                pltpu.VMEM((third, count), jnp.bfloat16),
                 pltpu.VMEM((count, width), jnp.bfloat16),
             ],
         ),

time: 202 us -> 205 us (1.015)
  local copies, waits for them, and re-layouts: 6.91 us -> 9.14 us
    unnamed x23 -> x15, local copies, waits for them, and re-layouts: 6.75 us -> 8.24 us
where the time goes in v1:
time: 205 us
  blocking collectives  76.3 us (37%)
  Pallas kernels  64.6 us (32%)
  starting transfers between devices  35.7 us (17%)
  waiting for transfers between devices  13.6 us (7%)
  local copies, waits for them, and re-layouts  9.14 us (4%)
  other arithmetic  3.27 us (2%)
    all_to_all x2, blocking collectives, spread_axes(): return lax.all_to_all(spread, axes, split_axis=0, concat_axis=0, tiled=True)  46.1 us
    ppermute x19, starting transfers between devices, from_ahead(): lax.ppermute(value, axis, [((i + step) % size, i) for i in range(size)])  35.7 us
    pallas_call x4, Pallas kernels, all_steps(): outs = call(place, own, other, adapter_w, index_rows)  33.4 us
    all_to_all x1, blocking collectives, all_steps(): lax.all_to_all(merged, CHIPS, split_axis=0, concat_axis=0, tiled=True)  30.2 us
    pallas_call x4, Pallas kernels, all_steps(): pl.pallas_call(back_kernel, grid=(2,), in_specs=[pl.BlockSpec((2, half),...  23.9 us
    ppermute x19, waiting for transfers between devices, from_ahead(): lax.ppermute(value, axis, [((i + step) % size, i) for i in range(size)])  13.6 us
    unnamed x15, local copies, waits for them, and re-layouts  8.24 us
    pallas_call x1, Pallas kernels, all_steps(): pl.pallas_call(adapter_kernel, grid_spec=pltpu.PrefetchScalarGridSpec(num...  5.02 us
  transfers between devices with their start and end apart: 19, of which 4 were waited for; matrix products, arithmetic and copies ran while one was open for 1% of the time, Pallas kernels for 24%

profile of v1, /device:TPU:1, one launch (start us, length us, event | category | flops | bytes accessed | tf_op | source)
XLA Modules:
  0.0 204.5 jit_solution(18213279867801189298)
XLA Ops:
  0.7 0.7 compare_select_fusion.1
  1.4 0.8 select_convert_fusion
  2.1 0.7 pad_maximum_fusion
  2.9 0.7 concatenate.19.place
  3.7 17.3 %all_to_all.25 = bf16[16,16,896]{2,1,0:T(8,128)(2,1)S(1)} all-to-all(bf16[16,16,896]{2,1,0:T(8,128)(2,1)S(1)} %broadcast_in_dim.57), channel_id=1, replica_groups=mesh['z'=4,'core'=2,'y'=4,'x'=4] {'y','x'}, dimensions={0} | all-to-all | bytes 917504 | tf_op jit(solution)/shard_map/all_to_all | solution.py:36
  21.0 3.8 %collective-permute-start.1 = (bf16[256,896]{1,0:T(8,128)(2,1)S(1)}, bf16[256,896]{1,0:T(8,128)(2,1)S(1)}, u32[]{:S(2)}, u32[]{:S(2)}) collective-permute-start(bf16[256,896]{1,0:T(8,128)(2,1)S(1)} %bitcast.10), channel_id=1, source_target_pairs={{32,0},{64,32},{96,64},{0,96},{33,1},{65,33},{97,65},{1,97},{34,2}... | collective-permute-start | bytes 1376264 | tf_op jit(solution)/shard_map/ppermute | solution.py:26
  24.7 0.0 collective-permute-start.3
  24.7 1.3 collective-permute-start.5
  26.0 2.6 %collective-permute-start = (bf16[256,896]{1,0:T(8,128)(2,1)S(1)}, bf16[256,896]{1,0:T(8,128)(2,1)S(1)}, u32[]{:S(2)}, u32[]{:S(2)}) collective-permute-start(bf16[256,896]{1,0:T(8,128)(2,1)S(1)} %bitcast.13), channel_id=1, source_target_pairs={{16,0},{0,16},{17,1},{1,17},{18,2},{2,18},{19,3},{3,19},{20,4},{4,... | collective-permute-start | bytes 1376264 | tf_op jit(solution)/shard_map/ppermute | solution.py:26
  28.7 5.8 %collective-permute-done.1.own_ref = bf16[256,896]{1,0:T(8,128)(2,1)S(1)} collective-permute-done((bf16[256,896]{1,0:T(8,128)(2,1)S(1)}, bf16[256,896]{1,0:T(8,128)(2,1)S(1)}, u32[]{:S(2)}, u32[]{:S(2)}) %collective-permute-start.1) | collective-permute-done | bytes 458784 | tf_op jit(solution)/shard_map/ppermute | solution.py:26
  34.5 10.8 %collective-permute-start.2 = (bf16[256,896]{1,0:T(8,128)(2,1)S(1)}, bf16[256,896]{1,0:T(8,128)(2,1)S(1)}, u32[]{:S(2)}, u32[]{:S(2)}) collective-permute-start(bf16[256,896]{1,0:T(8,128)(2,1)S(1)} %collective-permute-done.1.own_ref), channel_id=1, source_target_pairs={{16,0},{0,16},{17,1},{1,17},{18,2},{2,18},{19,3},{3,19},{20,4},{4,... | collective-permute-start | bytes 1376264 | tf_op jit(solution)/shard_map/ppermute | solution.py:26
  45.3 0.0 collective-permute-done.3.own_ref
  45.3 3.4 %collective-permute-start.4 = (bf16[256,896]{1,0:T(8,128)(2,1)S(1)}, bf16[256,896]{1,0:T(8,128)(2,1)S(1)}, u32[]{:S(2)}, u32[]{:S(2)}) collective-permute-start(bf16[256,896]{1,0:T(8,128)(2,1)S(1)} %collective-permute-done.3.own_ref), channel_id=1, source_target_pairs={{16,0},{0,16},{17,1},{1,17},{18,2},{2,18},{19,3},{3,19},{20,4},{4,... | collective-permute-start | bytes 1376264 | tf_op jit(solution)/shard_map/ppermute | solution.py:26
  48.7 0.0 collective-permute-done.5.own_ref
  48.7 0.0 collective-permute-start.6
  48.7 0.0 collective-permute-done.other_ref
  48.7 0.0 copy-start
  48.7 2.8 %copy-done = bf16[8,512,768]{2,1,0:T(8,128)(2,1)S(1)} copy-done((bf16[8,512,768]{2,1,0:T(8,128)(2,1)S(1)}, bf16[8,512,768]{2,1,0:T(8,128)(2,1)}, u32[]{:S(2)}) %copy-start) | copy-done | bytes 6291480
  51.5 1.3 copy-done.2
  52.8 8.2 %scores.4 = (bf16[512,4096]{1,0:T(8,128)(2,1)S(1)}, f32[8,512]{1,0:T(8,128)S(1)}, f32[2,512]{1,0:T(2,128)S(1)}, f32[1,512]{1,0:T(1,128)S(1)}, bf16[768,512]{1,0:T(8,128)(2,1)S(1)}) custom-call(s32[132]{0:T(256)S(1)} %concatenate.19.place, bf16[256,896]{1,0:T(8,128)(2,1)S(1)} %bitcast.14, bf16[256,896]{1,0:T(8,128)(2,1)S(1)} %collective-permute-done.other_ref, ...), custom_call_target="tpu_custom_call" | custom-call | flops 3825205248 | bytes 4194304 | tf_op jit(solution)/shard_map/scores/pallas_call | solution.py:299
  61.0 2.0 copy-done.4
  63.0 0.0 collective-permute-done.2.other_ref
  63.0 8.4 %scores.5 = (bf16[512,4096]{1,0:T(8,128)(2,1)S(1)}, f32[8,512]{1,0:T(8,128)S(1)}, f32[2,512]{1,0:T(2,128)S(1)}, f32[1,512]{1,0:T(1,128)S(1)}, bf16[768,512]{1,0:T(8,128)(2,1)S(1)}) custom-call(s32[132]{0:T(256)S(1)} %concatenate.19.place, bf16[256,896]{1,0:T(8,128)(2,1)S(1)} %collective-permute-done.1.own_ref, ...), custom_call_target="tpu_custom_call" | custom-call | flops 3825205248 | bytes 4194304 | tf_op jit(solution)/shard_map/scores/pallas_call | solution.py:299
  71.4 0.0 collective-permute-done.4.other_ref
  71.4 8.4 %scores.6 = (bf16[512,4096]{1,0:T(8,128)(2,1)S(1)}, f32[8,512]{1,0:T(8,128)S(1)}, f32[2,512]{1,0:T(2,128)S(1)}, f32[1,512]{1,0:T(1,128)S(1)}, bf16[768,512]{1,0:T(8,128)(2,1)S(1)}) custom-call(s32[132]{0:T(256)S(1)} %concatenate.19.place, bf16[256,896]{1,0:T(8,128)(2,1)S(1)} %collective-permute-done.3.own_ref, ...), custom_call_target="tpu_custom_call" | custom-call | flops 3825205248 | bytes 4194304 | tf_op jit(solution)/shard_map/scores/pallas_call | solution.py:299
  79.8 0.0 collective-permute-done.6.other_ref
  79.8 8.4 %scores.7 = (bf16[512,4096]{1,0:T(8,128)(2,1)S(1)}, f32[8,512]{1,0:T(8,128)S(1)}, f32[2,512]{1,0:T(2,128)S(1)}, f32[1,512]{1,0:T(1,128)S(1)}, bf16[768,512]{1,0:T(8,128)(2,1)S(1)}) custom-call(s32[132]{0:T(256)S(1)} %concatenate.19.place, bf16[256,896]{1,0:T(8,128)(2,1)S(1)} %collective-permute-done.5.own_ref, ...), custom_call_target="tpu_custom_call" | custom-call | flops 3825205248 | bytes 4194304 | tf_op jit(solution)/shard_map/scores/pallas_call | solution.py:299
  88.3 0.8 collective-permute-start.7
  89.1 2.2 %copy-done.5 = bf16[512,4096]{1,0:T(8,128)(2,1)S(1)} copy-done((bf16[512,4096]{1,0:T(8,128)(2,1)S(1)}, bf16[512,4096]{1,0:T(8,128)(2,1)}, u32[]{:S(2)}) %copy-start.5) | copy-done | bytes 4194328
  91.3 5.8 %backs.4 = (f32[2048,768]{1,0:T(8,128)S(1)}, bf16[2048,768]{1,0:T(8,128)(2,1)S(1)}) custom-call(f32[2,512]{1,0:T(2,128)S(1)} %get-tuple-element.36.stats_ref, f32[1,512]{1,0:T(1,128)S(1)} %get-tuple-element.49.code_ref, f32[8,512]{1,0:T(8,128)S(1)} %get-tuple-element.50.tops_ref, bf16[512,4096]{1,0:T(8,128)(2,1)S(1)} %copy-done.5, ...), custom_call_target="tpu_custom_call" | custom-call | flops 3221225472 | bytes 4194304 | tf_op jit(solution)/shard_map/backs/pallas_call | solution.py:306
  97.0 0.0 collective-permute-done.7
  97.1 0.2 collective-permute-start.10
  97.3 2.5 %collective-permute-start.8 = (f32[2,2048]{1,0:T(2,128)S(1)}, f32[2,2048]{1,0:T(2,128)S(1)}, u32[]{:S(2)}, u32[]{:S(2)}) collective-permute-start(f32[2,2048]{1,0:T(2,128)S(1)} %pad_maximum_fusion.1), channel_id=1, source_target_pairs={{1,0},{2,1},{3,2},{0,3},{5,4},{6,5},{7,6},{4,7},{9,8},{10,9},{11,1... | collective-permute-start | bytes 49160 | tf_op jit(solution)/shard_map/ppermute | solution.py:26
  99.9 0.0 collective-permute-start.9
  99.9 5.9 %backs.5 = (f32[2048,768]{1,0:T(8,128)S(1)}, bf16[2048,768]{1,0:T(8,128)(2,1)S(1)}) custom-call(f32[2,512]{1,0:T(2,128)S(1)} %get-tuple-element.37.stats_ref, f32[1,512]{1,0:T(1,128)S(1)} %get-tuple-element.46.code_ref, f32[8,512]{1,0:T(8,128)S(1)} %get-tuple-element.47.tops_ref, ...), custom_call_target="tpu_custom_call", output_to_operand_aliasing={{0}: (5, {}), {1}: (6, {})} | custom-call | flops 3221225472 | bytes 4194304 | tf_op jit(solution)/shard_map/backs/pallas_call | solution.py:306
  105.8 0.0 collective-permute-done.10
  105.8 0.0 collective-permute-done.8
  105.8 0.1 fusion.7
  105.9 0.1 collective-permute-start.11
  106.0 0.8 collective-permute-start.12
  106.8 0.8 collective-permute-start.13
  107.6 6.4 %backs.6 = (f32[2048,768]{1,0:T(8,128)S(1)}, bf16[2048,768]{1,0:T(8,128)(2,1)S(1)}) custom-call(f32[2,512]{1,0:T(2,128)S(1)} %get-tuple-element.38.stats_ref, f32[1,512]{1,0:T(1,128)S(1)} %get-tuple-element.43.code_ref, f32[8,512]{1,0:T(8,128)S(1)} %get-tuple-element.44.tops_ref, ...), custom_call_target="tpu_custom_call", output_to_operand_aliasing={{0}: (5, {}), {1}: (6, {})} | custom-call | flops 3221225472 | bytes 4194304 | tf_op jit(solution)/shard_map/backs/pallas_call | solution.py:306
  113.9 0.0 collective-permute-done.11
  114.0 0.1 fusion.4
  114.1 2.2 %collective-permute-start.14 = (f32[2,2048]{1,0:T(2,128)S(1)}, f32[2,2048]{1,0:T(2,128)S(1)}, u32[]{:S(2)}, u32[]{:S(2)}) collective-permute-start(f32[2,2048]{1,0:T(2,128)S(1)} %pad_maximum_fusion.3), channel_id=1, source_target_pairs={{32,0},{64,32},{96,64},{0,96},{33,1},{65,33},{97,65},{1,97},{34,2}... | collective-permute-start | bytes 49160 | tf_op jit(solution)/shard_map/ppermute | solution.py:26
  116.3 5.9 %backs.7 = (f32[2048,768]{1,0:T(8,128)S(1)}, bf16[2048,768]{1,0:T(8,128)(2,1)S(1)}) custom-call(f32[2,512]{1,0:T(2,128)S(1)} %get-tuple-element.39.stats_ref, f32[1,512]{1,0:T(1,128)S(1)} %get-tuple-element.40.code_ref, f32[8,512]{1,0:T(8,128)S(1)} %get-tuple-element.41.tops_ref, ...), custom_call_target="tpu_custom_call", output_to_operand_aliasing={{0}: (5, {}), {1}: (6, {})} | custom-call | flops 3221225472 | bytes 4194304 | tf_op jit(solution)/shard_map/backs/pallas_call | solution.py:306
  122.2 0.1 collective-permute-start.15
  122.3 1.4 collective-permute-start.16
  123.6 0.0 collective-permute-done.14
  123.7 2.7 %collective-permute-done.15 = f32[2,2048]{1,0:T(2,128)S(1)} collective-permute-done((f32[2,2048]{1,0:T(2,128)S(1)}, f32[2,2048]{1,0:T(2,128)S(1)}, u32[]{:S(2)}, u32[]{:S(2)}) %collective-permute-start.15) | collective-permute-done | bytes 16416 | tf_op jit(solution)/shard_map/ppermute | solution.py:26
  126.4 0.0 collective-permute-done.16
  126.4 0.1 fusion.1
  126.5 2.2 %scaled.1 = (bf16[1024,768]{1,0:T(8,128)(2,1)S(1)}, bf16[1024,768]{1,0:T(8,128)(2,1)S(1)}) custom-call(s32[132]{0:T(256)S(1)} %concatenate.19.place, f32[2,2048]{1,0:T(2,128)S(1)} %constant_dynamic-update-slice_fusion.local_ref, f32[2,2048]{1,0:T(2,128)S(1)} %pad_maximum_fusion.7.whole_ref, f32[2048,768]{1,0:T(8,128)S(1)} %get-tuple-element.58.out_ref, ...), custom_call_target="tpu_custom_call" | custom-call | tf_op jit(solution)/shard_map/scaled/pallas_call | solution.py:340
  128.7 2.5 %collective-permute-start.17 = (bf16[1024,768]{1,0:T(8,128)(2,1)S(1)}, bf16[1024,768]{1,0:T(8,128)(2,1)S(1)}, u32[]{:S(2)}, u32[]{:S(2)}) collective-permute-start(bf16[1024,768]{1,0:T(8,128)(2,1)S(1)} %get-tuple-element.61), channel_id=1, source_target_pairs={{16,0},{0,16},{17,1},{1,17},{18,2},{2,18},{19,3},{3,19},{20,4},{4,... | collective-permute-start | bytes 4718600 | tf_op jit(solution)/shard_map/ppermute | solution.py:26
  131.2 3.0 %collective-permute-done.17 = bf16[1024,768]{1,0:T(8,128)(2,1)S(1)} collective-permute-done((bf16[1024,768]{1,0:T(8,128)(2,1)S(1)}, bf16[1024,768]{1,0:T(8,128)(2,1)S(1)}, u32[]{:S(2)}, u32[]{:S(2)}) %collective-permute-start.17) | collective-permute-done | bytes 1572896 | tf_op jit(solution)/shard_map/ppermute | solution.py:26
  134.2 0.4 add_convert_fusion
  134.7 30.2 %all_to_all.26 = bf16[64,16,768]{2,1,0:T(8,128)(2,1)S(1)} all-to-all(bf16[64,16,768]{2,1,0:T(8,128)(2,1)S(1)} %bitcast.15), channel_id=1, replica_groups=mesh['z'=4,'core'=2,'y'=4,'x'=4] {'z','y','x'}, dimensions={0} | all-to-all | bytes 3145728 | tf_op jit(solution)/shard_map/all_to_all | solution.py:360
  164.9 0.2 convert_reduce_fusion
  165.1 0.1 broadcast_in_dim.58
  165.3 28.8 %all_to_all.27 = bf16[64,16,768]{2,1,0:T(8,128)(2,1)S(1)} all-to-all(bf16[64,16,768]{2,1,0:T(8,128)(2,1)S(1)} %broadcast_in_dim.58), channel_id=1, replica_groups=mesh['z'=4,'core'=2,'y'=4,'x'=4] {'z','y','x'}, dimensions={0} | all-to-all | bytes 3145728 | tf_op jit(solution)/shard_map/all_to_all | solution.py:36
  194.0 2.5 %collective-permute-start.18 = (bf16[1024,768]{1,0:T(8,128)(2,1)S(1)}, bf16[1024,768]{1,0:T(8,128)(2,1)S(1)}, u32[]{:S(2)}, u32[]{:S(2)}) collective-permute-start(bf16[1024,768]{1,0:T(8,128)(2,1)S(1)} %bitcast.8), channel_id=1, source_target_pairs={{16,0},{0,16},{17,1},{1,17},{18,2},{2,18},{19,3},{3,19},{20,4},{4,... | collective-permute-start | bytes 4718600 | tf_op jit(solution)/shard_map/ppermute | solution.py:26
  196.5 1.1 fusion
  197.6 2.0 collective-permute-done.18.b_other
  199.5 5.0 %adapter.1 = f32[768,768]{1,0:T(8,128)} custom-call(s32[132]{0:T(256)S(1)} %concatenate.19.place, bf16[768,512]{1,0:T(8,128)(2,1)S(1)} %get-tuple-element.62.q0, bf16[768,512]{1,0:T(8,128)(2,1)S(1)} %get-tuple-element.63.q1, bf16[768,512]{1,0:T(8,128)(2,1)S(1)} %get-tuple-element.64.q2, bf16[768,512]{1,0:T(8,128)(2,1)S(1)} %get-tuple-element.65.q3, ...), custom_call_target="tpu_custom_call" | custom-call | flops 2415919104 | bytes 6291456 | tf_op jit(solution)/shard_map/adapter/pallas_call | solution.py:371
  (30 shorter events, 0.3 us)
Async XLA Ops:
  21.0 13.5 %collective-permute-start.1 = (bf16[256,896]{1,0:T(8,128)(2,1)S(1)}, bf16[256,896]{1,0:T(8,128)(2,1)S(1)}, u32[]{:S(2)}, u32[]{:S(2)}) collective-permute-start(bf16[256,896]{1,0:T(8,128)(2,1)S(1)} %bitcast.10), channel_id=1, source_target_pairs={{32,0},{64,32},{96,64},{0,96},{33,1},{65,33},{97,65},{1,97},{34,2}... | collective-permute-start | bytes 1376264 | tf_op jit(solution)/shard_map/ppermute | solution.py:26
  24.7 20.6 %collective-permute-start.3 = (bf16[256,896]{1,0:T(8,128)(2,1)S(1)}, bf16[256,896]{1,0:T(8,128)(2,1)S(1)}, u32[]{:S(2)}, u32[]{:S(2)}) collective-permute-start(bf16[256,896]{1,0:T(8,128)(2,1)S(1)} %bitcast.11), channel_id=1, source_target_pairs={{96,0},{0,32},{32,64},{64,96},{97,1},{1,33},{33,65},{65,97},{98,2}... | collective-permute-start | bytes 1376264 | tf_op jit(solution)/shard_map/ppermute | solution.py:26
  24.7 24.0 %collective-permute-start.5 = (bf16[256,896]{1,0:T(8,128)(2,1)S(1)}, bf16[256,896]{1,0:T(8,128)(2,1)S(1)}, u32[]{:S(2)}, u32[]{:S(2)}) collective-permute-start(bf16[256,896]{1,0:T(8,128)(2,1)S(1)} %bitcast.12), channel_id=1, source_target_pairs={{64,0},{96,32},{0,64},{32,96},{65,1},{97,33},{1,65},{33,97},{66,2}... | collective-permute-start | bytes 1376264 | tf_op jit(solution)/shard_map/ppermute | solution.py:26
  26.0 22.7 %collective-permute-start = (bf16[256,896]{1,0:T(8,128)(2,1)S(1)}, bf16[256,896]{1,0:T(8,128)(2,1)S(1)}, u32[]{:S(2)}, u32[]{:S(2)}) collective-permute-start(bf16[256,896]{1,0:T(8,128)(2,1)S(1)} %bitcast.13), channel_id=1, source_target_pairs={{16,0},{0,16},{17,1},{1,17},{18,2},{2,18},{19,3},{3,19},{20,4},{4,... | collective-permute-start | bytes 1376264 | tf_op jit(solution)/shard_map/ppermute | solution.py:26
  34.5 28.5 %collective-permute-start.2 = (bf16[256,896]{1,0:T(8,128)(2,1)S(1)}, bf16[256,896]{1,0:T(8,128)(2,1)S(1)}, u32[]{:S(2)}, u32[]{:S(2)}) collective-permute-start(bf16[256,896]{1,0:T(8,128)(2,1)S(1)} %collective-permute-done.1.own_ref), channel_id=1, source_target_pairs={{16,0},{0,16},{17,1},{1,17},{18,2},{2,18},{19,3},{3,19},{20,4},{4,... | collective-permute-start | bytes 1376264 | tf_op jit(solution)/shard_map/ppermute | solution.py:26
  45.3 26.1 %collective-permute-start.4 = (bf16[256,896]{1,0:T(8,128)(2,1)S(1)}, bf16[256,896]{1,0:T(8,128)(2,1)S(1)}, u32[]{:S(2)}, u32[]{:S(2)}) collective-permute-start(bf16[256,896]{1,0:T(8,128)(2,1)S(1)} %collective-permute-done.3.own_ref), channel_id=1, source_target_pairs={{16,0},{0,16},{17,1},{1,17},{18,2},{2,18},{19,3},{3,19},{20,4},{4,... | collective-permute-start | bytes 1376264 | tf_op jit(solution)/shard_map/ppermute | solution.py:26
  48.7 31.1 %collective-permute-start.6 = (bf16[256,896]{1,0:T(8,128)(2,1)S(1)}, bf16[256,896]{1,0:T(8,128)(2,1)S(1)}, u32[]{:S(2)}, u32[]{:S(2)}) collective-permute-start(bf16[256,896]{1,0:T(8,128)(2,1)S(1)} %collective-permute-done.5.own_ref), channel_id=1, source_target_pairs={{16,0},{0,16},{17,1},{1,17},{18,2},{2,18},{19,3},{3,19},{20,4},{4,... | collective-permute-start | bytes 1376264 | tf_op jit(solution)/shard_map/ppermute | solution.py:26
  48.7 2.8 %copy-start = (bf16[8,512,768]{2,1,0:T(8,128)(2,1)S(1)}, bf16[8,512,768]{2,1,0:T(8,128)(2,1)}, u32[]{:S(2)}) copy-start(bf16[8,512,768]{2,1,0:T(8,128)(2,1)} %rows_ref.15) | copy-start | bytes 18874372
  51.5 1.3 copy-start.2
  52.8 10.2 %copy-start.1 = (bf16[8,512,768]{2,1,0:T(8,128)(2,1)S(1)}, bf16[8,512,768]{2,1,0:T(8,128)(2,1)}, u32[]{:S(2)}) copy-start(bf16[8,512,768]{2,1,0:T(8,128)(2,1)} %rows_ref.15) | copy-start | bytes 18874372
  61.0 2.0 copy-start.4
  88.3 8.8 %collective-permute-start.7 = (f32[2,2048]{1,0:T(2,128)S(1)}, f32[2,2048]{1,0:T(2,128)S(1)}, u32[]{:S(2)}, u32[]{:S(2)}) collective-permute-start(f32[2,2048]{1,0:T(2,128)S(1)} %constant_dynamic-update-slice_fusion.local_ref), channel_id=1, source_target_pairs={{16,0},{0,16},{17,1},{1,17},{18,2},{2,18},{19,3},{3,19},{20,4},{4,... | collective-permute-start | bytes 49160 | tf_op jit(solution)/shard_map/ppermute | solution.py:26
  89.1 2.2 %copy-start.5 = (bf16[512,4096]{1,0:T(8,128)(2,1)S(1)}, bf16[512,4096]{1,0:T(8,128)(2,1)}, u32[]{:S(2)}) copy-start(bf16[512,4096]{1,0:T(8,128)(2,1)} %copy-done.4) | copy-start | bytes 12582916
  97.1 8.7 %collective-permute-start.10 = (f32[2,2048]{1,0:T(2,128)S(1)}, f32[2,2048]{1,0:T(2,128)S(1)}, u32[]{:S(2)}, u32[]{:S(2)}) collective-permute-start(f32[2,2048]{1,0:T(2,128)S(1)} %pad_maximum_fusion.1), channel_id=1, source_target_pairs={{3,0},{0,1},{1,2},{2,3},{7,4},{4,5},{5,6},{6,7},{11,8},{8,9},{9,10... | collective-permute-start | bytes 49160 | tf_op jit(solution)/shard_map/ppermute | solution.py:26
  97.3 8.5 %collective-permute-start.8 = (f32[2,2048]{1,0:T(2,128)S(1)}, f32[2,2048]{1,0:T(2,128)S(1)}, u32[]{:S(2)}, u32[]{:S(2)}) collective-permute-start(f32[2,2048]{1,0:T(2,128)S(1)} %pad_maximum_fusion.1), channel_id=1, source_target_pairs={{1,0},{2,1},{3,2},{0,3},{5,4},{6,5},{7,6},{4,7},{9,8},{10,9},{11,1... | collective-permute-start | bytes 49160 | tf_op jit(solution)/shard_map/ppermute | solution.py:26
  99.9 5.9 %collective-permute-start.9 = (f32[2,2048]{1,0:T(2,128)S(1)}, f32[2,2048]{1,0:T(2,128)S(1)}, u32[]{:S(2)}, u32[]{:S(2)}) collective-permute-start(f32[2,2048]{1,0:T(2,128)S(1)} %pad_maximum_fusion.1), channel_id=1, source_target_pairs={{2,0},{3,1},{0,2},{1,3},{6,4},{7,5},{4,6},{5,7},{10,8},{11,9},{8,1... | collective-permute-start | bytes 49160 | tf_op jit(solution)/shard_map/ppermute | solution.py:26
  105.9 8.0 %collective-permute-start.11 = (f32[2,2048]{1,0:T(2,128)S(1)}, f32[2,2048]{1,0:T(2,128)S(1)}, u32[]{:S(2)}, u32[]{:S(2)}) collective-permute-start(f32[2,2048]{1,0:T(2,128)S(1)} %pad_maximum_fusion.2), channel_id=1, source_target_pairs={{4,0},{8,4},{12,8},{0,12},{5,1},{9,5},{13,9},{1,13},{6,2},{10,6},{... | collective-permute-start | bytes 49160 | tf_op jit(solution)/shard_map/ppermute | solution.py:26
  106.0 7.9 %collective-permute-start.12 = (f32[2,2048]{1,0:T(2,128)S(1)}, f32[2,2048]{1,0:T(2,128)S(1)}, u32[]{:S(2)}, u32[]{:S(2)}) collective-permute-start(f32[2,2048]{1,0:T(2,128)S(1)} %pad_maximum_fusion.2), channel_id=1, source_target_pairs={{8,0},{12,4},{0,8},{4,12},{9,1},{13,5},{1,9},{5,13},{10,2},{14,6},... | collective-permute-start | bytes 49160 | tf_op jit(solution)/shard_map/ppermute | solution.py:26
  106.8 7.2 %collective-permute-start.13 = (f32[2,2048]{1,0:T(2,128)S(1)}, f32[2,2048]{1,0:T(2,128)S(1)}, u32[]{:S(2)}, u32[]{:S(2)}) collective-permute-start(f32[2,2048]{1,0:T(2,128)S(1)} %pad_maximum_fusion.2), channel_id=1, source_target_pairs={{12,0},{0,4},{4,8},{8,12},{13,1},{1,5},{5,9},{9,13},{14,2},{2,6},{... | collective-permute-start | bytes 49160 | tf_op jit(solution)/shard_map/ppermute | solution.py:26
  114.1 9.6 %collective-permute-start.14 = (f32[2,2048]{1,0:T(2,128)S(1)}, f32[2,2048]{1,0:T(2,128)S(1)}, u32[]{:S(2)}, u32[]{:S(2)}) collective-permute-start(f32[2,2048]{1,0:T(2,128)S(1)} %pad_maximum_fusion.3), channel_id=1, source_target_pairs={{32,0},{64,32},{96,64},{0,96},{33,1},{65,33},{97,65},{1,97},{34,2}... | collective-permute-start | bytes 49160 | tf_op jit(solution)/shard_map/ppermute | solution.py:26
  122.2 4.2 %collective-permute-start.15 = (f32[2,2048]{1,0:T(2,128)S(1)}, f32[2,2048]{1,0:T(2,128)S(1)}, u32[]{:S(2)}, u32[]{:S(2)}) collective-permute-start(f32[2,2048]{1,0:T(2,128)S(1)} %pad_maximum_fusion.3), channel_id=1, source_target_pairs={{64,0},{96,32},{0,64},{32,96},{65,1},{97,33},{1,65},{33,97},{66,2}... | collective-permute-start | bytes 49160 | tf_op jit(solution)/shard_map/ppermute | solution.py:26
  122.3 4.1 %collective-permute-start.16 = (f32[2,2048]{1,0:T(2,128)S(1)}, f32[2,2048]{1,0:T(2,128)S(1)}, u32[]{:S(2)}, u32[]{:S(2)}) collective-permute-start(f32[2,2048]{1,0:T(2,128)S(1)} %pad_maximum_fusion.3), channel_id=1, source_target_pairs={{96,0},{0,32},{32,64},{64,96},{97,1},{1,33},{33,65},{65,97},{98,2}... | collective-permute-start | bytes 49160 | tf_op jit(solution)/shard_map/ppermute | solution.py:26
  128.7 5.5 %collective-permute-start.17 = (bf16[1024,768]{1,0:T(8,128)(2,1)S(1)}, bf16[1024,768]{1,0:T(8,128)(2,1)S(1)}, u32[]{:S(2)}, u32[]{:S(2)}) collective-permute-start(bf16[1024,768]{1,0:T(8,128)(2,1)S(1)} %get-tuple-element.61), channel_id=1, source_target_pairs={{16,0},{0,16},{17,1},{1,17},{18,2},{2,18},{19,3},{3,19},{20,4},{4,... | collective-permute-start | bytes 4718600 | tf_op jit(solution)/shard_map/ppermute | solution.py:26
  164.9 31.6 %copy-start.3 = (bf16[768,768]{1,0:T(8,128)(2,1)S(1)}, bf16[768,768]{1,0:T(8,128)(2,1)}, u32[]{:S(2)}) copy-start(bf16[768,768]{1,0:T(8,128)(2,1)} %w_ref.7) | copy-start | bytes 3538948
  194.0 5.5 %collective-permute-start.18 = (bf16[1024,768]{1,0:T(8,128)(2,1)S(1)}, bf16[1024,768]{1,0:T(8,128)(2,1)S(1)}, u32[]{:S(2)}, u32[]{:S(2)}) collective-permute-start(bf16[1024,768]{1,0:T(8,128)(2,1)S(1)} %bitcast.8), channel_id=1, source_target_pairs={{16,0},{0,16},{17,1},{1,17},{18,2},{2,18},{19,3},{3,19},{20,4},{4,... | collective-permute-start | bytes 4718600 | tf_op jit(solution)/shard_map/ppermute | solution.py:26

commit v2 on v1

--- a/solution.py
+++ b/solution.py
@@ -101,7 +101,6 @@
 
     lane = lax.broadcasted_iota(jnp.int32, (tile, LANES), 1)
     blocks = per // LANES
-    rows_at = pl.ds(pl.multiple_of(core * tile, tile), tile)
 
     def matmul(j):
         raw = lax.dot_general(
@@ -122,7 +121,7 @@
             weight = jnp.exp2(s_ref[j % 2, :, b * LANES : (b + 1) * LANES] * factor - peak)
             total = weight if total is None else total + weight
             at = j * per + b * LANES
-            p_ref[rows_at, at : at + LANES] = weight.astype(jnp.bfloat16)
+            p_ref[:, at : at + LANES] = weight.astype(jnp.bfloat16)
         return peak, lanes_of(jnp.sum(total, axis=1, keepdims=True), tile)
 
     tops = jnp.full((tile, LANES), NEG_FILL, jnp.float32)
@@ -146,14 +145,13 @@
     out_ref, target_ref, g_ref, row_ref = refs[-4:]
     lists, per, width = rows_ref.shape
     tile = tops_ref.shape[1]
-    rows_at = pl.ds(pl.multiple_of(pl.program_id(0) * tile, tile), tile)
     share = columns_of(jnp.exp2(tops_ref[...] - stats_ref[0:1, :]), tile)
     acc = None
     for j in range(lists):
         part = lanes_of(share[:, j : j + 1], tile)
         for b in range(per // LANES):
             at = j * per + b * LANES
-            g_ref[:, at : at + LANES] = (p_ref[rows_at, at : at + LANES].astype(jnp.float32) * part).astype(jnp.bfloat16)
+            g_ref[:, at : at + LANES] = (p_ref[:, at : at + LANES].astype(jnp.float32) * part).astype(jnp.bfloat16)
         out = jnp.dot(g_ref[:, j * per : (j + 1) * per], rows_ref[j], preferred_element_type=jnp.float32)
         acc = out if acc is None else acc + out
     out_ref[...] = acc
@@ -253,10 +251,14 @@
     count = steps * tile
     keys = lists_here * rows_here
     owns = [plane]
-    for ahead in ORDER[1:]:
+    for ahead in (1, 3):
         owns.append(from_ahead(plane, "z", ahead))
     weights, tops, stats, codes, gathered = [], [], [], [], []
-    for ahead, own in zip(ORDER, owns):
+    for i, ahead in enumerate(ORDER):
+        if i == 1:
+            held, codes[0] = lax.optimization_barrier((plane, codes[0]))
+            owns.append(from_ahead(held, "z", 2))
+        own = owns[i]
         other = from_ahead(own, "core", 1)
         call = pl.pallas_call(
             functools.partial(score_kernel, table),
@@ -270,7 +272,7 @@
                     WHOLE,
                 ],
                 out_specs=[
-                    WHOLE,
+                    pl.BlockSpec((half, keys), lambda i, *_: (i, 0)),
                     pl.BlockSpec((lists_here, half), lambda i, *_: (0, i)),
                     pl.BlockSpec((2, half), lambda i, *_: (0, i)),
                     pl.BlockSpec((1, half), lambda i, *_: (0, i)),
@@ -290,7 +292,7 @@
                 jax.ShapeDtypeStruct((1, tile), jnp.float32),
                 jax.ShapeDtypeStruct((width, tile), jnp.bfloat16),
             ],
-            compiler_params=pltpu.CompilerParams(vmem_limit_bytes=16 << 20),
+            compiler_params=pltpu.CompilerParams(vmem_limit_bytes=12 << 20),
             cost_estimate=pl.CostEstimate(
                 flops=2 * tile * width * (keys + width), bytes_accessed=tile * keys * 2, transcendentals=tile * keys
             ),
@@ -310,7 +312,7 @@
                 pl.BlockSpec((2, half), lambda k: (0, k)),
                 pl.BlockSpec((1, half), lambda k: (0, k)),
                 pl.BlockSpec((lists_here, half), lambda k: (0, k)),
-                WHOLE,
+                pl.BlockSpec((half, keys), lambda k: (k, 0)),
                 WHOLE,
             ]
             + [pl.BlockSpec(memory_space=pl.ANY)] * len(rest),

time: 205 us -> 194 us (0.946)
  starting transfers between devices: 35.7 us -> 23.3 us
  waiting for transfers between devices: 13.6 us -> 18.8 us
  local copies, waits for them, and re-layouts: 9.14 us -> 4.99 us
    ppermute x19, starting transfers between devices: 35.7 us -> 23.3 us  [from_ahead(): lax.ppermute(value, axis, [((i + step) % size, i) for i in range(size)])]
    ppermute x19, waiting for transfers between devices: 13.6 us -> 18.8 us  [from_ahead(): lax.ppermute(value, axis, [((i + step) % size, i) for i in range(size)])]
    unnamed x15 -> x11, local copies, waits for them, and re-layouts: 8.24 us -> 4.08 us
  transfers between devices with their start and end apart: 19 -> 19, of which waited for: 4 -> 4; matrix products, arithmetic and copies ran while one was open for 1% -> 1% of each run, Pallas kernels for 24% -> 25%
where the time goes in v2:
time: 194 us
  blocking collectives  76.6 us (39%)
  Pallas kernels  64.6 us (33%)
  starting transfers between devices  23.3 us (12%)
  waiting for transfers between devices  18.8 us (10%)
  local copies, waits for them, and re-layouts  4.99 us (3%)
  other arithmetic  3.27 us (2%)
    all_to_all x2, blocking collectives, spread_axes(): return lax.all_to_all(spread, axes, split_axis=0, concat_axis=0, tiled=True)  46.1 us
    pallas_call x4, Pallas kernels, all_steps(): outs = call(place, own, other, adapter_w, index_rows)  33.4 us
    all_to_all x1, blocking collectives, all_steps(): lax.all_to_all(merged, CHIPS, split_axis=0, concat_axis=0, tiled=True)  30.5 us
    pallas_call x4, Pallas kernels, all_steps(): pl.pallas_call(back_kernel, grid=(2,), in_specs=[pl.BlockSpec((2, half),...  23.9 us
    ppermute x19, starting transfers between devices, from_ahead(): lax.ppermute(value, axis, [((i + step) % size, i) for i in range(size)])  23.3 us
    ppermute x19, waiting for transfers between devices, from_ahead(): lax.ppermute(value, axis, [((i + step) % size, i) for i in range(size)])  18.8 us
    pallas_call x1, Pallas kernels, all_steps(): pl.pallas_call(adapter_kernel, grid_spec=pltpu.PrefetchScalarGridSpec(num...  5.01 us
    unnamed x11, local copies, waits for them, and re-layouts  4.08 us
  transfers between devices with their start and end apart: 19, of which 4 were waited for; matrix products, arithmetic and copies ran while one was open for 1% of the time, Pallas kernels for 25%

profile of v2, /device:TPU:1, one launch (start us, length us, event | category | flops | bytes accessed | tf_op | source)
XLA Modules:
  0.0 193.6 jit_solution(15651100202580170243)
XLA Ops:
  0.7 0.7 compare_select_fusion.1
  1.4 0.8 select_convert_fusion
  2.1 0.7 pad_maximum_fusion
  2.9 0.7 concatenate.19.place
  3.7 17.3 %all_to_all.25 = bf16[16,16,896]{2,1,0:T(8,128)(2,1)S(1)} all-to-all(bf16[16,16,896]{2,1,0:T(8,128)(2,1)S(1)} %broadcast_in_dim.57), channel_id=1, replica_groups=mesh['z'=4,'core'=2,'y'=4,'x'=4] {'y','x'}, dimensions={0} | all-to-all | bytes 917504 | tf_op jit(solution)/shard_map/all_to_all | solution.py:36
  21.0 1.8 collective-permute-start
  22.8 3.8 %collective-permute-start.1 = (bf16[256,896]{1,0:T(8,128)(2,1)S(1)}, bf16[256,896]{1,0:T(8,128)(2,1)S(1)}, u32[]{:S(2)}, u32[]{:S(2)}) collective-permute-start(bf16[256,896]{1,0:T(8,128)(2,1)S(1)} %bitcast.11), channel_id=1, source_target_pairs={{32,0},{64,32},{96,64},{0,96},{33,1},{65,33},{97,65},{1,97},{34,2}... | collective-permute-start | bytes 1376264 | tf_op jit(solution)/shard_map/ppermute | solution.py:26
  26.5 0.0 collective-permute-start.3
  26.5 0.0 collective-permute-done.other_ref
  26.5 2.8 %copy-done = bf16[8,512,768]{2,1,0:T(8,128)(2,1)S(1)} copy-done((bf16[8,512,768]{2,1,0:T(8,128)(2,1)S(1)}, bf16[8,512,768]{2,1,0:T(8,128)(2,1)}, u32[]{:S(2)}) %copy-start) | copy-done | bytes 6291480
  29.3 1.3 copy-done.2
  30.6 8.2 %scores.4 = (bf16[512,4096]{1,0:T(8,128)(2,1)S(1)}, f32[8,512]{1,0:T(8,128)S(1)}, f32[2,512]{1,0:T(2,128)S(1)}, f32[1,512]{1,0:T(1,128)S(1)}, bf16[768,512]{1,0:T(8,128)(2,1)S(1)}) custom-call(s32[132]{0:T(256)S(1)} %concatenate.19.place, bf16[256,896]{1,0:T(8,128)(2,1)S(1)} %bitcast.13, bf16[256,896]{1,0:T(8,128)(2,1)S(1)} %collective-permute-done.other_ref, ...), custom_call_target="tpu_custom_call" | custom-call | flops 3825205248 | bytes 4194304 | tf_op jit(solution)/shard_map/scores/pallas_call | solution.py:301
  38.8 1.4 collective-permute-start.5
  40.2 0.0 collective-permute-done.1.own_ref
  40.2 0.8 collective-permute-start.2
  41.0 0.0 collective-permute-done.3.own_ref
  41.0 0.1 collective-permute-start.4
  41.1 11.1 %collective-permute-done.5.own_ref = bf16[256,896]{1,0:T(8,128)(2,1)S(1)} collective-permute-done((bf16[256,896]{1,0:T(8,128)(2,1)S(1)}, bf16[256,896]{1,0:T(8,128)(2,1)S(1)}, u32[]{:S(2)}, u32[]{:S(2)}) %collective-permute-start.5) | collective-permute-done | bytes 458784 | tf_op jit(solution)/shard_map/ppermute | solution.py:26
  52.2 1.1 collective-permute-start.6
  53.3 0.0 collective-permute-done.2.other_ref
  53.3 8.4 %scores.5 = (bf16[512,4096]{1,0:T(8,128)(2,1)S(1)}, f32[8,512]{1,0:T(8,128)S(1)}, f32[2,512]{1,0:T(2,128)S(1)}, f32[1,512]{1,0:T(1,128)S(1)}, bf16[768,512]{1,0:T(8,128)(2,1)S(1)}) custom-call(s32[132]{0:T(256)S(1)} %concatenate.19.place, bf16[256,896]{1,0:T(8,128)(2,1)S(1)} %collective-permute-done.1.own_ref, ...), custom_call_target="tpu_custom_call" | custom-call | flops 3825205248 | bytes 4194304 | tf_op jit(solution)/shard_map/scores/pallas_call | solution.py:301
  61.8 0.0 collective-permute-done.4.other_ref
  61.8 8.4 %scores.6 = (bf16[512,4096]{1,0:T(8,128)(2,1)S(1)}, f32[8,512]{1,0:T(8,128)S(1)}, f32[2,512]{1,0:T(2,128)S(1)}, f32[1,512]{1,0:T(1,128)S(1)}, bf16[768,512]{1,0:T(8,128)(2,1)S(1)}) custom-call(s32[132]{0:T(256)S(1)} %concatenate.19.place, bf16[256,896]{1,0:T(8,128)(2,1)S(1)} %collective-permute-done.3.own_ref, ...), custom_call_target="tpu_custom_call" | custom-call | flops 3825205248 | bytes 4194304 | tf_op jit(solution)/shard_map/scores/pallas_call | solution.py:301
  70.2 0.0 collective-permute-done.6.other_ref
  70.2 8.4 %scores.7 = (bf16[512,4096]{1,0:T(8,128)(2,1)S(1)}, f32[8,512]{1,0:T(8,128)S(1)}, f32[2,512]{1,0:T(2,128)S(1)}, f32[1,512]{1,0:T(1,128)S(1)}, bf16[768,512]{1,0:T(8,128)(2,1)S(1)}) custom-call(s32[132]{0:T(256)S(1)} %concatenate.19.place, bf16[256,896]{1,0:T(8,128)(2,1)S(1)} %collective-permute-done.5.own_ref, ...), custom_call_target="tpu_custom_call" | custom-call | flops 3825205248 | bytes 4194304 | tf_op jit(solution)/shard_map/scores/pallas_call | solution.py:301
  78.7 0.1 collective-permute-start.7
  78.7 5.8 %backs.4 = (f32[2048,768]{1,0:T(8,128)S(1)}, bf16[2048,768]{1,0:T(8,128)(2,1)S(1)}) custom-call(f32[2,512]{1,0:T(2,128)S(1)} %get-tuple-element.38.stats_ref, f32[1,512]{1,0:T(1,128)S(1)} %get-tuple-element.53.code_ref, f32[8,512]{1,0:T(8,128)S(1)} %get-tuple-element.54.tops_ref, bf16[512,4096]{1,0:T(8,128)(2,1)S(1)} %get-tuple-element.55.p_ref, ...), custom_call_target="tpu_custom_call" | custom-call | flops 3221225472 | bytes 4194304 | tf_op jit(solution)/shard_map/backs/pallas_call | solution.py:308
  84.5 0.0 collective-permute-done.7
  84.6 0.2 collective-permute-start.10
  84.8 2.5 %collective-permute-start.8 = (f32[2,2048]{1,0:T(2,128)S(1)}, f32[2,2048]{1,0:T(2,128)S(1)}, u32[]{:S(2)}, u32[]{:S(2)}) collective-permute-start(f32[2,2048]{1,0:T(2,128)S(1)} %pad_maximum_fusion.1), channel_id=1, source_target_pairs={{1,0},{2,1},{3,2},{0,3},{5,4},{6,5},{7,6},{4,7},{9,8},{10,9},{11,1... | collective-permute-start | bytes 49160 | tf_op jit(solution)/shard_map/ppermute | solution.py:26
  87.4 0.0 collective-permute-start.9
  87.4 5.9 %backs.5 = (f32[2048,768]{1,0:T(8,128)S(1)}, bf16[2048,768]{1,0:T(8,128)(2,1)S(1)}) custom-call(f32[2,512]{1,0:T(2,128)S(1)} %get-tuple-element.39.stats_ref, f32[1,512]{1,0:T(1,128)S(1)} %get-tuple-element.50.code_ref, f32[8,512]{1,0:T(8,128)S(1)} %get-tuple-element.51.tops_ref, ...), custom_call_target="tpu_custom_call", output_to_operand_aliasing={{0}: (5, {}), {1}: (6, {})} | custom-call | flops 3221225472 | bytes 4194304 | tf_op jit(solution)/shard_map/backs/pallas_call | solution.py:308
  93.3 0.0 collective-permute-done.10
  93.3 0.0 collective-permute-done.8
  93.3 0.0 collective-permute-done.9
  93.3 0.1 fusion.7
  93.4 0.1 collective-permute-start.11
  93.5 0.7 collective-permute-start.12
  94.2 0.8 collective-permute-start.13
  95.0 6.4 %backs.6 = (f32[2048,768]{1,0:T(8,128)S(1)}, bf16[2048,768]{1,0:T(8,128)(2,1)S(1)}) custom-call(f32[2,512]{1,0:T(2,128)S(1)} %get-tuple-element.40.stats_ref, f32[1,512]{1,0:T(1,128)S(1)} %get-tuple-element.47.code_ref, f32[8,512]{1,0:T(8,128)S(1)} %get-tuple-element.48.tops_ref, ...), custom_call_target="tpu_custom_call", output_to_operand_aliasing={{0}: (5, {}), {1}: (6, {})} | custom-call | flops 3221225472 | bytes 4194304 | tf_op jit(solution)/shard_map/backs/pallas_call | solution.py:308
  101.3 0.0 collective-permute-done.11
  101.3 0.0 collective-permute-done.12
  101.3 0.0 collective-permute-done.13
  101.3 0.1 fusion.4
  101.5 4.7 %collective-permute-start.14 = (f32[2,2048]{1,0:T(2,128)S(1)}, f32[2,2048]{1,0:T(2,128)S(1)}, u32[]{:S(2)}, u32[]{:S(2)}) collective-permute-start(f32[2,2048]{1,0:T(2,128)S(1)} %pad_maximum_fusion.3), channel_id=1, source_target_pairs={{32,0},{64,32},{96,64},{0,96},{33,1},{65,33},{97,65},{1,97},{34,2}... | collective-permute-start | bytes 49160 | tf_op jit(solution)/shard_map/ppermute | solution.py:26
  106.2 5.9 %backs.7 = (f32[2048,768]{1,0:T(8,128)S(1)}, bf16[2048,768]{1,0:T(8,128)(2,1)S(1)}) custom-call(f32[2,512]{1,0:T(2,128)S(1)} %get-tuple-element.43.stats_ref, f32[1,512]{1,0:T(1,128)S(1)} %get-tuple-element.44.code_ref, f32[8,512]{1,0:T(8,128)S(1)} %get-tuple-element.45.tops_ref, ...), custom_call_target="tpu_custom_call", output_to_operand_aliasing={{0}: (5, {}), {1}: (6, {})} | custom-call | flops 3221225472 | bytes 4194304 | tf_op jit(solution)/shard_map/backs/pallas_call | solution.py:308
  112.1 0.1 collective-permute-start.15
  112.2 1.4 collective-permute-start.16
  113.5 0.0 collective-permute-done.14
  113.6 2.7 %collective-permute-done.15 = f32[2,2048]{1,0:T(2,128)S(1)} collective-permute-done((f32[2,2048]{1,0:T(2,128)S(1)}, f32[2,2048]{1,0:T(2,128)S(1)}, u32[]{:S(2)}, u32[]{:S(2)}) %collective-permute-start.15) | collective-permute-done | bytes 16416 | tf_op jit(solution)/shard_map/ppermute | solution.py:26
  116.3 0.0 collective-permute-done.16
  116.3 0.1 fusion.1
  116.4 2.2 %scaled.1 = (bf16[1024,768]{1,0:T(8,128)(2,1)S(1)}, bf16[1024,768]{1,0:T(8,128)(2,1)S(1)}) custom-call(s32[132]{0:T(256)S(1)} %concatenate.19.place, f32[2,2048]{1,0:T(2,128)S(1)} %constant_dynamic-update-slice_fusion.local_ref, f32[2,2048]{1,0:T(2,128)S(1)} %pad_maximum_fusion.7.whole_ref, f32[2048,768]{1,0:T(8,128)S(1)} %get-tuple-element.62.out_ref, ...), custom_call_target="tpu_custom_call" | custom-call | tf_op jit(solution)/shard_map/scaled/pallas_call | solution.py:342
  118.6 1.3 collective-permute-start.17
  119.9 3.0 %collective-permute-done.17 = bf16[1024,768]{1,0:T(8,128)(2,1)S(1)} collective-permute-done((bf16[1024,768]{1,0:T(8,128)(2,1)S(1)}, bf16[1024,768]{1,0:T(8,128)(2,1)S(1)}, u32[]{:S(2)}, u32[]{:S(2)}) %collective-permute-start.17) | collective-permute-done | bytes 1572896 | tf_op jit(solution)/shard_map/ppermute | solution.py:26
  123.0 0.4 add_convert_fusion
  123.4 30.5 %all_to_all.26 = bf16[64,16,768]{2,1,0:T(8,128)(2,1)S(1)} all-to-all(bf16[64,16,768]{2,1,0:T(8,128)(2,1)S(1)} %bitcast.15), channel_id=1, replica_groups=mesh['z'=4,'core'=2,'y'=4,'x'=4] {'z','y','x'}, dimensions={0} | all-to-all | bytes 3145728 | tf_op jit(solution)/shard_map/all_to_all | solution.py:362
  153.9 0.2 convert_reduce_fusion
  154.2 0.1 broadcast_in_dim.58
  154.3 28.8 %all_to_all.27 = bf16[64,16,768]{2,1,0:T(8,128)(2,1)S(1)} all-to-all(bf16[64,16,768]{2,1,0:T(8,128)(2,1)S(1)} %broadcast_in_dim.58), channel_id=1, replica_groups=mesh['z'=4,'core'=2,'y'=4,'x'=4] {'z','y','x'}, dimensions={0} | all-to-all | bytes 3145728 | tf_op jit(solution)/shard_map/all_to_all | solution.py:36
  183.0 2.5 %collective-permute-start.18 = (bf16[1024,768]{1,0:T(8,128)(2,1)S(1)}, bf16[1024,768]{1,0:T(8,128)(2,1)S(1)}, u32[]{:S(2)}, u32[]{:S(2)}) collective-permute-start(bf16[1024,768]{1,0:T(8,128)(2,1)S(1)} %bitcast.8), channel_id=1, source_target_pairs={{16,0},{0,16},{17,1},{1,17},{18,2},{2,18},{19,3},{3,19},{20,4},{4,... | collective-permute-start | bytes 4718600 | tf_op jit(solution)/shard_map/ppermute | solution.py:26
  185.5 1.1 fusion
  186.6 2.0 %collective-permute-done.18.b_other = bf16[1024,768]{1,0:T(8,128)(2,1)S(1)} collective-permute-done((bf16[1024,768]{1,0:T(8,128)(2,1)S(1)}, bf16[1024,768]{1,0:T(8,128)(2,1)S(1)}, u32[]{:S(2)}, u32[]{:S(2)}) %collective-permute-start.18) | collective-permute-done | bytes 1572896 | tf_op jit(solution)/shard_map/ppermute | solution.py:26
  188.6 5.0 %adapter.1 = f32[768,768]{1,0:T(8,128)} custom-call(s32[132]{0:T(256)S(1)} %concatenate.19.place, bf16[768,512]{1,0:T(8,128)(2,1)S(1)} %get-tuple-element.66.q0, bf16[768,512]{1,0:T(8,128)(2,1)S(1)} %get-tuple-element.67.q1, bf16[768,512]{1,0:T(8,128)(2,1)S(1)} %get-tuple-element.68.q2, bf16[768,512]{1,0:T(8,128)(2,1)S(1)} %get-tuple-element.69.q3, ...), custom_call_target="tpu_custom_call" | custom-call | flops 2415919104 | bytes 6291456 | tf_op jit(solution)/shard_map/adapter/pallas_call | solution.py:373
  (26 shorter events, 0.3 us)
Async XLA Ops:
  21.0 5.6 %collective-permute-start = (bf16[256,896]{1,0:T(8,128)(2,1)S(1)}, bf16[256,896]{1,0:T(8,128)(2,1)S(1)}, u32[]{:S(2)}, u32[]{:S(2)}) collective-permute-start(bf16[256,896]{1,0:T(8,128)(2,1)S(1)} %bitcast.10), channel_id=1, source_target_pairs={{16,0},{0,16},{17,1},{1,17},{18,2},{2,18},{19,3},{3,19},{20,4},{4,... | collective-permute-start | bytes 1376264 | tf_op jit(solution)/shard_map/ppermute | solution.py:26
  22.8 17.4 %collective-permute-start.1 = (bf16[256,896]{1,0:T(8,128)(2,1)S(1)}, bf16[256,896]{1,0:T(8,128)(2,1)S(1)}, u32[]{:S(2)}, u32[]{:S(2)}) collective-permute-start(bf16[256,896]{1,0:T(8,128)(2,1)S(1)} %bitcast.11), channel_id=1, source_target_pairs={{32,0},{64,32},{96,64},{0,96},{33,1},{65,33},{97,65},{1,97},{34,2}... | collective-permute-start | bytes 1376264 | tf_op jit(solution)/shard_map/ppermute | solution.py:26
  26.5 14.5 %collective-permute-start.3 = (bf16[256,896]{1,0:T(8,128)(2,1)S(1)}, bf16[256,896]{1,0:T(8,128)(2,1)S(1)}, u32[]{:S(2)}, u32[]{:S(2)}) collective-permute-start(bf16[256,896]{1,0:T(8,128)(2,1)S(1)} %bitcast.12), channel_id=1, source_target_pairs={{96,0},{0,32},{32,64},{64,96},{97,1},{1,33},{33,65},{65,97},{98,2}... | collective-permute-start | bytes 1376264 | tf_op jit(solution)/shard_map/ppermute | solution.py:26
  26.5 2.8 %copy-start = (bf16[8,512,768]{2,1,0:T(8,128)(2,1)S(1)}, bf16[8,512,768]{2,1,0:T(8,128)(2,1)}, u32[]{:S(2)}) copy-start(bf16[8,512,768]{2,1,0:T(8,128)(2,1)} %rows_ref.15) | copy-start | bytes 18874372
  29.3 1.3 copy-start.2
  30.6 22.7 %copy-start.1 = (bf16[8,512,768]{2,1,0:T(8,128)(2,1)S(1)}, bf16[8,512,768]{2,1,0:T(8,128)(2,1)}, u32[]{:S(2)}) copy-start(bf16[8,512,768]{2,1,0:T(8,128)(2,1)} %rows_ref.15) | copy-start | bytes 18874372
  38.8 13.4 %collective-permute-start.5 = (bf16[256,896]{1,0:T(8,128)(2,1)S(1)}, bf16[256,896]{1,0:T(8,128)(2,1)S(1)}, u32[]{:S(2)}, u32[]{:S(2)}) collective-permute-start(bf16[256,896]{1,0:T(8,128)(2,1)S(1)} %bitcast.14), channel_id=1, source_target_pairs={{64,0},{96,32},{0,64},{32,96},{65,1},{97,33},{1,65},{33,97},{66,2}... | collective-permute-start | bytes 1376264 | tf_op jit(solution)/shard_map/ppermute | solution.py:26
  40.2 13.1 %collective-permute-start.2 = (bf16[256,896]{1,0:T(8,128)(2,1)S(1)}, bf16[256,896]{1,0:T(8,128)(2,1)S(1)}, u32[]{:S(2)}, u32[]{:S(2)}) collective-permute-start(bf16[256,896]{1,0:T(8,128)(2,1)S(1)} %collective-permute-done.1.own_ref), channel_id=1, source_target_pairs={{16,0},{0,16},{17,1},{1,17},{18,2},{2,18},{19,3},{3,19},{20,4},{4,... | collective-permute-start | bytes 1376264 | tf_op jit(solution)/shard_map/ppermute | solution.py:26
  41.0 20.7 %collective-permute-start.4 = (bf16[256,896]{1,0:T(8,128)(2,1)S(1)}, bf16[256,896]{1,0:T(8,128)(2,1)S(1)}, u32[]{:S(2)}, u32[]{:S(2)}) collective-permute-start(bf16[256,896]{1,0:T(8,128)(2,1)S(1)} %collective-permute-done.3.own_ref), channel_id=1, source_target_pairs={{16,0},{0,16},{17,1},{1,17},{18,2},{2,18},{19,3},{3,19},{20,4},{4,... | collective-permute-start | bytes 1376264 | tf_op jit(solution)/shard_map/ppermute | solution.py:26
  52.2 18.0 %collective-permute-start.6 = (bf16[256,896]{1,0:T(8,128)(2,1)S(1)}, bf16[256,896]{1,0:T(8,128)(2,1)S(1)}, u32[]{:S(2)}, u32[]{:S(2)}) collective-permute-start(bf16[256,896]{1,0:T(8,128)(2,1)S(1)} %collective-permute-done.5.own_ref), channel_id=1, source_target_pairs={{16,0},{0,16},{17,1},{1,17},{18,2},{2,18},{19,3},{3,19},{20,4},{4,... | collective-permute-start | bytes 1376264 | tf_op jit(solution)/shard_map/ppermute | solution.py:26
  78.7 5.9 %collective-permute-start.7 = (f32[2,2048]{1,0:T(2,128)S(1)}, f32[2,2048]{1,0:T(2,128)S(1)}, u32[]{:S(2)}, u32[]{:S(2)}) collective-permute-start(f32[2,2048]{1,0:T(2,128)S(1)} %constant_dynamic-update-slice_fusion.local_ref), channel_id=1, source_target_pairs={{16,0},{0,16},{17,1},{1,17},{18,2},{2,18},{19,3},{3,19},{20,4},{4,... | collective-permute-start | bytes 49160 | tf_op jit(solution)/shard_map/ppermute | solution.py:26
  84.6 8.7 %collective-permute-start.10 = (f32[2,2048]{1,0:T(2,128)S(1)}, f32[2,2048]{1,0:T(2,128)S(1)}, u32[]{:S(2)}, u32[]{:S(2)}) collective-permute-start(f32[2,2048]{1,0:T(2,128)S(1)} %pad_maximum_fusion.1), channel_id=1, source_target_pairs={{3,0},{0,1},{1,2},{2,3},{7,4},{4,5},{5,6},{6,7},{11,8},{8,9},{9,10... | collective-permute-start | bytes 49160 | tf_op jit(solution)/shard_map/ppermute | solution.py:26
  84.8 8.5 %collective-permute-start.8 = (f32[2,2048]{1,0:T(2,128)S(1)}, f32[2,2048]{1,0:T(2,128)S(1)}, u32[]{:S(2)}, u32[]{:S(2)}) collective-permute-start(f32[2,2048]{1,0:T(2,128)S(1)} %pad_maximum_fusion.1), channel_id=1, source_target_pairs={{1,0},{2,1},{3,2},{0,3},{5,4},{6,5},{7,6},{4,7},{9,8},{10,9},{11,1... | collective-permute-start | bytes 49160 | tf_op jit(solution)/shard_map/ppermute | solution.py:26
  87.4 5.9 %collective-permute-start.9 = (f32[2,2048]{1,0:T(2,128)S(1)}, f32[2,2048]{1,0:T(2,128)S(1)}, u32[]{:S(2)}, u32[]{:S(2)}) collective-permute-start(f32[2,2048]{1,0:T(2,128)S(1)} %pad_maximum_fusion.1), channel_id=1, source_target_pairs={{2,0},{3,1},{0,2},{1,3},{6,4},{7,5},{4,6},{5,7},{10,8},{11,9},{8,1... | collective-permute-start | bytes 49160 | tf_op jit(solution)/shard_map/ppermute | solution.py:26
  93.4 7.9 %collective-permute-start.11 = (f32[2,2048]{1,0:T(2,128)S(1)}, f32[2,2048]{1,0:T(2,128)S(1)}, u32[]{:S(2)}, u32[]{:S(2)}) collective-permute-start(f32[2,2048]{1,0:T(2,128)S(1)} %pad_maximum_fusion.2), channel_id=1, source_target_pairs={{4,0},{8,4},{12,8},{0,12},{5,1},{9,5},{13,9},{1,13},{6,2},{10,6},{... | collective-permute-start | bytes 49160 | tf_op jit(solution)/shard_map/ppermute | solution.py:26
  93.5 7.8 %collective-permute-start.12 = (f32[2,2048]{1,0:T(2,128)S(1)}, f32[2,2048]{1,0:T(2,128)S(1)}, u32[]{:S(2)}, u32[]{:S(2)}) collective-permute-start(f32[2,2048]{1,0:T(2,128)S(1)} %pad_maximum_fusion.2), channel_id=1, source_target_pairs={{8,0},{12,4},{0,8},{4,12},{9,1},{13,5},{1,9},{5,13},{10,2},{14,6},... | collective-permute-start | bytes 49160 | tf_op jit(solution)/shard_map/ppermute | solution.py:26
  94.2 7.2 %collective-permute-start.13 = (f32[2,2048]{1,0:T(2,128)S(1)}, f32[2,2048]{1,0:T(2,128)S(1)}, u32[]{:S(2)}, u32[]{:S(2)}) collective-permute-start(f32[2,2048]{1,0:T(2,128)S(1)} %pad_maximum_fusion.2), channel_id=1, source_target_pairs={{12,0},{0,4},{4,8},{8,12},{13,1},{1,5},{5,9},{9,13},{14,2},{2,6},{... | collective-permute-start | bytes 49160 | tf_op jit(solution)/shard_map/ppermute | solution.py:26
  101.5 12.1 %collective-permute-start.14 = (f32[2,2048]{1,0:T(2,128)S(1)}, f32[2,2048]{1,0:T(2,128)S(1)}, u32[]{:S(2)}, u32[]{:S(2)}) collective-permute-start(f32[2,2048]{1,0:T(2,128)S(1)} %pad_maximum_fusion.3), channel_id=1, source_target_pairs={{32,0},{64,32},{96,64},{0,96},{33,1},{65,33},{97,65},{1,97},{34,2}... | collective-permute-start | bytes 49160 | tf_op jit(solution)/shard_map/ppermute | solution.py:26
  112.1 4.2 %collective-permute-start.15 = (f32[2,2048]{1,0:T(2,128)S(1)}, f32[2,2048]{1,0:T(2,128)S(1)}, u32[]{:S(2)}, u32[]{:S(2)}) collective-permute-start(f32[2,2048]{1,0:T(2,128)S(1)} %pad_maximum_fusion.3), channel_id=1, source_target_pairs={{64,0},{96,32},{0,64},{32,96},{65,1},{97,33},{1,65},{33,97},{66,2}... | collective-permute-start | bytes 49160 | tf_op jit(solution)/shard_map/ppermute | solution.py:26
  112.2 4.1 %collective-permute-start.16 = (f32[2,2048]{1,0:T(2,128)S(1)}, f32[2,2048]{1,0:T(2,128)S(1)}, u32[]{:S(2)}, u32[]{:S(2)}) collective-permute-start(f32[2,2048]{1,0:T(2,128)S(1)} %pad_maximum_fusion.3), channel_id=1, source_target_pairs={{96,0},{0,32},{32,64},{64,96},{97,1},{1,33},{33,65},{65,97},{98,2}... | collective-permute-start | bytes 49160 | tf_op jit(solution)/shard_map/ppermute | solution.py:26
  118.6 4.3 %collective-permute-start.17 = (bf16[1024,768]{1,0:T(8,128)(2,1)S(1)}, bf16[1024,768]{1,0:T(8,128)(2,1)S(1)}, u32[]{:S(2)}, u32[]{:S(2)}) collective-permute-start(bf16[1024,768]{1,0:T(8,128)(2,1)S(1)} %get-tuple-element.65), channel_id=1, source_target_pairs={{16,0},{0,16},{17,1},{1,17},{18,2},{2,18},{19,3},{3,19},{20,4},{4,... | collective-permute-start | bytes 4718600 | tf_op jit(solution)/shard_map/ppermute | solution.py:26
  153.9 31.6 %copy-start.3 = (bf16[768,768]{1,0:T(8,128)(2,1)S(1)}, bf16[768,768]{1,0:T(8,128)(2,1)}, u32[]{:S(2)}) copy-start(bf16[768,768]{1,0:T(8,128)(2,1)} %w_ref.7) | copy-start | bytes 3538948
  183.0 5.5 %collective-permute-start.18 = (bf16[1024,768]{1,0:T(8,128)(2,1)S(1)}, bf16[1024,768]{1,0:T(8,128)(2,1)S(1)}, u32[]{:S(2)}, u32[]{:S(2)}) collective-permute-start(bf16[1024,768]{1,0:T(8,128)(2,1)S(1)} %bitcast.8), channel_id=1, source_target_pairs={{16,0},{0,16},{17,1},{1,17},{18,2},{2,18},{19,3},{3,19},{20,4},{4,... | collective-permute-start | bytes 4718600 | tf_op jit(solution)/shard_map/ppermute | solution.py:26

commit v3 on v2

--- a/solution.py
+++ b/solution.py
@@ -54,12 +54,12 @@
     factor = LOG2E / math.sqrt(width)
     core = pl.program_id(0)
 
-    def find(n, _):
-        at = place[4 + n] - place[2]
-        here_ref[jnp.where((at >= 0) & (at < lists), at, lists)] = n
-        return 0
-
-    lax.fori_loop(0, table, find, 0)
+    @pl.when(core == 0)
+    def _():
+        for n in range(table):
+            at = place[4 + n] - place[2]
+            here_ref[jnp.where((at >= 0) & (at < lists), at, lists)] = n
+
     here = [here_ref[j] for j in range(lists)]
     total_rows = [ROWS * place[4 + table + n] for n in here]
     live = [n - place[3] for n in total_rows]
@@ -176,36 +176,28 @@
     target_ref[...] = row_ref[...].astype(jnp.bfloat16)
 
 
-def scale_kernel(place, local_ref, whole_ref, out_ref, target_ref, mine_ref, theirs_ref, r_ref):
+def scale_kernel(place, local_ref, whole_ref, out_ref, target_ref, scaled_ref):
     tile, width = out_ref.shape
-    half = tile // 2
     share = jnp.exp2(local_ref[0:1, :] - whole_ref[0:1, :]) / whole_ref[1:2, :]
     share = jnp.broadcast_to(share, (LANES, tile)).T
     for b in range(width // LANES):
         at = slice(b * LANES, (b + 1) * LANES)
-        r_ref[:, at] = (
+        scaled_ref[:, at] = (
             (out_ref[:, at] * share - target_ref[:, at].astype(jnp.float32)) * (1.0 / math.sqrt(width))
         ).astype(jnp.bfloat16)
-    mine_ref[...] = r_ref[pl.ds(pl.multiple_of(place[1] * half, half), half), :]
-    theirs_ref[...] = r_ref[pl.ds(pl.multiple_of((1 - place[1]) * half, half), half), :]
-
-
-def adapter_kernel(place, q0, q1, q2, q3, b_own, b_other, out_ref, q_ref, b_ref):
-    tile = q0.shape[1]
-    half = tile // 2
-    count = 4 * tile
-
-    @pl.when(pl.program_id(0) == 0)
-    def _():
-        for i in range(4):
-            for source, core in ((b_own, place[1]), (b_other, 1 - place[1])):
-                to = pl.multiple_of(i * tile + core * half, half)
-                b_ref[pl.ds(to, half), :] = source[i * half : (i + 1) * half, :]
-
+
+
+def adapter_kernel(other, place, q0, q1, q2, q3, b_ref, *refs):
+    out_ref, q_ref = refs[-2:]
+    half = b_ref.shape[0] // 4
+    core = 1 - place[1] if other else place[1]
     for ahead, q in zip(ORDER, (q0, q1, q2, q3)):
-        to = pl.multiple_of(lax.rem(place[0] + ahead, 4) * tile, tile)
-        q_ref[:, pl.ds(to, tile)] = q[...]
-    out_ref[...] = jnp.dot(q_ref[...], b_ref[...], preferred_element_type=jnp.float32) * (1.0 / math.sqrt(count))
+        to = pl.multiple_of(lax.rem(place[0] + ahead, 4) * half, half)
+        q_ref[:, pl.ds(to, half)] = q[:, pl.ds(pl.multiple_of(core * half, half), half)]
+    total = jnp.dot(q_ref[...], b_ref[...], preferred_element_type=jnp.float32)
+    if other:
+        total = (total + refs[0][...]) * (1.0 / math.sqrt(8 * half))
+    out_ref[...] = total
 
 
 def merge_axis(stats, axis):
@@ -338,26 +330,36 @@
     for axis in ("core", "x", "y", "z"):
         whole_stats = merge_axis(whole_stats, axis)
 
-    placed = pl.BlockSpec((half, width), lambda i, place: (lax.rem(place[0] + chunk_of(i), 4), 0))
-    mine, theirs = pl.pallas_call(
-        scale_kernel,
-        grid_spec=pltpu.PrefetchScalarGridSpec(
-            num_scalar_prefetch=1,
-            grid=(steps,),
-            in_specs=[
-                pl.BlockSpec((2, tile), lambda i, place: (0, i)),
-                pl.BlockSpec((2, tile), lambda i, place: (0, i)),
-                pl.BlockSpec((tile, width), lambda i, place: (i, 0)),
-                pl.BlockSpec((tile, width), lambda i, place: (i, 0)),
-            ],
-            out_specs=[placed, placed],
-            scratch_shapes=[pltpu.VMEM((tile, width), jnp.bfloat16)],
-        ),
-        out_shape=[jax.ShapeDtypeStruct((count // 2, width), jnp.bfloat16)] * 2,
-        compiler_params=pltpu.CompilerParams(vmem_limit_bytes=24 << 20),
-        name="scaled",
-    )(place, local_stats, whole_stats, out_all, target_all)
+    def scaled(other):
+        def part(i, place):
+            return 2 * i + (1 - place[1] if other else place[1])
+
+        return pl.pallas_call(
+            scale_kernel,
+            grid_spec=pltpu.PrefetchScalarGridSpec(
+                num_scalar_prefetch=1,
+                grid=(steps,),
+                in_specs=[
+                    pl.BlockSpec((2, half), lambda i, place: (0, part(i, place))),
+                    pl.BlockSpec((2, half), lambda i, place: (0, part(i, place))),
+                    pl.BlockSpec((half, width), lambda i, place: (part(i, place), 0)),
+                    pl.BlockSpec((half, width), lambda i, place: (part(i, place), 0)),
+                ],
+                out_specs=pl.BlockSpec(
+                    (half, width), lambda i, place: (lax.rem(place[0] + chunk_of(i), 4), 0)
+                ),
+            ),
+            out_shape=jax.ShapeDtypeStruct((count // 2, width), jnp.bfloat16),
+            compiler_params=pltpu.CompilerParams(vmem_limit_bytes=12 << 20),
+            cost_estimate=pl.CostEstimate(
+                flops=2 * count * width, bytes_accessed=count * width * 4, transcendentals=0
+            ),
+            name="scaled",
+        )(place, local_stats, whole_stats, out_all, target_all)
+
+    theirs = scaled(True)
     received = from_ahead(theirs, "core", 1)
+    mine = scaled(False)
     merged = (mine.astype(jnp.float32) + received.astype(jnp.float32)).astype(jnp.bfloat16)
     pieces = lax.all_to_all(merged, CHIPS, split_axis=0, concat_axis=0, tiled=True)
     back = jnp.sum(pieces.reshape(-1, queries.shape[0], width).astype(jnp.float32), axis=0)
@@ -370,25 +372,28 @@
     b_other = from_ahead(b_own, "core", 1)
     third = width // 3
     column = pl.BlockSpec((third, tile), lambda i, place: (i, 0))
-    adapter_grad = pl.pallas_call(
-        adapter_kernel,
-        grid_spec=pltpu.PrefetchScalarGridSpec(
-            num_scalar_prefetch=1,
-            grid=(3,),
-            in_specs=[column, column, column, column, WHOLE, WHOLE],
-            out_specs=pl.BlockSpec((third, width), lambda i, place: (i, 0)),
-            scratch_shapes=[
-                pltpu.VMEM((third, count), jnp.bfloat16),
-                pltpu.VMEM((count, width), jnp.bfloat16),
-            ],
-        ),
-        out_shape=jax.ShapeDtypeStruct((width, width), jnp.float32),
-        compiler_params=pltpu.CompilerParams(vmem_limit_bytes=24 << 20),
-        cost_estimate=pl.CostEstimate(
-            flops=2 * count * width * width, bytes_accessed=count * width * 4, transcendentals=0
-        ),
-        name="adapter",
-    )(place, *gathered, b_own, b_other)
+    block = pl.BlockSpec((third, width), lambda i, place: (i, 0))
+
+    def product(other, *rest):
+        return pl.pallas_call(
+            functools.partial(adapter_kernel, other),
+            grid_spec=pltpu.PrefetchScalarGridSpec(
+                num_scalar_prefetch=1,
+                grid=(3,),
+                in_specs=[column, column, column, column, WHOLE] + [block] * (len(rest) - 1),
+                out_specs=block,
+                scratch_shapes=[pltpu.VMEM((third, count // 2), jnp.bfloat16)],
+            ),
+            out_shape=jax.ShapeDtypeStruct((width, width), jnp.float32),
+            compiler_params=pltpu.CompilerParams(vmem_limit_bytes=16 << 20),
+            cost_estimate=pl.CostEstimate(
+                flops=count * width * width, bytes_accessed=count * width * 2, transcendentals=0
+            ),
+            name="adapter",
+        )(place, *gathered, *rest)
+
+    partial = product(False, b_own)
+    adapter_grad = product(True, b_other, partial)
     return (query_grad, adapter_grad)
 
 

time: 194 us -> 187 us (0.964)
  waiting for transfers between devices: 18.8 us -> 14.4 us
  Pallas kernels: 64.6 us -> 60.5 us
    pallas_call x4, Pallas kernels: 33.4 us -> 27.6 us  [all_steps(): outs = call(place, own, other, adapter_w, index_rows)]
    ppermute x19, waiting for transfers between devices: 18.8 us -> 14.4 us  [from_ahead(): lax.ppermute(value, axis, [((i + step) % size, i) for i in range(size)])]
    pallas_call x2 -> x4, Pallas kernels: 7.22 us -> 8.93 us  [the longest x2 6.03 us: product(): pl.pallas_call(functools.partial(adapter_kernel, other), grid_spec=pltpu....]
  transfers between devices with their start and end apart: 19 -> 19, of which waited for: 4 -> 3; matrix products, arithmetic and copies ran while one was open for 1% -> 1% of each run, Pallas kernels for 25% -> 26%
where the time goes in v3:
time: 187 us; the launch traced here: 186 us
  blocking collectives  76.7 us (41%)
  Pallas kernels  60.5 us (32%)
  starting transfers between devices  24.3 us (13%)
  waiting for transfers between devices  14.4 us (8%)
  local copies, waits for them, and re-layouts  4.99 us (3%)
  other arithmetic  3.33 us (2%)
    all_to_all x2, blocking collectives, spread_axes(): return lax.all_to_all(spread, axes, split_axis=0, concat_axis=0, tiled=True)  46.2 us
    all_to_all x1, blocking collectives, all_steps(): lax.all_to_all(merged, CHIPS, split_axis=0, concat_axis=0, tiled=True)  30.5 us
    pallas_call x4, Pallas kernels, all_steps(): outs = call(place, own, other, adapter_w, index_rows)  27.6 us
    ppermute x19, starting transfers between devices, from_ahead(): lax.ppermute(value, axis, [((i + step) % size, i) for i in range(size)])  24.3 us
    pallas_call x4, Pallas kernels, all_steps(): pl.pallas_call(back_kernel, grid=(2,), in_specs=[pl.BlockSpec((2, half),...  24 us
    ppermute x19, waiting for transfers between devices, from_ahead(): lax.ppermute(value, axis, [((i + step) % size, i) for i in range(size)])  14.4 us
    pallas_call x2, Pallas kernels, product(): pl.pallas_call(functools.partial(adapter_kernel, other), grid_spec=pltpu....  6.03 us
    unnamed x11, local copies, waits for them, and re-layouts  4.08 us
  transfers between devices with their start and end apart: 19, of which 3 were waited for; matrix products, arithmetic and copies ran while one was open for 1% of the time, Pallas kernels for 26%

profile of v3, /device:TPU:1, one launch (start us, length us, event | category | flops | bytes accessed | tf_op | source)
XLA Modules:
  0.0 186.3 jit_solution(7932094056532726895)
XLA Ops:
  0.7 0.7 compare_select_fusion.1
  1.4 0.8 select_convert_fusion
  2.1 0.7 pad_maximum_fusion
  2.9 0.7 concatenate.19.place
  3.7 17.3 %all_to_all.25 = bf16[16,16,896]{2,1,0:T(8,128)(2,1)S(1)} all-to-all(bf16[16,16,896]{2,1,0:T(8,128)(2,1)S(1)} %broadcast_in_dim.57), channel_id=1, replica_groups=mesh['z'=4,'core'=2,'y'=4,'x'=4] {'y','x'}, dimensions={0} | all-to-all | bytes 917504 | tf_op jit(solution)/shard_map/all_to_all | solution.py:36
  21.0 1.8 collective-permute-start
  22.8 3.8 %collective-permute-start.1 = (bf16[256,896]{1,0:T(8,128)(2,1)S(1)}, bf16[256,896]{1,0:T(8,128)(2,1)S(1)}, u32[]{:S(2)}, u32[]{:S(2)}) collective-permute-start(bf16[256,896]{1,0:T(8,128)(2,1)S(1)} %bitcast.11), channel_id=1, source_target_pairs={{32,0},{64,32},{96,64},{0,96},{33,1},{65,33},{97,65},{1,97},{34,2}... | collective-permute-start | bytes 1376264 | tf_op jit(solution)/shard_map/ppermute | solution.py:26
  26.5 0.0 collective-permute-start.3
  26.5 0.0 collective-permute-done.other_ref
  26.5 2.8 %copy-done = bf16[8,512,768]{2,1,0:T(8,128)(2,1)S(1)} copy-done((bf16[8,512,768]{2,1,0:T(8,128)(2,1)S(1)}, bf16[8,512,768]{2,1,0:T(8,128)(2,1)}, u32[]{:S(2)}) %copy-start) | copy-done | bytes 6291480
  29.3 1.3 copy-done.2
  30.6 6.7 %scores.4 = (bf16[512,4096]{1,0:T(8,128)(2,1)S(1)}, f32[8,512]{1,0:T(8,128)S(1)}, f32[2,512]{1,0:T(2,128)S(1)}, f32[1,512]{1,0:T(1,128)S(1)}, bf16[768,512]{1,0:T(8,128)(2,1)S(1)}) custom-call(s32[132]{0:T(256)S(1)} %concatenate.19.place, bf16[256,896]{1,0:T(8,128)(2,1)S(1)} %bitcast.13, bf16[256,896]{1,0:T(8,128)(2,1)S(1)} %collective-permute-done.other_ref, ...), custom_call_target="tpu_custom_call" | custom-call | flops 3825205248 | bytes 4194304 | tf_op jit(solution)/shard_map/scores/pallas_call | solution.py:293
  37.4 1.4 collective-permute-start.5
  38.7 0.0 collective-permute-done.1.own_ref
  38.8 0.8 collective-permute-start.2
  39.6 0.0 collective-permute-done.3.own_ref
  39.6 1.1 collective-permute-start.4
  40.7 10.0 %collective-permute-done.5.own_ref = bf16[256,896]{1,0:T(8,128)(2,1)S(1)} collective-permute-done((bf16[256,896]{1,0:T(8,128)(2,1)S(1)}, bf16[256,896]{1,0:T(8,128)(2,1)S(1)}, u32[]{:S(2)}, u32[]{:S(2)}) %collective-permute-start.5) | collective-permute-done | bytes 458784 | tf_op jit(solution)/shard_map/ppermute | solution.py:26
  50.7 1.1 collective-permute-start.6
  51.9 0.0 collective-permute-done.2.other_ref
  51.9 7.0 %scores.5 = (bf16[512,4096]{1,0:T(8,128)(2,1)S(1)}, f32[8,512]{1,0:T(8,128)S(1)}, f32[2,512]{1,0:T(2,128)S(1)}, f32[1,512]{1,0:T(1,128)S(1)}, bf16[768,512]{1,0:T(8,128)(2,1)S(1)}) custom-call(s32[132]{0:T(256)S(1)} %concatenate.19.place, bf16[256,896]{1,0:T(8,128)(2,1)S(1)} %collective-permute-done.1.own_ref, ...), custom_call_target="tpu_custom_call" | custom-call | flops 3825205248 | bytes 4194304 | tf_op jit(solution)/shard_map/scores/pallas_call | solution.py:293
  58.9 0.0 collective-permute-done.4.other_ref
  58.9 7.0 %scores.6 = (bf16[512,4096]{1,0:T(8,128)(2,1)S(1)}, f32[8,512]{1,0:T(8,128)S(1)}, f32[2,512]{1,0:T(2,128)S(1)}, f32[1,512]{1,0:T(1,128)S(1)}, bf16[768,512]{1,0:T(8,128)(2,1)S(1)}) custom-call(s32[132]{0:T(256)S(1)} %concatenate.19.place, bf16[256,896]{1,0:T(8,128)(2,1)S(1)} %collective-permute-done.3.own_ref, ...), custom_call_target="tpu_custom_call" | custom-call | flops 3825205248 | bytes 4194304 | tf_op jit(solution)/shard_map/scores/pallas_call | solution.py:293
  65.9 0.0 collective-permute-done.6.other_ref
  65.9 7.0 %scores.7 = (bf16[512,4096]{1,0:T(8,128)(2,1)S(1)}, f32[8,512]{1,0:T(8,128)S(1)}, f32[2,512]{1,0:T(2,128)S(1)}, f32[1,512]{1,0:T(1,128)S(1)}, bf16[768,512]{1,0:T(8,128)(2,1)S(1)}) custom-call(s32[132]{0:T(256)S(1)} %concatenate.19.place, bf16[256,896]{1,0:T(8,128)(2,1)S(1)} %collective-permute-done.5.own_ref, ...), custom_call_target="tpu_custom_call" | custom-call | flops 3825205248 | bytes 4194304 | tf_op jit(solution)/shard_map/scores/pallas_call | solution.py:293
  72.9 0.1 collective-permute-start.7
  73.0 5.8 %backs.4 = (f32[2048,768]{1,0:T(8,128)S(1)}, bf16[2048,768]{1,0:T(8,128)(2,1)S(1)}) custom-call(f32[2,512]{1,0:T(2,128)S(1)} %get-tuple-element.36.stats_ref, f32[1,512]{1,0:T(1,128)S(1)} %get-tuple-element.51.code_ref, f32[8,512]{1,0:T(8,128)S(1)} %get-tuple-element.52.tops_ref, bf16[512,4096]{1,0:T(8,128)(2,1)S(1)} %get-tuple-element.53.p_ref, ...), custom_call_target="tpu_custom_call" | custom-call | flops 3221225472 | bytes 4194304 | tf_op jit(solution)/shard_map/backs/pallas_call | solution.py:300
  78.8 0.0 collective-permute-done.7
  78.8 0.2 collective-permute-start.10
  79.1 2.5 %collective-permute-start.8 = (f32[2,2048]{1,0:T(2,128)S(1)}, f32[2,2048]{1,0:T(2,128)S(1)}, u32[]{:S(2)}, u32[]{:S(2)}) collective-permute-start(f32[2,2048]{1,0:T(2,128)S(1)} %pad_maximum_fusion.1), channel_id=1, source_target_pairs={{1,0},{2,1},{3,2},{0,3},{5,4},{6,5},{7,6},{4,7},{9,8},{10,9},{11,1... | collective-permute-start | bytes 49160 | tf_op jit(solution)/shard_map/ppermute | solution.py:26
  81.6 0.0 collective-permute-start.9
  81.6 5.9 %backs.5 = (f32[2048,768]{1,0:T(8,128)S(1)}, bf16[2048,768]{1,0:T(8,128)(2,1)S(1)}) custom-call(f32[2,512]{1,0:T(2,128)S(1)} %get-tuple-element.37.stats_ref, f32[1,512]{1,0:T(1,128)S(1)} %get-tuple-element.48.code_ref, f32[8,512]{1,0:T(8,128)S(1)} %get-tuple-element.49.tops_ref, ...), custom_call_target="tpu_custom_call", output_to_operand_aliasing={{0}: (5, {}), {1}: (6, {})} | custom-call | flops 3221225472 | bytes 4194304 | tf_op jit(solution)/shard_map/backs/pallas_call | solution.py:300
  87.5 0.0 collective-permute-done.10
  87.5 0.0 collective-permute-done.8
  87.5 0.0 collective-permute-done.9
  87.5 0.1 fusion.7
  87.6 0.1 collective-permute-start.11
  87.7 0.7 collective-permute-start.12
  88.4 0.8 collective-permute-start.13
  89.2 6.4 %backs.6 = (f32[2048,768]{1,0:T(8,128)S(1)}, bf16[2048,768]{1,0:T(8,128)(2,1)S(1)}) custom-call(f32[2,512]{1,0:T(2,128)S(1)} %get-tuple-element.38.stats_ref, f32[1,512]{1,0:T(1,128)S(1)} %get-tuple-element.45.code_ref, f32[8,512]{1,0:T(8,128)S(1)} %get-tuple-element.46.tops_ref, ...), custom_call_target="tpu_custom_call", output_to_operand_aliasing={{0}: (5, {}), {1}: (6, {})} | custom-call | flops 3221225472 | bytes 4194304 | tf_op jit(solution)/shard_map/backs/pallas_call | solution.py:300
  95.5 0.0 collective-permute-done.11
  95.6 0.0 collective-permute-done.13
  95.6 0.1 fusion.4
  95.7 4.7 %collective-permute-start.14 = (f32[2,2048]{1,0:T(2,128)S(1)}, f32[2,2048]{1,0:T(2,128)S(1)}, u32[]{:S(2)}, u32[]{:S(2)}) collective-permute-start(f32[2,2048]{1,0:T(2,128)S(1)} %pad_maximum_fusion.3), channel_id=1, source_target_pairs={{32,0},{64,32},{96,64},{0,96},{33,1},{65,33},{97,65},{1,97},{34,2}... | collective-permute-start | bytes 49160 | tf_op jit(solution)/shard_map/ppermute | solution.py:26
  100.4 5.9 %backs.7 = (f32[2048,768]{1,0:T(8,128)S(1)}, bf16[2048,768]{1,0:T(8,128)(2,1)S(1)}) custom-call(f32[2,512]{1,0:T(2,128)S(1)} %get-tuple-element.41.stats_ref, f32[1,512]{1,0:T(1,128)S(1)} %get-tuple-element.42.code_ref, f32[8,512]{1,0:T(8,128)S(1)} %get-tuple-element.43.tops_ref, ...), custom_call_target="tpu_custom_call", output_to_operand_aliasing={{0}: (5, {}), {1}: (6, {})} | custom-call | flops 3221225472 | bytes 4194304 | tf_op jit(solution)/shard_map/backs/pallas_call | solution.py:300
  106.3 0.1 collective-permute-start.15
  106.4 1.4 collective-permute-start.16
  107.8 2.7 %collective-permute-done.15 = f32[2,2048]{1,0:T(2,128)S(1)} collective-permute-done((f32[2,2048]{1,0:T(2,128)S(1)}, f32[2,2048]{1,0:T(2,128)S(1)}, u32[]{:S(2)}, u32[]{:S(2)}) %collective-permute-start.15) | collective-permute-done | bytes 16416 | tf_op jit(solution)/shard_map/ppermute | solution.py:26
  110.5 0.0 collective-permute-done.16
  110.6 0.1 fusion.1
  110.7 1.5 scaled.3
  112.1 1.3 collective-permute-start.17
  113.4 1.5 scaled.2
  114.9 1.6 collective-permute-done.17
  116.5 0.5 add_convert_fusion
  117.0 30.5 %all_to_all.26 = bf16[64,16,768]{2,1,0:T(8,128)(2,1)S(1)} all-to-all(bf16[64,16,768]{2,1,0:T(8,128)(2,1)S(1)} %bitcast.15), channel_id=1, replica_groups=mesh['z'=4,'core'=2,'y'=4,'x'=4] {'z','y','x'}, dimensions={0} | all-to-all | bytes 3145728 | tf_op jit(solution)/shard_map/all_to_all | solution.py:364
  147.5 0.2 convert_reduce_fusion
  147.7 0.0 copy-start.3
  147.8 0.1 broadcast_in_dim.58
  147.9 28.9 %all_to_all.27 = bf16[64,16,768]{2,1,0:T(8,128)(2,1)S(1)} all-to-all(bf16[64,16,768]{2,1,0:T(8,128)(2,1)S(1)} %broadcast_in_dim.58), channel_id=1, replica_groups=mesh['z'=4,'core'=2,'y'=4,'x'=4] {'z','y','x'}, dimensions={0} | all-to-all | bytes 3145728 | tf_op jit(solution)/shard_map/all_to_all | solution.py:36
  176.8 2.5 %collective-permute-start.18 = (bf16[1024,768]{1,0:T(8,128)(2,1)S(1)}, bf16[1024,768]{1,0:T(8,128)(2,1)S(1)}, u32[]{:S(2)}, u32[]{:S(2)}) collective-permute-start(bf16[1024,768]{1,0:T(8,128)(2,1)S(1)} %bitcast.8), channel_id=1, source_target_pairs={{16,0},{0,16},{17,1},{1,17},{18,2},{2,18},{19,3},{3,19},{20,4},{4,... | collective-permute-start | bytes 4718600 | tf_op jit(solution)/shard_map/ppermute | solution.py:26
  179.2 1.1 fusion
  180.3 2.4 %adapter.2.refs_0_ = f32[768,768]{1,0:T(8,128)S(1)} custom-call(s32[132]{0:T(256)S(1)} %concatenate.19.place, bf16[768,512]{1,0:T(8,128)(2,1)S(1)} %get-tuple-element.62.q0, bf16[768,512]{1,0:T(8,128)(2,1)S(1)} %get-tuple-element.63.q1, bf16[768,512]{1,0:T(8,128)(2,1)S(1)} %get-tuple-element.64.q2, bf16[768,512]{1,0:T(8,128)(2,1)S(1)} %get-tuple-element.65.q3, ...), custom_call_target="tpu_custom_call" | custom-call | flops 1207959552 | bytes 3145728 | tf_op jit(solution)/shard_map/adapter/pallas_call | solution.py:378
  182.7 3.6 %adapter.3 = f32[768,768]{1,0:T(8,128)} custom-call(s32[132]{0:T(256)S(1)} %concatenate.19.place, bf16[768,512]{1,0:T(8,128)(2,1)S(1)} %get-tuple-element.62.q0, bf16[768,512]{1,0:T(8,128)(2,1)S(1)} %get-tuple-element.63.q1, bf16[768,512]{1,0:T(8,128)(2,1)S(1)} %get-tuple-element.64.q2, bf16[768,512]{1,0:T(8,128)(2,1)S(1)} %get-tuple-element.65.q3, ...), custom_call_target="tpu_custom_call" | custom-call | flops 1207959552 | bytes 3145728 | tf_op jit(solution)/shard_map/adapter/pallas_call | solution.py:378
  (28 shorter events, 0.3 us)
Async XLA Ops:
  21.0 5.6 %collective-permute-start = (bf16[256,896]{1,0:T(8,128)(2,1)S(1)}, bf16[256,896]{1,0:T(8,128)(2,1)S(1)}, u32[]{:S(2)}, u32[]{:S(2)}) collective-permute-start(bf16[256,896]{1,0:T(8,128)(2,1)S(1)} %bitcast.10), channel_id=1, source_target_pairs={{16,0},{0,16},{17,1},{1,17},{18,2},{2,18},{19,3},{3,19},{20,4},{4,... | collective-permute-start | bytes 1376264 | tf_op jit(solution)/shard_map/ppermute | solution.py:26
  22.8 16.0 %collective-permute-start.1 = (bf16[256,896]{1,0:T(8,128)(2,1)S(1)}, bf16[256,896]{1,0:T(8,128)(2,1)S(1)}, u32[]{:S(2)}, u32[]{:S(2)}) collective-permute-start(bf16[256,896]{1,0:T(8,128)(2,1)S(1)} %bitcast.11), channel_id=1, source_target_pairs={{32,0},{64,32},{96,64},{0,96},{33,1},{65,33},{97,65},{1,97},{34,2}... | collective-permute-start | bytes 1376264 | tf_op jit(solution)/shard_map/ppermute | solution.py:26
  26.5 13.1 %collective-permute-start.3 = (bf16[256,896]{1,0:T(8,128)(2,1)S(1)}, bf16[256,896]{1,0:T(8,128)(2,1)S(1)}, u32[]{:S(2)}, u32[]{:S(2)}) collective-permute-start(bf16[256,896]{1,0:T(8,128)(2,1)S(1)} %bitcast.12), channel_id=1, source_target_pairs={{96,0},{0,32},{32,64},{64,96},{97,1},{1,33},{33,65},{65,97},{98,2}... | collective-permute-start | bytes 1376264 | tf_op jit(solution)/shard_map/ppermute | solution.py:26
  26.5 2.8 %copy-start = (bf16[8,512,768]{2,1,0:T(8,128)(2,1)S(1)}, bf16[8,512,768]{2,1,0:T(8,128)(2,1)}, u32[]{:S(2)}) copy-start(bf16[8,512,768]{2,1,0:T(8,128)(2,1)} %rows_ref.15) | copy-start | bytes 18874372
  29.3 1.3 copy-start.2
  30.6 21.3 %copy-start.1 = (bf16[8,512,768]{2,1,0:T(8,128)(2,1)S(1)}, bf16[8,512,768]{2,1,0:T(8,128)(2,1)}, u32[]{:S(2)}) copy-start(bf16[8,512,768]{2,1,0:T(8,128)(2,1)} %rows_ref.15) | copy-start | bytes 18874372
  37.4 13.4 %collective-permute-start.5 = (bf16[256,896]{1,0:T(8,128)(2,1)S(1)}, bf16[256,896]{1,0:T(8,128)(2,1)S(1)}, u32[]{:S(2)}, u32[]{:S(2)}) collective-permute-start(bf16[256,896]{1,0:T(8,128)(2,1)S(1)} %bitcast.14), channel_id=1, source_target_pairs={{64,0},{96,32},{0,64},{32,96},{65,1},{97,33},{1,65},{33,97},{66,2}... | collective-permute-start | bytes 1376264 | tf_op jit(solution)/shard_map/ppermute | solution.py:26
  38.8 13.1 %collective-permute-start.2 = (bf16[256,896]{1,0:T(8,128)(2,1)S(1)}, bf16[256,896]{1,0:T(8,128)(2,1)S(1)}, u32[]{:S(2)}, u32[]{:S(2)}) collective-permute-start(bf16[256,896]{1,0:T(8,128)(2,1)S(1)} %collective-permute-done.1.own_ref), channel_id=1, source_target_pairs={{16,0},{0,16},{17,1},{1,17},{18,2},{2,18},{19,3},{3,19},{20,4},{4,... | collective-permute-start | bytes 1376264 | tf_op jit(solution)/shard_map/ppermute | solution.py:26
  39.6 19.3 %collective-permute-start.4 = (bf16[256,896]{1,0:T(8,128)(2,1)S(1)}, bf16[256,896]{1,0:T(8,128)(2,1)S(1)}, u32[]{:S(2)}, u32[]{:S(2)}) collective-permute-start(bf16[256,896]{1,0:T(8,128)(2,1)S(1)} %collective-permute-done.3.own_ref), channel_id=1, source_target_pairs={{16,0},{0,16},{17,1},{1,17},{18,2},{2,18},{19,3},{3,19},{20,4},{4,... | collective-permute-start | bytes 1376264 | tf_op jit(solution)/shard_map/ppermute | solution.py:26
  50.7 15.1 %collective-permute-start.6 = (bf16[256,896]{1,0:T(8,128)(2,1)S(1)}, bf16[256,896]{1,0:T(8,128)(2,1)S(1)}, u32[]{:S(2)}, u32[]{:S(2)}) collective-permute-start(bf16[256,896]{1,0:T(8,128)(2,1)S(1)} %collective-permute-done.5.own_ref), channel_id=1, source_target_pairs={{16,0},{0,16},{17,1},{1,17},{18,2},{2,18},{19,3},{3,19},{20,4},{4,... | collective-permute-start | bytes 1376264 | tf_op jit(solution)/shard_map/ppermute | solution.py:26
  72.9 5.9 %collective-permute-start.7 = (f32[2,2048]{1,0:T(2,128)S(1)}, f32[2,2048]{1,0:T(2,128)S(1)}, u32[]{:S(2)}, u32[]{:S(2)}) collective-permute-start(f32[2,2048]{1,0:T(2,128)S(1)} %constant_dynamic-update-slice_fusion.local_ref), channel_id=1, source_target_pairs={{16,0},{0,16},{17,1},{1,17},{18,2},{2,18},{19,3},{3,19},{20,4},{4,... | collective-permute-start | bytes 49160 | tf_op jit(solution)/shard_map/ppermute | solution.py:26
  78.8 8.7 %collective-permute-start.10 = (f32[2,2048]{1,0:T(2,128)S(1)}, f32[2,2048]{1,0:T(2,128)S(1)}, u32[]{:S(2)}, u32[]{:S(2)}) collective-permute-start(f32[2,2048]{1,0:T(2,128)S(1)} %pad_maximum_fusion.1), channel_id=1, source_target_pairs={{3,0},{0,1},{1,2},{2,3},{7,4},{4,5},{5,6},{6,7},{11,8},{8,9},{9,10... | collective-permute-start | bytes 49160 | tf_op jit(solution)/shard_map/ppermute | solution.py:26
  79.1 8.5 %collective-permute-start.8 = (f32[2,2048]{1,0:T(2,128)S(1)}, f32[2,2048]{1,0:T(2,128)S(1)}, u32[]{:S(2)}, u32[]{:S(2)}) collective-permute-start(f32[2,2048]{1,0:T(2,128)S(1)} %pad_maximum_fusion.1), channel_id=1, source_target_pairs={{1,0},{2,1},{3,2},{0,3},{5,4},{6,5},{7,6},{4,7},{9,8},{10,9},{11,1... | collective-permute-start | bytes 49160 | tf_op jit(solution)/shard_map/ppermute | solution.py:26
  81.6 5.9 %collective-permute-start.9 = (f32[2,2048]{1,0:T(2,128)S(1)}, f32[2,2048]{1,0:T(2,128)S(1)}, u32[]{:S(2)}, u32[]{:S(2)}) collective-permute-start(f32[2,2048]{1,0:T(2,128)S(1)} %pad_maximum_fusion.1), channel_id=1, source_target_pairs={{2,0},{3,1},{0,2},{1,3},{6,4},{7,5},{4,6},{5,7},{10,8},{11,9},{8,1... | collective-permute-start | bytes 49160 | tf_op jit(solution)/shard_map/ppermute | solution.py:26
  87.6 7.9 %collective-permute-start.11 = (f32[2,2048]{1,0:T(2,128)S(1)}, f32[2,2048]{1,0:T(2,128)S(1)}, u32[]{:S(2)}, u32[]{:S(2)}) collective-permute-start(f32[2,2048]{1,0:T(2,128)S(1)} %pad_maximum_fusion.2), channel_id=1, source_target_pairs={{4,0},{8,4},{12,8},{0,12},{5,1},{9,5},{13,9},{1,13},{6,2},{10,6},{... | collective-permute-start | bytes 49160 | tf_op jit(solution)/shard_map/ppermute | solution.py:26
  87.7 7.8 %collective-permute-start.12 = (f32[2,2048]{1,0:T(2,128)S(1)}, f32[2,2048]{1,0:T(2,128)S(1)}, u32[]{:S(2)}, u32[]{:S(2)}) collective-permute-start(f32[2,2048]{1,0:T(2,128)S(1)} %pad_maximum_fusion.2), channel_id=1, source_target_pairs={{8,0},{12,4},{0,8},{4,12},{9,1},{13,5},{1,9},{5,13},{10,2},{14,6},... | collective-permute-start | bytes 49160 | tf_op jit(solution)/shard_map/ppermute | solution.py:26
  88.4 7.2 %collective-permute-start.13 = (f32[2,2048]{1,0:T(2,128)S(1)}, f32[2,2048]{1,0:T(2,128)S(1)}, u32[]{:S(2)}, u32[]{:S(2)}) collective-permute-start(f32[2,2048]{1,0:T(2,128)S(1)} %pad_maximum_fusion.2), channel_id=1, source_target_pairs={{12,0},{0,4},{4,8},{8,12},{13,1},{1,5},{5,9},{9,13},{14,2},{2,6},{... | collective-permute-start | bytes 49160 | tf_op jit(solution)/shard_map/ppermute | solution.py:26
  95.7 12.1 %collective-permute-start.14 = (f32[2,2048]{1,0:T(2,128)S(1)}, f32[2,2048]{1,0:T(2,128)S(1)}, u32[]{:S(2)}, u32[]{:S(2)}) collective-permute-start(f32[2,2048]{1,0:T(2,128)S(1)} %pad_maximum_fusion.3), channel_id=1, source_target_pairs={{32,0},{64,32},{96,64},{0,96},{33,1},{65,33},{97,65},{1,97},{34,2}... | collective-permute-start | bytes 49160 | tf_op jit(solution)/shard_map/ppermute | solution.py:26
  106.3 4.2 %collective-permute-start.15 = (f32[2,2048]{1,0:T(2,128)S(1)}, f32[2,2048]{1,0:T(2,128)S(1)}, u32[]{:S(2)}, u32[]{:S(2)}) collective-permute-start(f32[2,2048]{1,0:T(2,128)S(1)} %pad_maximum_fusion.3), channel_id=1, source_target_pairs={{64,0},{96,32},{0,64},{32,96},{65,1},{97,33},{1,65},{33,97},{66,2}... | collective-permute-start | bytes 49160 | tf_op jit(solution)/shard_map/ppermute | solution.py:26
  106.4 4.1 %collective-permute-start.16 = (f32[2,2048]{1,0:T(2,128)S(1)}, f32[2,2048]{1,0:T(2,128)S(1)}, u32[]{:S(2)}, u32[]{:S(2)}) collective-permute-start(f32[2,2048]{1,0:T(2,128)S(1)} %pad_maximum_fusion.3), channel_id=1, source_target_pairs={{96,0},{0,32},{32,64},{64,96},{97,1},{1,33},{33,65},{65,97},{98,2}... | collective-permute-start | bytes 49160 | tf_op jit(solution)/shard_map/ppermute | solution.py:26
  112.1 4.3 %collective-permute-start.17 = (bf16[1024,768]{1,0:T(8,128)(2,1)S(1)}, bf16[1024,768]{1,0:T(8,128)(2,1)S(1)}, u32[]{:S(2)}, u32[]{:S(2)}) collective-permute-start(bf16[1024,768]{1,0:T(8,128)(2,1)S(1)} %scaled.3), channel_id=1, source_target_pairs={{16,0},{0,16},{17,1},{1,17},{18,2},{2,18},{19,3},{3,19},{20,4},{4,... | collective-permute-start | bytes 4718600 | tf_op jit(solution)/shard_map/ppermute | solution.py:26
  147.7 31.5 %copy-start.3 = (bf16[768,768]{1,0:T(8,128)(2,1)S(1)}, bf16[768,768]{1,0:T(8,128)(2,1)}, u32[]{:S(2)}) copy-start(bf16[768,768]{1,0:T(8,128)(2,1)} %w_ref.7) | copy-start | bytes 3538948
  176.8 6.0 %collective-permute-start.18 = (bf16[1024,768]{1,0:T(8,128)(2,1)S(1)}, bf16[1024,768]{1,0:T(8,128)(2,1)S(1)}, u32[]{:S(2)}, u32[]{:S(2)}) collective-permute-start(bf16[1024,768]{1,0:T(8,128)(2,1)S(1)} %bitcast.8), channel_id=1, source_target_pairs={{16,0},{0,16},{17,1},{1,17},{18,2},{2,18},{19,3},{3,19},{20,4},{4,... | collective-permute-start | bytes 4718600 | tf_op jit(solution)/shard_map/ppermute | solution.py:26

commit v4 on v3

--- a/solution.py
+++ b/solution.py
@@ -160,19 +160,22 @@
     code = code_ref[...]
     index = lax.broadcasted_iota(jnp.int32, (1, tile), 1).astype(jnp.float32)
     sub = lax.broadcasted_iota(jnp.int32, (16, width), 0)
-    none = float(tile)
+    keys = lists * per
+    none = float(tile * keys)
+    both = jnp.where(code >= 0.0, index * float(keys) + code, none)
 
     def first_after(last):
-        return jnp.min(jnp.where((code >= 0.0) & (index > last), index, none))
-
-    def step(at):
-        key = jnp.max(jnp.where(index == at, code, -1.0)).astype(jnp.int32)
+        return jnp.min(jnp.where(both > last, both, none))
+
+    def step(found):
+        at = found.astype(jnp.int32) // keys
+        key = found.astype(jnp.int32) % keys
         group = rows_ref[key // per, pl.ds(pl.multiple_of((key % per) // 16 * 16, 16), 16), :]
         row = jnp.sum(jnp.where(sub == key % 16, group.astype(jnp.float32), 0.0), axis=0, keepdims=True)
-        row_ref[pl.ds(at.astype(jnp.int32), 1), :] = row
-        return first_after(at)
-
-    lax.while_loop(lambda at: at < none, step, first_after(-1.0))
+        row_ref[pl.ds(at, 1), :] = row
+        return first_after(found)
+
+    lax.while_loop(lambda found: found < none, step, first_after(-1.0))
     target_ref[...] = row_ref[...].astype(jnp.bfloat16)
 
 
@@ -297,7 +300,7 @@
     out_all = target_all = None
     for i in range(steps):
         rest = [] if i == 0 else [out_all, target_all]
-        out_all, target_all = pl.pallas_call(
+        call = pl.pallas_call(
             back_kernel,
             grid=(2,),
             in_specs=[
@@ -323,7 +326,8 @@
                 flops=2 * tile * width * keys, bytes_accessed=tile * keys * 2, transcendentals=0
             ),
             name="backs",
-        )(stats[i], codes[i], tops[i], weights[i], index_rows, *rest)
+        )
+        out_all, target_all = call(stats[i], codes[i], tops[i], weights[i], index_rows, *rest)
 
     local_stats = jnp.concatenate(stats, axis=1)
     whole_stats = local_stats

time: 187 us -> 186 us (level)
  no operation moved by 1% of the time
where the time goes in v4:
time: 186 us
  blocking collectives  77.7 us (42%)
  Pallas kernels  59.5 us (32%)
  starting transfers between devices  23.8 us (13%)
  waiting for transfers between devices  14.5 us (8%)
  local copies, waits for them, and re-layouts  4.99 us (3%)
  other arithmetic  3.33 us (2%)
    all_to_all x2, blocking collectives, spread_axes(): return lax.all_to_all(spread, axes, split_axis=0, concat_axis=0, tiled=True)  46.2 us
    all_to_all x1, blocking collectives, all_steps(): lax.all_to_all(merged, CHIPS, split_axis=0, concat_axis=0, tiled=True)  31.5 us
    pallas_call x4, Pallas kernels, all_steps(): outs = call(place, own, other, adapter_w, index_rows)  27.6 us
    ppermute x19, starting transfers between devices, from_ahead(): lax.ppermute(value, axis, [((i + step) % size, i) for i in range(size)])  23.8 us
    pallas_call x4, Pallas kernels, all_steps(): call(stats[i], codes[i], tops[i], weights[i], index_rows, *rest)  23 us
    ppermute x19, waiting for transfers between devices, from_ahead(): lax.ppermute(value, axis, [((i + step) % size, i) for i in range(size)])  14.5 us
    pallas_call x2, Pallas kernels, product(): pl.pallas_call(functools.partial(adapter_kernel, other), grid_spec=pltpu....  6.02 us
    unnamed x11, local copies, waits for them, and re-layouts  4.08 us
  transfers between devices with their start and end apart: 19, of which 3 were waited for; matrix products, arithmetic and copies ran while one was open for 1% of the time, Pallas kernels for 26%

profile of v4, /device:TPU:1, one launch (start us, length us, event | category | flops | bytes accessed | tf_op | source)
XLA Modules:
  0.0 185.9 jit_solution(11926167389226219905)
XLA Ops:
  0.7 0.7 compare_select_fusion.1
  1.4 0.8 select_convert_fusion
  2.1 0.7 pad_maximum_fusion
  2.9 0.7 concatenate.19.place
  3.7 17.3 %all_to_all.25 = bf16[16,16,896]{2,1,0:T(8,128)(2,1)S(1)} all-to-all(bf16[16,16,896]{2,1,0:T(8,128)(2,1)S(1)} %broadcast_in_dim.57), channel_id=1, replica_groups=mesh['z'=4,'core'=2,'y'=4,'x'=4] {'y','x'}, dimensions={0} | all-to-all | bytes 917504 | tf_op jit(solution)/shard_map/all_to_all | solution.py:36
  21.0 1.8 collective-permute-start
  22.8 3.8 %collective-permute-start.1 = (bf16[256,896]{1,0:T(8,128)(2,1)S(1)}, bf16[256,896]{1,0:T(8,128)(2,1)S(1)}, u32[]{:S(2)}, u32[]{:S(2)}) collective-permute-start(bf16[256,896]{1,0:T(8,128)(2,1)S(1)} %bitcast.11), channel_id=1, source_target_pairs={{32,0},{64,32},{96,64},{0,96},{33,1},{65,33},{97,65},{1,97},{34,2}... | collective-permute-start | bytes 1376264 | tf_op jit(solution)/shard_map/ppermute | solution.py:26
  26.5 0.0 collective-permute-start.3
  26.5 0.0 collective-permute-done.other_ref
  26.5 2.8 %copy-done = bf16[8,512,768]{2,1,0:T(8,128)(2,1)S(1)} copy-done((bf16[8,512,768]{2,1,0:T(8,128)(2,1)S(1)}, bf16[8,512,768]{2,1,0:T(8,128)(2,1)}, u32[]{:S(2)}) %copy-start) | copy-done | bytes 6291480
  29.3 1.3 copy-done.2
  30.6 6.7 %scores.4 = (bf16[512,4096]{1,0:T(8,128)(2,1)S(1)}, f32[8,512]{1,0:T(8,128)S(1)}, f32[2,512]{1,0:T(2,128)S(1)}, f32[1,512]{1,0:T(1,128)S(1)}, bf16[768,512]{1,0:T(8,128)(2,1)S(1)}) custom-call(s32[132]{0:T(256)S(1)} %concatenate.19.place, bf16[256,896]{1,0:T(8,128)(2,1)S(1)} %bitcast.13, bf16[256,896]{1,0:T(8,128)(2,1)S(1)} %collective-permute-done.other_ref, ...), custom_call_target="tpu_custom_call" | custom-call | flops 3825205248 | bytes 4194304 | tf_op jit(solution)/shard_map/scores/pallas_call | solution.py:296
  37.4 1.4 collective-permute-start.5
  38.7 0.0 collective-permute-done.1.own_ref
  38.8 0.8 collective-permute-start.2
  39.6 0.0 collective-permute-done.3.own_ref
  39.6 1.1 collective-permute-start.4
  40.7 10.0 %collective-permute-done.5.own_ref = bf16[256,896]{1,0:T(8,128)(2,1)S(1)} collective-permute-done((bf16[256,896]{1,0:T(8,128)(2,1)S(1)}, bf16[256,896]{1,0:T(8,128)(2,1)S(1)}, u32[]{:S(2)}, u32[]{:S(2)}) %collective-permute-start.5) | collective-permute-done | bytes 458784 | tf_op jit(solution)/shard_map/ppermute | solution.py:26
  50.7 1.1 collective-permute-start.6
  51.9 0.0 collective-permute-done.2.other_ref
  51.9 7.0 %scores.5 = (bf16[512,4096]{1,0:T(8,128)(2,1)S(1)}, f32[8,512]{1,0:T(8,128)S(1)}, f32[2,512]{1,0:T(2,128)S(1)}, f32[1,512]{1,0:T(1,128)S(1)}, bf16[768,512]{1,0:T(8,128)(2,1)S(1)}) custom-call(s32[132]{0:T(256)S(1)} %concatenate.19.place, bf16[256,896]{1,0:T(8,128)(2,1)S(1)} %collective-permute-done.1.own_ref, ...), custom_call_target="tpu_custom_call" | custom-call | flops 3825205248 | bytes 4194304 | tf_op jit(solution)/shard_map/scores/pallas_call | solution.py:296
  58.9 0.0 collective-permute-done.4.other_ref
  58.9 7.0 %scores.6 = (bf16[512,4096]{1,0:T(8,128)(2,1)S(1)}, f32[8,512]{1,0:T(8,128)S(1)}, f32[2,512]{1,0:T(2,128)S(1)}, f32[1,512]{1,0:T(1,128)S(1)}, bf16[768,512]{1,0:T(8,128)(2,1)S(1)}) custom-call(s32[132]{0:T(256)S(1)} %concatenate.19.place, bf16[256,896]{1,0:T(8,128)(2,1)S(1)} %collective-permute-done.3.own_ref, ...), custom_call_target="tpu_custom_call" | custom-call | flops 3825205248 | bytes 4194304 | tf_op jit(solution)/shard_map/scores/pallas_call | solution.py:296
  65.9 0.0 collective-permute-done.6.other_ref
  65.9 7.0 %scores.7 = (bf16[512,4096]{1,0:T(8,128)(2,1)S(1)}, f32[8,512]{1,0:T(8,128)S(1)}, f32[2,512]{1,0:T(2,128)S(1)}, f32[1,512]{1,0:T(1,128)S(1)}, bf16[768,512]{1,0:T(8,128)(2,1)S(1)}) custom-call(s32[132]{0:T(256)S(1)} %concatenate.19.place, bf16[256,896]{1,0:T(8,128)(2,1)S(1)} %collective-permute-done.5.own_ref, ...), custom_call_target="tpu_custom_call" | custom-call | flops 3825205248 | bytes 4194304 | tf_op jit(solution)/shard_map/scores/pallas_call | solution.py:296
  72.9 0.1 collective-permute-start.7
  73.0 5.6 %backs.4 = (f32[2048,768]{1,0:T(8,128)S(1)}, bf16[2048,768]{1,0:T(8,128)(2,1)S(1)}) custom-call(f32[2,512]{1,0:T(2,128)S(1)} %get-tuple-element.36.stats_ref, f32[1,512]{1,0:T(1,128)S(1)} %get-tuple-element.51.code_ref, f32[8,512]{1,0:T(8,128)S(1)} %get-tuple-element.52.tops_ref, bf16[512,4096]{1,0:T(8,128)(2,1)S(1)} %get-tuple-element.53.p_ref, ...), custom_call_target="tpu_custom_call" | custom-call | flops 3221225472 | bytes 4194304 | tf_op jit(solution)/shard_map/backs/pallas_call | solution.py:330
  78.5 0.0 collective-permute-done.7
  78.6 0.2 collective-permute-start.10
  78.9 2.5 %collective-permute-start.8 = (f32[2,2048]{1,0:T(2,128)S(1)}, f32[2,2048]{1,0:T(2,128)S(1)}, u32[]{:S(2)}, u32[]{:S(2)}) collective-permute-start(f32[2,2048]{1,0:T(2,128)S(1)} %pad_maximum_fusion.1), channel_id=1, source_target_pairs={{1,0},{2,1},{3,2},{0,3},{5,4},{6,5},{7,6},{4,7},{9,8},{10,9},{11,1... | collective-permute-start | bytes 49160 | tf_op jit(solution)/shard_map/ppermute | solution.py:26
  81.4 0.0 collective-permute-start.9
  81.4 5.7 %backs.5 = (f32[2048,768]{1,0:T(8,128)S(1)}, bf16[2048,768]{1,0:T(8,128)(2,1)S(1)}) custom-call(f32[2,512]{1,0:T(2,128)S(1)} %get-tuple-element.37.stats_ref, f32[1,512]{1,0:T(1,128)S(1)} %get-tuple-element.48.code_ref, f32[8,512]{1,0:T(8,128)S(1)} %get-tuple-element.49.tops_ref, ...), custom_call_target="tpu_custom_call", output_to_operand_aliasing={{0}: (5, {}), {1}: (6, {})} | custom-call | flops 3221225472 | bytes 4194304 | tf_op jit(solution)/shard_map/backs/pallas_call | solution.py:330
  87.0 0.0 collective-permute-done.10
  87.1 0.0 collective-permute-done.8
  87.1 0.0 collective-permute-done.9
  87.1 0.1 fusion.7
  87.2 0.1 collective-permute-start.11
  87.3 0.8 collective-permute-start.12
  88.1 0.6 collective-permute-start.13
  88.7 6.0 %backs.6 = (f32[2048,768]{1,0:T(8,128)S(1)}, bf16[2048,768]{1,0:T(8,128)(2,1)S(1)}) custom-call(f32[2,512]{1,0:T(2,128)S(1)} %get-tuple-element.38.stats_ref, f32[1,512]{1,0:T(1,128)S(1)} %get-tuple-element.45.code_ref, f32[8,512]{1,0:T(8,128)S(1)} %get-tuple-element.46.tops_ref, ...), custom_call_target="tpu_custom_call", output_to_operand_aliasing={{0}: (5, {}), {1}: (6, {})} | custom-call | flops 3221225472 | bytes 4194304 | tf_op jit(solution)/shard_map/backs/pallas_call | solution.py:330
  94.8 0.0 collective-permute-done.11
  94.8 0.1 fusion.4
  94.9 4.3 %collective-permute-start.14 = (f32[2,2048]{1,0:T(2,128)S(1)}, f32[2,2048]{1,0:T(2,128)S(1)}, u32[]{:S(2)}, u32[]{:S(2)}) collective-permute-start(f32[2,2048]{1,0:T(2,128)S(1)} %pad_maximum_fusion.3), channel_id=1, source_target_pairs={{32,0},{64,32},{96,64},{0,96},{33,1},{65,33},{97,65},{1,97},{34,2}... | collective-permute-start | bytes 49160 | tf_op jit(solution)/shard_map/ppermute | solution.py:26
  99.3 5.7 %backs.7 = (f32[2048,768]{1,0:T(8,128)S(1)}, bf16[2048,768]{1,0:T(8,128)(2,1)S(1)}) custom-call(f32[2,512]{1,0:T(2,128)S(1)} %get-tuple-element.41.stats_ref, f32[1,512]{1,0:T(1,128)S(1)} %get-tuple-element.42.code_ref, f32[8,512]{1,0:T(8,128)S(1)} %get-tuple-element.43.tops_ref, ...), custom_call_target="tpu_custom_call", output_to_operand_aliasing={{0}: (5, {}), {1}: (6, {})} | custom-call | flops 3221225472 | bytes 4194304 | tf_op jit(solution)/shard_map/backs/pallas_call | solution.py:330
  105.0 0.1 collective-permute-start.15
  105.0 1.2 collective-permute-start.16
  106.3 0.0 collective-permute-done.14
  106.3 2.9 %collective-permute-done.15 = f32[2,2048]{1,0:T(2,128)S(1)} collective-permute-done((f32[2,2048]{1,0:T(2,128)S(1)}, f32[2,2048]{1,0:T(2,128)S(1)}, u32[]{:S(2)}, u32[]{:S(2)}) %collective-permute-start.15) | collective-permute-done | bytes 16416 | tf_op jit(solution)/shard_map/ppermute | solution.py:26
  109.2 0.1 fusion.1
  109.3 1.5 scaled.3
  110.8 1.3 collective-permute-start.17
  112.1 1.5 scaled.2
  113.5 1.6 collective-permute-done.17
  115.1 0.5 add_convert_fusion
  115.6 31.5 %all_to_all.26 = bf16[64,16,768]{2,1,0:T(8,128)(2,1)S(1)} all-to-all(bf16[64,16,768]{2,1,0:T(8,128)(2,1)S(1)} %bitcast.15), channel_id=1, replica_groups=mesh['z'=4,'core'=2,'y'=4,'x'=4] {'z','y','x'}, dimensions={0} | all-to-all | bytes 3145728 | tf_op jit(solution)/shard_map/all_to_all | solution.py:368
  147.1 0.2 convert_reduce_fusion
  147.3 0.0 copy-start.3
  147.3 0.1 broadcast_in_dim.58
  147.5 28.9 %all_to_all.27 = bf16[64,16,768]{2,1,0:T(8,128)(2,1)S(1)} all-to-all(bf16[64,16,768]{2,1,0:T(8,128)(2,1)S(1)} %broadcast_in_dim.58), channel_id=1, replica_groups=mesh['z'=4,'core'=2,'y'=4,'x'=4] {'z','y','x'}, dimensions={0} | all-to-all | bytes 3145728 | tf_op jit(solution)/shard_map/all_to_all | solution.py:36
  176.3 2.5 %collective-permute-start.18 = (bf16[1024,768]{1,0:T(8,128)(2,1)S(1)}, bf16[1024,768]{1,0:T(8,128)(2,1)S(1)}, u32[]{:S(2)}, u32[]{:S(2)}) collective-permute-start(bf16[1024,768]{1,0:T(8,128)(2,1)S(1)} %bitcast.8), channel_id=1, source_target_pairs={{16,0},{0,16},{17,1},{1,17},{18,2},{2,18},{19,3},{3,19},{20,4},{4,... | collective-permute-start | bytes 4718600 | tf_op jit(solution)/shard_map/ppermute | solution.py:26
  178.8 1.1 fusion
  179.9 2.4 %adapter.2.refs_0_ = f32[768,768]{1,0:T(8,128)S(1)} custom-call(s32[132]{0:T(256)S(1)} %concatenate.19.place, bf16[768,512]{1,0:T(8,128)(2,1)S(1)} %get-tuple-element.62.q0, bf16[768,512]{1,0:T(8,128)(2,1)S(1)} %get-tuple-element.63.q1, bf16[768,512]{1,0:T(8,128)(2,1)S(1)} %get-tuple-element.64.q2, bf16[768,512]{1,0:T(8,128)(2,1)S(1)} %get-tuple-element.65.q3, ...), custom_call_target="tpu_custom_call" | custom-call | flops 1207959552 | bytes 3145728 | tf_op jit(solution)/shard_map/adapter/pallas_call | solution.py:382
  182.3 0.0 collective-permute-done.18.b_ref
  182.3 3.6 %adapter.3 = f32[768,768]{1,0:T(8,128)} custom-call(s32[132]{0:T(256)S(1)} %concatenate.19.place, bf16[768,512]{1,0:T(8,128)(2,1)S(1)} %get-tuple-element.62.q0, bf16[768,512]{1,0:T(8,128)(2,1)S(1)} %get-tuple-element.63.q1, bf16[768,512]{1,0:T(8,128)(2,1)S(1)} %get-tuple-element.64.q2, bf16[768,512]{1,0:T(8,128)(2,1)S(1)} %get-tuple-element.65.q3, ...), custom_call_target="tpu_custom_call" | custom-call | flops 1207959552 | bytes 3145728 | tf_op jit(solution)/shard_map/adapter/pallas_call | solution.py:382
  (28 shorter events, 0.3 us)
Async XLA Ops:
  21.0 5.6 %collective-permute-start = (bf16[256,896]{1,0:T(8,128)(2,1)S(1)}, bf16[256,896]{1,0:T(8,128)(2,1)S(1)}, u32[]{:S(2)}, u32[]{:S(2)}) collective-permute-start(bf16[256,896]{1,0:T(8,128)(2,1)S(1)} %bitcast.10), channel_id=1, source_target_pairs={{16,0},{0,16},{17,1},{1,17},{18,2},{2,18},{19,3},{3,19},{20,4},{4,... | collective-permute-start | bytes 1376264 | tf_op jit(solution)/shard_map/ppermute | solution.py:26
  22.8 16.0 %collective-permute-start.1 = (bf16[256,896]{1,0:T(8,128)(2,1)S(1)}, bf16[256,896]{1,0:T(8,128)(2,1)S(1)}, u32[]{:S(2)}, u32[]{:S(2)}) collective-permute-start(bf16[256,896]{1,0:T(8,128)(2,1)S(1)} %bitcast.11), channel_id=1, source_target_pairs={{32,0},{64,32},{96,64},{0,96},{33,1},{65,33},{97,65},{1,97},{34,2}... | collective-permute-start | bytes 1376264 | tf_op jit(solution)/shard_map/ppermute | solution.py:26
  26.5 13.1 %collective-permute-start.3 = (bf16[256,896]{1,0:T(8,128)(2,1)S(1)}, bf16[256,896]{1,0:T(8,128)(2,1)S(1)}, u32[]{:S(2)}, u32[]{:S(2)}) collective-permute-start(bf16[256,896]{1,0:T(8,128)(2,1)S(1)} %bitcast.12), channel_id=1, source_target_pairs={{96,0},{0,32},{32,64},{64,96},{97,1},{1,33},{33,65},{65,97},{98,2}... | collective-permute-start | bytes 1376264 | tf_op jit(solution)/shard_map/ppermute | solution.py:26
  26.5 2.8 %copy-start = (bf16[8,512,768]{2,1,0:T(8,128)(2,1)S(1)}, bf16[8,512,768]{2,1,0:T(8,128)(2,1)}, u32[]{:S(2)}) copy-start(bf16[8,512,768]{2,1,0:T(8,128)(2,1)} %rows_ref.15) | copy-start | bytes 18874372
  29.3 1.3 copy-start.2
  30.6 21.3 %copy-start.1 = (bf16[8,512,768]{2,1,0:T(8,128)(2,1)S(1)}, bf16[8,512,768]{2,1,0:T(8,128)(2,1)}, u32[]{:S(2)}) copy-start(bf16[8,512,768]{2,1,0:T(8,128)(2,1)} %rows_ref.15) | copy-start | bytes 18874372
  37.4 13.4 %collective-permute-start.5 = (bf16[256,896]{1,0:T(8,128)(2,1)S(1)}, bf16[256,896]{1,0:T(8,128)(2,1)S(1)}, u32[]{:S(2)}, u32[]{:S(2)}) collective-permute-start(bf16[256,896]{1,0:T(8,128)(2,1)S(1)} %bitcast.14), channel_id=1, source_target_pairs={{64,0},{96,32},{0,64},{32,96},{65,1},{97,33},{1,65},{33,97},{66,2}... | collective-permute-start | bytes 1376264 | tf_op jit(solution)/shard_map/ppermute | solution.py:26
  38.8 13.1 %collective-permute-start.2 = (bf16[256,896]{1,0:T(8,128)(2,1)S(1)}, bf16[256,896]{1,0:T(8,128)(2,1)S(1)}, u32[]{:S(2)}, u32[]{:S(2)}) collective-permute-start(bf16[256,896]{1,0:T(8,128)(2,1)S(1)} %collective-permute-done.1.own_ref), channel_id=1, source_target_pairs={{16,0},{0,16},{17,1},{1,17},{18,2},{2,18},{19,3},{3,19},{20,4},{4,... | collective-permute-start | bytes 1376264 | tf_op jit(solution)/shard_map/ppermute | solution.py:26
  39.6 19.3 %collective-permute-start.4 = (bf16[256,896]{1,0:T(8,128)(2,1)S(1)}, bf16[256,896]{1,0:T(8,128)(2,1)S(1)}, u32[]{:S(2)}, u32[]{:S(2)}) collective-permute-start(bf16[256,896]{1,0:T(8,128)(2,1)S(1)} %collective-permute-done.3.own_ref), channel_id=1, source_target_pairs={{16,0},{0,16},{17,1},{1,17},{18,2},{2,18},{19,3},{3,19},{20,4},{4,... | collective-permute-start | bytes 1376264 | tf_op jit(solution)/shard_map/ppermute | solution.py:26
  50.7 15.1 %collective-permute-start.6 = (bf16[256,896]{1,0:T(8,128)(2,1)S(1)}, bf16[256,896]{1,0:T(8,128)(2,1)S(1)}, u32[]{:S(2)}, u32[]{:S(2)}) collective-permute-start(bf16[256,896]{1,0:T(8,128)(2,1)S(1)} %collective-permute-done.5.own_ref), channel_id=1, source_target_pairs={{16,0},{0,16},{17,1},{1,17},{18,2},{2,18},{19,3},{3,19},{20,4},{4,... | collective-permute-start | bytes 1376264 | tf_op jit(solution)/shard_map/ppermute | solution.py:26
  72.9 5.7 %collective-permute-start.7 = (f32[2,2048]{1,0:T(2,128)S(1)}, f32[2,2048]{1,0:T(2,128)S(1)}, u32[]{:S(2)}, u32[]{:S(2)}) collective-permute-start(f32[2,2048]{1,0:T(2,128)S(1)} %constant_dynamic-update-slice_fusion.local_ref), channel_id=1, source_target_pairs={{16,0},{0,16},{17,1},{1,17},{18,2},{2,18},{19,3},{3,19},{20,4},{4,... | collective-permute-start | bytes 49160 | tf_op jit(solution)/shard_map/ppermute | solution.py:26
  78.6 8.4 %collective-permute-start.10 = (f32[2,2048]{1,0:T(2,128)S(1)}, f32[2,2048]{1,0:T(2,128)S(1)}, u32[]{:S(2)}, u32[]{:S(2)}) collective-permute-start(f32[2,2048]{1,0:T(2,128)S(1)} %pad_maximum_fusion.1), channel_id=1, source_target_pairs={{3,0},{0,1},{1,2},{2,3},{7,4},{4,5},{5,6},{6,7},{11,8},{8,9},{9,10... | collective-permute-start | bytes 49160 | tf_op jit(solution)/shard_map/ppermute | solution.py:26
  78.9 8.2 %collective-permute-start.8 = (f32[2,2048]{1,0:T(2,128)S(1)}, f32[2,2048]{1,0:T(2,128)S(1)}, u32[]{:S(2)}, u32[]{:S(2)}) collective-permute-start(f32[2,2048]{1,0:T(2,128)S(1)} %pad_maximum_fusion.1), channel_id=1, source_target_pairs={{1,0},{2,1},{3,2},{0,3},{5,4},{6,5},{7,6},{4,7},{9,8},{10,9},{11,1... | collective-permute-start | bytes 49160 | tf_op jit(solution)/shard_map/ppermute | solution.py:26
  81.4 5.7 %collective-permute-start.9 = (f32[2,2048]{1,0:T(2,128)S(1)}, f32[2,2048]{1,0:T(2,128)S(1)}, u32[]{:S(2)}, u32[]{:S(2)}) collective-permute-start(f32[2,2048]{1,0:T(2,128)S(1)} %pad_maximum_fusion.1), channel_id=1, source_target_pairs={{2,0},{3,1},{0,2},{1,3},{6,4},{7,5},{4,6},{5,7},{10,8},{11,9},{8,1... | collective-permute-start | bytes 49160 | tf_op jit(solution)/shard_map/ppermute | solution.py:26
  87.2 7.6 %collective-permute-start.11 = (f32[2,2048]{1,0:T(2,128)S(1)}, f32[2,2048]{1,0:T(2,128)S(1)}, u32[]{:S(2)}, u32[]{:S(2)}) collective-permute-start(f32[2,2048]{1,0:T(2,128)S(1)} %pad_maximum_fusion.2), channel_id=1, source_target_pairs={{4,0},{8,4},{12,8},{0,12},{5,1},{9,5},{13,9},{1,13},{6,2},{10,6},{... | collective-permute-start | bytes 49160 | tf_op jit(solution)/shard_map/ppermute | solution.py:26
  87.3 7.5 %collective-permute-start.12 = (f32[2,2048]{1,0:T(2,128)S(1)}, f32[2,2048]{1,0:T(2,128)S(1)}, u32[]{:S(2)}, u32[]{:S(2)}) collective-permute-start(f32[2,2048]{1,0:T(2,128)S(1)} %pad_maximum_fusion.2), channel_id=1, source_target_pairs={{8,0},{12,4},{0,8},{4,12},{9,1},{13,5},{1,9},{5,13},{10,2},{14,6},... | collective-permute-start | bytes 49160 | tf_op jit(solution)/shard_map/ppermute | solution.py:26
  88.1 6.7 %collective-permute-start.13 = (f32[2,2048]{1,0:T(2,128)S(1)}, f32[2,2048]{1,0:T(2,128)S(1)}, u32[]{:S(2)}, u32[]{:S(2)}) collective-permute-start(f32[2,2048]{1,0:T(2,128)S(1)} %pad_maximum_fusion.2), channel_id=1, source_target_pairs={{12,0},{0,4},{4,8},{8,12},{13,1},{1,5},{5,9},{9,13},{14,2},{2,6},{... | collective-permute-start | bytes 49160 | tf_op jit(solution)/shard_map/ppermute | solution.py:26
  94.9 11.3 %collective-permute-start.14 = (f32[2,2048]{1,0:T(2,128)S(1)}, f32[2,2048]{1,0:T(2,128)S(1)}, u32[]{:S(2)}, u32[]{:S(2)}) collective-permute-start(f32[2,2048]{1,0:T(2,128)S(1)} %pad_maximum_fusion.3), channel_id=1, source_target_pairs={{32,0},{64,32},{96,64},{0,96},{33,1},{65,33},{97,65},{1,97},{34,2}... | collective-permute-start | bytes 49160 | tf_op jit(solution)/shard_map/ppermute | solution.py:26
  105.0 4.2 %collective-permute-start.15 = (f32[2,2048]{1,0:T(2,128)S(1)}, f32[2,2048]{1,0:T(2,128)S(1)}, u32[]{:S(2)}, u32[]{:S(2)}) collective-permute-start(f32[2,2048]{1,0:T(2,128)S(1)} %pad_maximum_fusion.3), channel_id=1, source_target_pairs={{64,0},{96,32},{0,64},{32,96},{65,1},{97,33},{1,65},{33,97},{66,2}... | collective-permute-start | bytes 49160 | tf_op jit(solution)/shard_map/ppermute | solution.py:26
  105.0 4.1 %collective-permute-start.16 = (f32[2,2048]{1,0:T(2,128)S(1)}, f32[2,2048]{1,0:T(2,128)S(1)}, u32[]{:S(2)}, u32[]{:S(2)}) collective-permute-start(f32[2,2048]{1,0:T(2,128)S(1)} %pad_maximum_fusion.3), channel_id=1, source_target_pairs={{96,0},{0,32},{32,64},{64,96},{97,1},{1,33},{33,65},{65,97},{98,2}... | collective-permute-start | bytes 49160 | tf_op jit(solution)/shard_map/ppermute | solution.py:26
  110.8 4.3 %collective-permute-start.17 = (bf16[1024,768]{1,0:T(8,128)(2,1)S(1)}, bf16[1024,768]{1,0:T(8,128)(2,1)S(1)}, u32[]{:S(2)}, u32[]{:S(2)}) collective-permute-start(bf16[1024,768]{1,0:T(8,128)(2,1)S(1)} %scaled.3), channel_id=1, source_target_pairs={{16,0},{0,16},{17,1},{1,17},{18,2},{2,18},{19,3},{3,19},{20,4},{4,... | collective-permute-start | bytes 4718600 | tf_op jit(solution)/shard_map/ppermute | solution.py:26
  147.3 31.5 %copy-start.3 = (bf16[768,768]{1,0:T(8,128)(2,1)S(1)}, bf16[768,768]{1,0:T(8,128)(2,1)}, u32[]{:S(2)}) copy-start(bf16[768,768]{1,0:T(8,128)(2,1)} %w_ref.7) | copy-start | bytes 3538948
  176.3 6.0 %collective-permute-start.18 = (bf16[1024,768]{1,0:T(8,128)(2,1)S(1)}, bf16[1024,768]{1,0:T(8,128)(2,1)S(1)}, u32[]{:S(2)}, u32[]{:S(2)}) collective-permute-start(bf16[1024,768]{1,0:T(8,128)(2,1)S(1)} %bitcast.8), channel_id=1, source_target_pairs={{16,0},{0,16},{17,1},{1,17},{18,2},{2,18},{19,3},{3,19},{20,4},{4,... | collective-permute-start | bytes 4718600 | tf_op jit(solution)/shard_map/ppermute | solution.py:26

commit v5 on v4

--- a/solution.py
+++ b/solution.py
@@ -17,6 +17,7 @@
 AXES = ("z", "core", "y", "x")
 CHIPS = ("z", "y", "x")
 ORDER = (0, 1, 3, 2)
+COVER = 5000000000
 LOG2E = 1.4426950408889634
 WHOLE = pl.BlockSpec(memory_space=pltpu.VMEM)
 
@@ -45,7 +46,7 @@
 
 
 def score_kernel(
-    table, place, own_ref, other_ref, w_ref, rows_ref,
+    table, place, own_ref, other_ref, w_ref, rows_ref, _,
     p_ref, tops_ref, stats_ref, code_ref, q_out, q_ref, bias_ref, s_ref, here_ref,
 ):
     width = w_ref.shape[0]
@@ -141,6 +142,10 @@
     stats_ref[1:2, :] = jnp.sum(sums * jnp.exp2(tops - high), axis=0, keepdims=True)
 
 
+def turn_kernel(plane_ref, out_ref):
+    out_ref[...] = plane_ref[...].astype(jnp.float32).T.astype(jnp.bfloat16)
+
+
 def back_kernel(stats_ref, code_ref, tops_ref, p_ref, rows_ref, *refs):
     out_ref, target_ref, g_ref, row_ref = refs[-4:]
     lists, per, width = rows_ref.shape
@@ -245,13 +250,23 @@
     steps = 4
     count = steps * tile
     keys = lists_here * rows_here
+    turned = pl.pallas_call(
+        turn_kernel,
+        grid=(1,),
+        in_specs=[pl.BlockSpec((half, LANES), lambda k: (0, width // LANES))],
+        out_specs=pl.BlockSpec((LANES, half), lambda k: (0, 0)),
+        out_shape=jax.ShapeDtypeStruct((LANES, half), jnp.bfloat16),
+        compiler_params=pltpu.CompilerParams(vmem_limit_bytes=4 << 20),
+        cost_estimate=pl.CostEstimate(flops=COVER, bytes_accessed=half * LANES * 4, transcendentals=0),
+        name="turn",
+    )(plane)
     owns = [plane]
     for ahead in (1, 3):
         owns.append(from_ahead(plane, "z", ahead))
     weights, tops, stats, codes, gathered = [], [], [], [], []
     for i, ahead in enumerate(ORDER):
         if i == 1:
-            held, codes[0] = lax.optimization_barrier((plane, codes[0]))
+            held, codes[0], owns[1] = lax.optimization_barrier((plane, codes[0], owns[1]))
             owns.append(from_ahead(held, "z", 2))
         own = owns[i]
         other = from_ahead(own, "core", 1)
@@ -265,6 +280,7 @@
                     pl.BlockSpec((half, width + LANES), lambda i, *_: (0, 0)),
                     WHOLE,
                     WHOLE,
+                    pl.BlockSpec(memory_space=pl.ANY),
                 ],
                 out_specs=[
                     pl.BlockSpec((half, keys), lambda i, *_: (i, 0)),
@@ -293,7 +309,7 @@
             ),
             name="scores",
         )
-        outs = call(place, own, other, adapter_w, index_rows)
+        outs = call(place, own, other, adapter_w, index_rows, turned)
         for kept, value in zip((weights, tops, stats, codes, gathered), outs):
             kept.append(value)
 

time: 186 us -> 186 us (level)
  local copies, waits for them, and re-layouts: 4.99 us -> 0.94 us
  starting transfers between devices: 23.8 us -> 26.4 us
    unnamed x11 -> x9, local copies, waits for them, and re-layouts: 4.08 us -> 0.03 us
    ppermute x19, starting transfers between devices: 23.8 us -> 26.4 us  [from_ahead(): lax.ppermute(value, axis, [((i + step) % size, i) for i in range(size)])]
    pallas_call x4 -> x5, Pallas kernels: 27.6 us -> 28.1 us  [the longest x4 28 us: all_steps(): outs = call(place, own, other, adapter_w, index_rows, turned)]
  transfers between devices with their start and end apart: 19 -> 19, of which waited for: 3 -> 5; matrix products, arithmetic and copies ran while one was open for 1% -> 1% of each run, Pallas kernels for 26% -> 26%
where the time goes in v5:
time: 186 us; the launch traced here: 185 us
  blocking collectives  77.6 us (42%)
  Pallas kernels  60 us (32%)
  starting transfers between devices  26.4 us (14%)
  waiting for transfers between devices  15.2 us (8%)
  other arithmetic  3.29 us (2%)
    all_to_all x2, blocking collectives, spread_axes(): return lax.all_to_all(spread, axes, split_axis=0, concat_axis=0, tiled=True)  46.1 us
    all_to_all x1, blocking collectives, all_steps(): lax.all_to_all(merged, CHIPS, split_axis=0, concat_axis=0, tiled=True)  31.5 us
    pallas_call x4, Pallas kernels, all_steps(): outs = call(place, own, other, adapter_w, index_rows, turned)  28 us
    ppermute x19, starting transfers between devices, from_ahead(): lax.ppermute(value, axis, [((i + step) % size, i) for i in range(size)])  26.4 us
    pallas_call x4, Pallas kernels, all_steps(): call(stats[i], codes[i], tops[i], weights[i], index_rows, *rest)  23 us
    ppermute x19, waiting for transfers between devices, from_ahead(): lax.ppermute(value, axis, [((i + step) % size, i) for i in range(size)])  15.2 us
    pallas_call x2, Pallas kernels, product(): pl.pallas_call(functools.partial(adapter_kernel, other), grid_spec=pltpu....  6.02 us
  transfers between devices with their start and end apart: 19, of which 5 were waited for; matrix products, arithmetic and copies ran while one was open for 1% of the time, Pallas kernels for 26%

profile of v5, /device:TPU:1, one launch (start us, length us, event | category | flops | bytes accessed | tf_op | source)
XLA Modules:
  0.0 185.5 jit_solution(9862108900801688004)
XLA Ops:
  0.7 0.7 compare_select_fusion.1
  1.4 0.8 select_convert_fusion
  2.1 0.7 pad_maximum_fusion
  2.9 0.7 concatenate.19.place
  3.7 17.3 %all_to_all.25 = bf16[16,16,896]{2,1,0:T(8,128)(2,1)S(1)} all-to-all(bf16[16,16,896]{2,1,0:T(8,128)(2,1)S(1)} %broadcast_in_dim.57), channel_id=1, replica_groups=mesh['z'=4,'core'=2,'y'=4,'x'=4] {'y','x'}, dimensions={0} | all-to-all | bytes 917504 | tf_op jit(solution)/shard_map/all_to_all | solution.py:37
  21.0 1.8 collective-permute-start
  22.8 3.8 %collective-permute-start.1 = (bf16[256,896]{1,0:T(8,128)(2,1)S(1)}, bf16[256,896]{1,0:T(8,128)(2,1)S(1)}, u32[]{:S(2)}, u32[]{:S(2)}) collective-permute-start(bf16[256,896]{1,0:T(8,128)(2,1)S(1)} %bitcast.13), channel_id=1, source_target_pairs={{32,0},{64,32},{96,64},{0,96},{33,1},{65,33},{97,65},{1,97},{34,2}... | collective-permute-start | bytes 1376264 | tf_op jit(solution)/shard_map/ppermute | solution.py:27
  26.5 0.1 turn.1._
  26.7 0.1 collective-permute-start.3
  26.7 0.0 collective-permute-done.other_ref
  26.8 7.0 %scores.4 = (bf16[512,4096]{1,0:T(8,128)(2,1)S(1)}, f32[8,512]{1,0:T(8,128)S(1)}, f32[2,512]{1,0:T(2,128)S(1)}, f32[1,512]{1,0:T(1,128)S(1)}, bf16[768,512]{1,0:T(8,128)(2,1)S(1)}) custom-call(s32[132]{0:T(256)S(1)} %concatenate.19.place, bf16[256,896]{1,0:T(8,128)(2,1)S(1)} %bitcast.16, bf16[256,896]{1,0:T(8,128)(2,1)S(1)} %collective-permute-done.other_ref, ...), custom_call_target="tpu_custom_call" | custom-call | flops 3825205248 | bytes 4194304 | tf_op jit(solution)/shard_map/scores/pallas_call | solution.py:312
  33.8 2.5 %collective-permute-done.1.own_ref = bf16[256,896]{1,0:T(8,128)(2,1)S(1)} collective-permute-done((bf16[256,896]{1,0:T(8,128)(2,1)S(1)}, bf16[256,896]{1,0:T(8,128)(2,1)S(1)}, u32[]{:S(2)}, u32[]{:S(2)}) %collective-permute-start.1) | collective-permute-done | bytes 458784 | tf_op jit(solution)/shard_map/ppermute | solution.py:27
  36.3 2.0 %collective-permute-start.5 = (bf16[256,896]{1,0:T(8,128)(2,1)S(1)}, bf16[256,896]{1,0:T(8,128)(2,1)S(1)}, u32[]{:S(2)}, u32[]{:S(2)}) collective-permute-start(bf16[256,896]{1,0:T(8,128)(2,1)S(1)} %bitcast.17), channel_id=1, source_target_pairs={{64,0},{96,32},{0,64},{32,96},{65,1},{97,33},{1,65},{33,97},{66,2}... | collective-permute-start | bytes 1376264 | tf_op jit(solution)/shard_map/ppermute | solution.py:27
  38.4 1.2 collective-permute-start.2
  39.6 0.1 collective-permute-done.3.own_ref
  39.7 1.2 collective-permute-start.4
  40.9 8.1 %collective-permute-done.5.own_ref = bf16[256,896]{1,0:T(8,128)(2,1)S(1)} collective-permute-done((bf16[256,896]{1,0:T(8,128)(2,1)S(1)}, bf16[256,896]{1,0:T(8,128)(2,1)S(1)}, u32[]{:S(2)}, u32[]{:S(2)}) %collective-permute-start.5) | collective-permute-done | bytes 458784 | tf_op jit(solution)/shard_map/ppermute | solution.py:27
  49.0 1.8 collective-permute-start.6
  50.8 0.0 collective-permute-done.2.other_ref
  50.8 7.0 %scores.5 = (bf16[512,4096]{1,0:T(8,128)(2,1)S(1)}, f32[8,512]{1,0:T(8,128)S(1)}, f32[2,512]{1,0:T(2,128)S(1)}, f32[1,512]{1,0:T(1,128)S(1)}, bf16[768,512]{1,0:T(8,128)(2,1)S(1)}) custom-call(s32[132]{0:T(256)S(1)} %concatenate.19.place, bf16[256,896]{1,0:T(8,128)(2,1)S(1)} %collective-permute-done.1.own_ref, ...), custom_call_target="tpu_custom_call" | custom-call | flops 3825205248 | bytes 4194304 | tf_op jit(solution)/shard_map/scores/pallas_call | solution.py:312
  57.8 0.0 collective-permute-done.4.other_ref
  57.8 7.0 %scores.6 = (bf16[512,4096]{1,0:T(8,128)(2,1)S(1)}, f32[8,512]{1,0:T(8,128)S(1)}, f32[2,512]{1,0:T(2,128)S(1)}, f32[1,512]{1,0:T(1,128)S(1)}, bf16[768,512]{1,0:T(8,128)(2,1)S(1)}) custom-call(s32[132]{0:T(256)S(1)} %concatenate.19.place, bf16[256,896]{1,0:T(8,128)(2,1)S(1)} %collective-permute-done.3.own_ref, ...), custom_call_target="tpu_custom_call" | custom-call | flops 3825205248 | bytes 4194304 | tf_op jit(solution)/shard_map/scores/pallas_call | solution.py:312
  64.8 0.0 collective-permute-done.6.other_ref
  64.8 7.0 %scores.7 = (bf16[512,4096]{1,0:T(8,128)(2,1)S(1)}, f32[8,512]{1,0:T(8,128)S(1)}, f32[2,512]{1,0:T(2,128)S(1)}, f32[1,512]{1,0:T(1,128)S(1)}, bf16[768,512]{1,0:T(8,128)(2,1)S(1)}) custom-call(s32[132]{0:T(256)S(1)} %concatenate.19.place, bf16[256,896]{1,0:T(8,128)(2,1)S(1)} %collective-permute-done.5.own_ref, ...), custom_call_target="tpu_custom_call" | custom-call | flops 3825205248 | bytes 4194304 | tf_op jit(solution)/shard_map/scores/pallas_call | solution.py:312
  71.8 0.1 collective-permute-start.7
  71.9 5.6 %backs.4 = (f32[2048,768]{1,0:T(8,128)S(1)}, bf16[2048,768]{1,0:T(8,128)(2,1)S(1)}) custom-call(f32[2,512]{1,0:T(2,128)S(1)} %get-tuple-element.37.stats_ref, f32[1,512]{1,0:T(1,128)S(1)} %get-tuple-element.53.code_ref, f32[8,512]{1,0:T(8,128)S(1)} %get-tuple-element.54.tops_ref, bf16[512,4096]{1,0:T(8,128)(2,1)S(1)} %get-tuple-element.55.p_ref, ...), custom_call_target="tpu_custom_call" | custom-call | flops 3221225472 | bytes 4194304 | tf_op jit(solution)/shard_map/backs/pallas_call | solution.py:346
  77.5 0.0 collective-permute-done.7
  77.6 0.2 collective-permute-start.10
  77.8 2.5 %collective-permute-start.8 = (f32[2,2048]{1,0:T(2,128)S(1)}, f32[2,2048]{1,0:T(2,128)S(1)}, u32[]{:S(2)}, u32[]{:S(2)}) collective-permute-start(f32[2,2048]{1,0:T(2,128)S(1)} %pad_maximum_fusion.1), channel_id=1, source_target_pairs={{1,0},{2,1},{3,2},{0,3},{5,4},{6,5},{7,6},{4,7},{9,8},{10,9},{11,1... | collective-permute-start | bytes 49160 | tf_op jit(solution)/shard_map/ppermute | solution.py:27
  80.4 0.0 collective-permute-start.9
  80.4 5.7 %backs.5 = (f32[2048,768]{1,0:T(8,128)S(1)}, bf16[2048,768]{1,0:T(8,128)(2,1)S(1)}) custom-call(f32[2,512]{1,0:T(2,128)S(1)} %get-tuple-element.40.stats_ref, f32[1,512]{1,0:T(1,128)S(1)} %get-tuple-element.50.code_ref, f32[8,512]{1,0:T(8,128)S(1)} %get-tuple-element.51.tops_ref, ...), custom_call_target="tpu_custom_call", output_to_operand_aliasing={{0}: (5, {}), {1}: (6, {})} | custom-call | flops 3221225472 | bytes 4194304 | tf_op jit(solution)/shard_map/backs/pallas_call | solution.py:346
  86.0 0.0 collective-permute-done.10
  86.0 0.0 collective-permute-done.8
  86.0 0.0 collective-permute-done.9
  86.1 0.1 fusion.7
  86.2 0.1 collective-permute-start.11
  86.3 0.8 collective-permute-start.12
  87.1 0.6 collective-permute-start.13
  87.7 6.0 %backs.6 = (f32[2048,768]{1,0:T(8,128)S(1)}, bf16[2048,768]{1,0:T(8,128)(2,1)S(1)}) custom-call(f32[2,512]{1,0:T(2,128)S(1)} %get-tuple-element.41.stats_ref, f32[1,512]{1,0:T(1,128)S(1)} %get-tuple-element.47.code_ref, f32[8,512]{1,0:T(8,128)S(1)} %get-tuple-element.48.tops_ref, ...), custom_call_target="tpu_custom_call", output_to_operand_aliasing={{0}: (5, {}), {1}: (6, {})} | custom-call | flops 3221225472 | bytes 4194304 | tf_op jit(solution)/shard_map/backs/pallas_call | solution.py:346
  93.8 0.0 collective-permute-done.11
  93.8 0.0 collective-permute-done.12
  93.8 0.0 collective-permute-done.13
  93.8 0.1 fusion.4
  93.9 5.1 %collective-permute-start.14 = (f32[2,2048]{1,0:T(2,128)S(1)}, f32[2,2048]{1,0:T(2,128)S(1)}, u32[]{:S(2)}, u32[]{:S(2)}) collective-permute-start(f32[2,2048]{1,0:T(2,128)S(1)} %pad_maximum_fusion.3), channel_id=1, source_target_pairs={{32,0},{64,32},{96,64},{0,96},{33,1},{65,33},{97,65},{1,97},{34,2}... | collective-permute-start | bytes 49160 | tf_op jit(solution)/shard_map/ppermute | solution.py:27
  99.0 5.7 %backs.7 = (f32[2048,768]{1,0:T(8,128)S(1)}, bf16[2048,768]{1,0:T(8,128)(2,1)S(1)}) custom-call(f32[2,512]{1,0:T(2,128)S(1)} %get-tuple-element.43.stats_ref, f32[1,512]{1,0:T(1,128)S(1)} %get-tuple-element.44.code_ref, f32[8,512]{1,0:T(8,128)S(1)} %get-tuple-element.45.tops_ref, ...), custom_call_target="tpu_custom_call", output_to_operand_aliasing={{0}: (5, {}), {1}: (6, {})} | custom-call | flops 3221225472 | bytes 4194304 | tf_op jit(solution)/shard_map/backs/pallas_call | solution.py:346
  104.7 0.1 collective-permute-start.15
  104.8 1.2 collective-permute-start.16
  106.0 0.0 collective-permute-done.14
  106.0 2.9 %collective-permute-done.15 = f32[2,2048]{1,0:T(2,128)S(1)} collective-permute-done((f32[2,2048]{1,0:T(2,128)S(1)}, f32[2,2048]{1,0:T(2,128)S(1)}, u32[]{:S(2)}, u32[]{:S(2)}) %collective-permute-start.15) | collective-permute-done | bytes 16416 | tf_op jit(solution)/shard_map/ppermute | solution.py:27
  108.9 0.0 collective-permute-done.16
  108.9 0.1 fusion.1
  109.0 1.5 scaled.3
  110.5 1.3 collective-permute-start.17
  111.8 1.5 scaled.2
  113.2 1.6 collective-permute-done.17
  114.8 0.4 add_convert_fusion
  115.3 31.5 %all_to_all.26 = bf16[64,16,768]{2,1,0:T(8,128)(2,1)S(1)} all-to-all(bf16[64,16,768]{2,1,0:T(8,128)(2,1)S(1)} %bitcast.18), channel_id=1, replica_groups=mesh['z'=4,'core'=2,'y'=4,'x'=4] {'z','y','x'}, dimensions={0} | all-to-all | bytes 3145728 | tf_op jit(solution)/shard_map/all_to_all | solution.py:384
  146.8 0.2 convert_reduce_fusion
  147.0 0.1 broadcast_in_dim.58
  147.1 28.8 %all_to_all.27 = bf16[64,16,768]{2,1,0:T(8,128)(2,1)S(1)} all-to-all(bf16[64,16,768]{2,1,0:T(8,128)(2,1)S(1)} %broadcast_in_dim.58), channel_id=1, replica_groups=mesh['z'=4,'core'=2,'y'=4,'x'=4] {'z','y','x'}, dimensions={0} | all-to-all | bytes 3145728 | tf_op jit(solution)/shard_map/all_to_all | solution.py:37
  175.9 2.5 %collective-permute-start.18 = (bf16[1024,768]{1,0:T(8,128)(2,1)S(1)}, bf16[1024,768]{1,0:T(8,128)(2,1)S(1)}, u32[]{:S(2)}, u32[]{:S(2)}) collective-permute-start(bf16[1024,768]{1,0:T(8,128)(2,1)S(1)} %bitcast.10), channel_id=1, source_target_pairs={{16,0},{0,16},{17,1},{1,17},{18,2},{2,18},{19,3},{3,19},{20,4},{4,... | collective-permute-start | bytes 4718600 | tf_op jit(solution)/shard_map/ppermute | solution.py:27
  178.4 1.1 fusion
  179.4 2.4 %adapter.2.refs_0_ = f32[768,768]{1,0:T(8,128)S(1)} custom-call(s32[132]{0:T(256)S(1)} %concatenate.19.place, bf16[768,512]{1,0:T(8,128)(2,1)S(1)} %get-tuple-element.64.q0, bf16[768,512]{1,0:T(8,128)(2,1)S(1)} %get-tuple-element.65.q1, bf16[768,512]{1,0:T(8,128)(2,1)S(1)} %get-tuple-element.66.q2, bf16[768,512]{1,0:T(8,128)(2,1)S(1)} %get-tuple-element.67.q3, ...), custom_call_target="tpu_custom_call" | custom-call | flops 1207959552 | bytes 3145728 | tf_op jit(solution)/shard_map/adapter/pallas_call | solution.py:398
  181.9 3.6 %adapter.3 = f32[768,768]{1,0:T(8,128)} custom-call(s32[132]{0:T(256)S(1)} %concatenate.19.place, bf16[768,512]{1,0:T(8,128)(2,1)S(1)} %get-tuple-element.64.q0, bf16[768,512]{1,0:T(8,128)(2,1)S(1)} %get-tuple-element.65.q1, bf16[768,512]{1,0:T(8,128)(2,1)S(1)} %get-tuple-element.66.q2, bf16[768,512]{1,0:T(8,128)(2,1)S(1)} %get-tuple-element.67.q3, ...), custom_call_target="tpu_custom_call" | custom-call | flops 1207959552 | bytes 3145728 | tf_op jit(solution)/shard_map/adapter/pallas_call | solution.py:398
  (28 shorter events, 0.3 us)
Async XLA Ops:
  21.0 5.8 %slice-start = ((s8[6291456]{0:T(1024)(128)(4,1)}), s8[4194304]{0:T(1024)(128)(4,1)S(1)}, s32[]{:S(2)}) async-start(s8[6291456]{0:T(1024)(128)(4,1)} %bitcast.8), calls=%async_computation.3 | async-start | bytes 8388608
  21.0 5.8 %slice-start.1 = ((s8[6291456]{0:T(1024)(128)(4,1)}), s8[2097152]{0:T(1024)(128)(4,1)S(1)}, s32[]{:S(2)}) async-start(s8[6291456]{0:T(1024)(128)(4,1)} %bitcast.8), calls=%async_computation.4 | async-start | bytes 4194304
  21.0 5.8 %copy-start = (bf16[768,768]{1,0:T(8,128)(2,1)S(1)}, bf16[768,768]{1,0:T(8,128)(2,1)}, u32[]{:S(2)}) copy-start(bf16[768,768]{1,0:T(8,128)(2,1)} %w_ref.7) | copy-start | bytes 3538948
  21.0 5.8 %collective-permute-start = (bf16[256,896]{1,0:T(8,128)(2,1)S(1)}, bf16[256,896]{1,0:T(8,128)(2,1)S(1)}, u32[]{:S(2)}, u32[]{:S(2)}) collective-permute-start(bf16[256,896]{1,0:T(8,128)(2,1)S(1)} %bitcast.12), channel_id=1, source_target_pairs={{16,0},{0,16},{17,1},{1,17},{18,2},{2,18},{19,3},{3,19},{20,4},{4,... | collective-permute-start | bytes 1376264 | tf_op jit(solution)/shard_map/ppermute | solution.py:27
  22.8 13.6 %collective-permute-start.1 = (bf16[256,896]{1,0:T(8,128)(2,1)S(1)}, bf16[256,896]{1,0:T(8,128)(2,1)S(1)}, u32[]{:S(2)}, u32[]{:S(2)}) collective-permute-start(bf16[256,896]{1,0:T(8,128)(2,1)S(1)} %bitcast.13), channel_id=1, source_target_pairs={{32,0},{64,32},{96,64},{0,96},{33,1},{65,33},{97,65},{1,97},{34,2}... | collective-permute-start | bytes 1376264 | tf_op jit(solution)/shard_map/ppermute | solution.py:27
  26.7 13.0 %collective-permute-start.3 = (bf16[256,896]{1,0:T(8,128)(2,1)S(1)}, bf16[256,896]{1,0:T(8,128)(2,1)S(1)}, u32[]{:S(2)}, u32[]{:S(2)}) collective-permute-start(bf16[256,896]{1,0:T(8,128)(2,1)S(1)} %bitcast.15), channel_id=1, source_target_pairs={{96,0},{0,32},{32,64},{64,96},{97,1},{1,33},{33,65},{65,97},{98,2}... | collective-permute-start | bytes 1376264 | tf_op jit(solution)/shard_map/ppermute | solution.py:27
  36.3 12.7 %collective-permute-start.5 = (bf16[256,896]{1,0:T(8,128)(2,1)S(1)}, bf16[256,896]{1,0:T(8,128)(2,1)S(1)}, u32[]{:S(2)}, u32[]{:S(2)}) collective-permute-start(bf16[256,896]{1,0:T(8,128)(2,1)S(1)} %bitcast.17), channel_id=1, source_target_pairs={{64,0},{96,32},{0,64},{32,96},{65,1},{97,33},{1,65},{33,97},{66,2}... | collective-permute-start | bytes 1376264 | tf_op jit(solution)/shard_map/ppermute | solution.py:27
  38.4 12.4 %collective-permute-start.2 = (bf16[256,896]{1,0:T(8,128)(2,1)S(1)}, bf16[256,896]{1,0:T(8,128)(2,1)S(1)}, u32[]{:S(2)}, u32[]{:S(2)}) collective-permute-start(bf16[256,896]{1,0:T(8,128)(2,1)S(1)} %collective-permute-done.1.own_ref), channel_id=1, source_target_pairs={{16,0},{0,16},{17,1},{1,17},{18,2},{2,18},{19,3},{3,19},{20,4},{4,... | collective-permute-start | bytes 1376264 | tf_op jit(solution)/shard_map/ppermute | solution.py:27
  39.7 18.1 %collective-permute-start.4 = (bf16[256,896]{1,0:T(8,128)(2,1)S(1)}, bf16[256,896]{1,0:T(8,128)(2,1)S(1)}, u32[]{:S(2)}, u32[]{:S(2)}) collective-permute-start(bf16[256,896]{1,0:T(8,128)(2,1)S(1)} %collective-permute-done.3.own_ref), channel_id=1, source_target_pairs={{16,0},{0,16},{17,1},{1,17},{18,2},{2,18},{19,3},{3,19},{20,4},{4,... | collective-permute-start | bytes 1376264 | tf_op jit(solution)/shard_map/ppermute | solution.py:27
  49.0 15.8 %collective-permute-start.6 = (bf16[256,896]{1,0:T(8,128)(2,1)S(1)}, bf16[256,896]{1,0:T(8,128)(2,1)S(1)}, u32[]{:S(2)}, u32[]{:S(2)}) collective-permute-start(bf16[256,896]{1,0:T(8,128)(2,1)S(1)} %collective-permute-done.5.own_ref), channel_id=1, source_target_pairs={{16,0},{0,16},{17,1},{1,17},{18,2},{2,18},{19,3},{3,19},{20,4},{4,... | collective-permute-start | bytes 1376264 | tf_op jit(solution)/shard_map/ppermute | solution.py:27
  71.8 5.7 %collective-permute-start.7 = (f32[2,2048]{1,0:T(2,128)S(1)}, f32[2,2048]{1,0:T(2,128)S(1)}, u32[]{:S(2)}, u32[]{:S(2)}) collective-permute-start(f32[2,2048]{1,0:T(2,128)S(1)} %constant_dynamic-update-slice_fusion.local_ref), channel_id=1, source_target_pairs={{16,0},{0,16},{17,1},{1,17},{18,2},{2,18},{19,3},{3,19},{20,4},{4,... | collective-permute-start | bytes 49160 | tf_op jit(solution)/shard_map/ppermute | solution.py:27
  77.6 8.4 %collective-permute-start.10 = (f32[2,2048]{1,0:T(2,128)S(1)}, f32[2,2048]{1,0:T(2,128)S(1)}, u32[]{:S(2)}, u32[]{:S(2)}) collective-permute-start(f32[2,2048]{1,0:T(2,128)S(1)} %pad_maximum_fusion.1), channel_id=1, source_target_pairs={{3,0},{0,1},{1,2},{2,3},{7,4},{4,5},{5,6},{6,7},{11,8},{8,9},{9,10... | collective-permute-start | bytes 49160 | tf_op jit(solution)/shard_map/ppermute | solution.py:27
  77.8 8.2 %collective-permute-start.8 = (f32[2,2048]{1,0:T(2,128)S(1)}, f32[2,2048]{1,0:T(2,128)S(1)}, u32[]{:S(2)}, u32[]{:S(2)}) collective-permute-start(f32[2,2048]{1,0:T(2,128)S(1)} %pad_maximum_fusion.1), channel_id=1, source_target_pairs={{1,0},{2,1},{3,2},{0,3},{5,4},{6,5},{7,6},{4,7},{9,8},{10,9},{11,1... | collective-permute-start | bytes 49160 | tf_op jit(solution)/shard_map/ppermute | solution.py:27
  80.4 5.7 %collective-permute-start.9 = (f32[2,2048]{1,0:T(2,128)S(1)}, f32[2,2048]{1,0:T(2,128)S(1)}, u32[]{:S(2)}, u32[]{:S(2)}) collective-permute-start(f32[2,2048]{1,0:T(2,128)S(1)} %pad_maximum_fusion.1), channel_id=1, source_target_pairs={{2,0},{3,1},{0,2},{1,3},{6,4},{7,5},{4,6},{5,7},{10,8},{11,9},{8,1... | collective-permute-start | bytes 49160 | tf_op jit(solution)/shard_map/ppermute | solution.py:27
  86.2 7.6 %collective-permute-start.11 = (f32[2,2048]{1,0:T(2,128)S(1)}, f32[2,2048]{1,0:T(2,128)S(1)}, u32[]{:S(2)}, u32[]{:S(2)}) collective-permute-start(f32[2,2048]{1,0:T(2,128)S(1)} %pad_maximum_fusion.2), channel_id=1, source_target_pairs={{4,0},{8,4},{12,8},{0,12},{5,1},{9,5},{13,9},{1,13},{6,2},{10,6},{... | collective-permute-start | bytes 49160 | tf_op jit(solution)/shard_map/ppermute | solution.py:27
  86.3 7.5 %collective-permute-start.12 = (f32[2,2048]{1,0:T(2,128)S(1)}, f32[2,2048]{1,0:T(2,128)S(1)}, u32[]{:S(2)}, u32[]{:S(2)}) collective-permute-start(f32[2,2048]{1,0:T(2,128)S(1)} %pad_maximum_fusion.2), channel_id=1, source_target_pairs={{8,0},{12,4},{0,8},{4,12},{9,1},{13,5},{1,9},{5,13},{10,2},{14,6},... | collective-permute-start | bytes 49160 | tf_op jit(solution)/shard_map/ppermute | solution.py:27
  87.1 6.7 %collective-permute-start.13 = (f32[2,2048]{1,0:T(2,128)S(1)}, f32[2,2048]{1,0:T(2,128)S(1)}, u32[]{:S(2)}, u32[]{:S(2)}) collective-permute-start(f32[2,2048]{1,0:T(2,128)S(1)} %pad_maximum_fusion.2), channel_id=1, source_target_pairs={{12,0},{0,4},{4,8},{8,12},{13,1},{1,5},{5,9},{9,13},{14,2},{2,6},{... | collective-permute-start | bytes 49160 | tf_op jit(solution)/shard_map/ppermute | solution.py:27
  93.9 12.1 %collective-permute-start.14 = (f32[2,2048]{1,0:T(2,128)S(1)}, f32[2,2048]{1,0:T(2,128)S(1)}, u32[]{:S(2)}, u32[]{:S(2)}) collective-permute-start(f32[2,2048]{1,0:T(2,128)S(1)} %pad_maximum_fusion.3), channel_id=1, source_target_pairs={{32,0},{64,32},{96,64},{0,96},{33,1},{65,33},{97,65},{1,97},{34,2}... | collective-permute-start | bytes 49160 | tf_op jit(solution)/shard_map/ppermute | solution.py:27
  104.7 4.2 %collective-permute-start.15 = (f32[2,2048]{1,0:T(2,128)S(1)}, f32[2,2048]{1,0:T(2,128)S(1)}, u32[]{:S(2)}, u32[]{:S(2)}) collective-permute-start(f32[2,2048]{1,0:T(2,128)S(1)} %pad_maximum_fusion.3), channel_id=1, source_target_pairs={{64,0},{96,32},{0,64},{32,96},{65,1},{97,33},{1,65},{33,97},{66,2}... | collective-permute-start | bytes 49160 | tf_op jit(solution)/shard_map/ppermute | solution.py:27
  104.8 4.1 %collective-permute-start.16 = (f32[2,2048]{1,0:T(2,128)S(1)}, f32[2,2048]{1,0:T(2,128)S(1)}, u32[]{:S(2)}, u32[]{:S(2)}) collective-permute-start(f32[2,2048]{1,0:T(2,128)S(1)} %pad_maximum_fusion.3), channel_id=1, source_target_pairs={{96,0},{0,32},{32,64},{64,96},{97,1},{1,33},{33,65},{65,97},{98,2}... | collective-permute-start | bytes 49160 | tf_op jit(solution)/shard_map/ppermute | solution.py:27
  110.5 4.3 %collective-permute-start.17 = (bf16[1024,768]{1,0:T(8,128)(2,1)S(1)}, bf16[1024,768]{1,0:T(8,128)(2,1)S(1)}, u32[]{:S(2)}, u32[]{:S(2)}) collective-permute-start(bf16[1024,768]{1,0:T(8,128)(2,1)S(1)} %scaled.3), channel_id=1, source_target_pairs={{16,0},{0,16},{17,1},{1,17},{18,2},{2,18},{19,3},{3,19},{20,4},{4,... | collective-permute-start | bytes 4718600 | tf_op jit(solution)/shard_map/ppermute | solution.py:27
  175.9 6.0 %collective-permute-start.18 = (bf16[1024,768]{1,0:T(8,128)(2,1)S(1)}, bf16[1024,768]{1,0:T(8,128)(2,1)S(1)}, u32[]{:S(2)}, u32[]{:S(2)}) collective-permute-start(bf16[1024,768]{1,0:T(8,128)(2,1)S(1)} %bitcast.10), channel_id=1, source_target_pairs={{16,0},{0,16},{17,1},{1,17},{18,2},{2,18},{19,3},{3,19},{20,4},{4,... | collective-permute-start | bytes 4718600 | tf_op jit(solution)/shard_map/ppermute | solution.py:27
